TPU v7x, 128 devices: a whole 4x4x4 slice. The times are simulated.
128 devices in a mesh: frame: 16 (over y, x), tensor: 8 (over z, core).
Axes of the slice: x: 4, y: 4, z: 4, core: 2. Of those that a mesh axis runs over, the one named last changes fastest.
Arguments:
- latents: bfloat16 [8192, 5120], P('frame', 'tensor'), may hold values from -6 to 6
- w_query: bfloat16 [5120, 3072], P(None, 'tensor'), may hold values from -0.078125 to 0.078125
- w_key: bfloat16 [5120, 3072], P(None, 'tensor'), may hold values from -0.078125 to 0.078125
- w_value: bfloat16 [5120, 3072], P(None, 'tensor'), may hold values from -0.078125 to 0.078125
- w_out: bfloat16 [3072, 5120], P('tensor'), may hold values from -0.109375 to 0.109375
- query_gain: float32 [24, 128], P('tensor'), may hold values from 0.5 to 14, as said below
- key_gain: float32 [24, 128], P('tensor'), may hold values from 0.5 to 14, as said below
- mod_table: float32 [16, 3, 5120], replicated, may hold values from -3 to 3
- levels: int32 [16], P('frame'), may hold values from 0 to 15
- span_counts: int32 [16], replicated, may hold values from 1 to 512, 6144 in all
- block_mask: int32 [16, 16], P('frame'), may hold values 0 or 1
- span_order: int32 [16], replicated, may hold values from 0 to 15, each once
Outputs:
- updated: bfloat16 [8192, 5120], P('frame', 'tensor')
Inputs may be any that keep to these rules, and one draw needn't show every extreme that they name: `query_gain`: gains are positive. `key_gain`: gains are positive. `span_order`: each rank appears once.
All inputs are finite; a program needn't handle non-finite values. No bound on the sum of `block_mask` on one device may be relied on, other than what follows from the above.
Results may differ from a plain program's by a relative error of at most 0.012.
The roundings to bfloat16 on the way count: a program that leaves them out, or rounds other values in their place, can miss the bound.
Values may be sent and summed in bfloat16 or wider, within the bound.
No kernel may reach another device: no remote copies, remote signals or barrier semaphores. Data moves between devices by JAX's collectives and lax.ppermute only.
A program may use at most 128 MiB of HBM per device.

v0:
```python
import functools
import math

import jax
import jax.numpy as jnp
from jax import lax
from jax.experimental import pallas as pl
from jax.experimental.pallas import tpu as pltpu
from jax.sharding import Mesh
from jax.sharding import PartitionSpec as P


HEAD_DIM = 128
HEADS_HERE = 3
WIDTH = HEADS_HERE * HEAD_DIM
SIDE = 4
ROWS = 512
HALF = ROWS // 2
EPSILON = 1e-06
NEG_FILL = -1e30
LOG2E = math.log2(math.e)
STEPS = (0, -1, 1, 2)
AXES = ("y", "x", "z", "core")
STAT_ROWS = 16


def permute(value, move):
    pairs = []
    for y in range(SIDE):
        for x in range(SIDE):
            for z in range(SIDE):
                for c in range(2):
                    source = ((y * SIDE + x) * SIDE + z) * 2 + c
                    ty, tx, tz, tc = move(y, x, z, c)
                    target = (((ty % SIDE) * SIDE + tx % SIDE) * SIDE + tz % SIDE) * 2 + tc
                    pairs.append((source, target))
    return lax.ppermute(value, AXES, pairs)


def along_z(step):
    return lambda y, x, z, c: (y, x, z + step, c)


def other_core(y, x, z, c):
    return (y, x, z, 1 - c)


def along_keys(step):
    return lambda y, x, z, c: (y, x + step, z, c) if c == 0 else (y + step, x, z, c)


def along_queries(step):
    return lambda y, x, z, c: (y + step, x, z, c) if c == 0 else (y, x + step, z, c)


def in_vmem(value):
    return pltpu.with_memory_space_constraint(value, pltpu.VMEM)


def project_kernel(places, *refs):
    pieces = refs[:16]
    mod_ref, gain_q, gain_k, wq_ref, wk_ref, wv_ref = refs[16:22]
    q_ref, k_ref, v_ref = refs[22:25]
    mean_ref, factor_ref, n_even, n_odd, acc_q, acc_k, acc_v = refs[25:]
    wide = pieces[0].shape[1]
    groups = wide // 128
    block = 64
    for half in range(2):
        here = pieces[half * 8 : half * 8 + 8]

        def chunk(n, carry, here=here, half=half):
            at = pl.ds(pl.multiple_of(n * block, block), block)
            total = jnp.zeros((block, 128), jnp.float32)
            square = jnp.zeros((block, 128), jnp.float32)
            for piece in here:
                for g in range(groups):
                    part = piece[at, g * 128 : (g + 1) * 128].astype(jnp.float32)
                    total = total + part
                    square = square + part * part
            mean = jnp.sum(total, axis=1, keepdims=True) * (1.0 / (8 * wide))
            mean_square = jnp.sum(square, axis=1, keepdims=True) * (1.0 / (8 * wide))
            factor = lax.rsqrt(mean_square - mean * mean + EPSILON)
            to = pl.ds(pl.multiple_of(half * HALF + n * block, block), block)
            mean_ref[to, :] = jnp.broadcast_to(mean, (block, 128))
            factor_ref[to, :] = jnp.broadcast_to(factor, (block, 128))
            return carry

        lax.fori_loop(0, HALF // block, chunk, 0)
    core = places[4]
    for n in range(SIDE):
        n_buf = n_odd if n % 2 else n_even
        start = places[n] * (2 * wide)
        for e in range(2):
            inside = (core if e == 0 else 1 - core) * wide
            at = pl.ds(pl.multiple_of(start + inside, 128), wide)
            shift = mod_ref[0:1, at]
            scale = 1.0 + mod_ref[1:2, at]
            for half in range(2):
                rows = slice(half * HALF, (half + 1) * HALF)
                mean = jnp.concatenate([mean_ref[rows, :]] * groups, axis=1)
                factor = jnp.concatenate([factor_ref[rows, :]] * groups, axis=1)
                value = pieces[half * 8 + 2 * n + e][...].astype(jnp.float32)
                normed = (value - mean) * factor * scale + shift
                n_buf[rows, pl.ds(pl.multiple_of(inside, 128), wide)] = normed.astype(jnp.bfloat16)
        at = pl.ds(pl.multiple_of(start, 128), 2 * wide)
        for acc, weight in ((acc_k, wk_ref), (acc_v, wv_ref), (acc_q, wq_ref)):
            product = lax.dot_general(
                weight[at, :], n_buf[...], (((0,), (1,)), ((), ())), preferred_element_type=jnp.float32
            )
            if n == 0:
                acc[...] = product
            else:
                acc[...] += product
    for acc, gain, out, turn in ((acc_q, gain_q, q_ref, False), (acc_k, gain_k, k_ref, True)):
        for h in range(HEADS_HERE):
            cut = slice(h * HEAD_DIM, (h + 1) * HEAD_DIM)
            part = acc[cut, :]
            square = jnp.mean(part * part, axis=0, keepdims=True)
            gains = jnp.transpose(jnp.broadcast_to(gain[h : h + 1, :], (HEAD_DIM, HEAD_DIM)))
            gains = jnp.concatenate([gains] * (ROWS // HEAD_DIM), axis=1)
            scaled = part * lax.rsqrt(square + EPSILON) * gains
            if turn:
                out[:, cut] = jnp.transpose(scaled).astype(jnp.bfloat16)
            else:
                out[cut, :] = scaled.astype(jnp.bfloat16)
    v_ref[...] = acc_v[...].astype(jnp.bfloat16)


def project(pieces, places, modulation, gains, weights):
    wide = pieces[0].shape[1]
    vmem = pl.BlockSpec(memory_space=pltpu.VMEM)
    operands = [in_vmem(v) for v in (*pieces, modulation, *gains, *weights)]
    return pl.pallas_call(
        project_kernel,
        in_specs=[pl.BlockSpec(memory_space=pltpu.SMEM)] + [vmem] * 22,
        out_specs=[vmem] * 3,
        out_shape=[
            pltpu.VMEM((WIDTH, ROWS), jnp.bfloat16),
            pltpu.VMEM((ROWS, WIDTH), jnp.bfloat16),
            pltpu.VMEM((WIDTH, ROWS), jnp.bfloat16),
        ],
        scratch_shapes=[
            pltpu.VMEM((ROWS, 128), jnp.float32),
            pltpu.VMEM((ROWS, 128), jnp.float32),
            pltpu.VMEM((ROWS, 2 * wide), jnp.bfloat16),
            pltpu.VMEM((ROWS, 2 * wide), jnp.bfloat16),
            pltpu.VMEM((WIDTH, ROWS), jnp.float32),
            pltpu.VMEM((WIDTH, ROWS), jnp.float32),
            pltpu.VMEM((WIDTH, ROWS), jnp.float32),
        ],
        compiler_params=pltpu.CompilerParams(vmem_limit_bytes=24 * 2**20),
        name="project",
    )(places, *operands)


def attention_kernel(allowed, counts, *refs):
    q_in, k_in, v_in = refs[0:5], refs[5:9], refs[9:13]
    outs = refs[13:17]
    q_buf, k_buf, v_buf, top_ref, sum_ref, acc_ref, out_buf, sem, out_sem = refs[17:]
    copies = []
    for i in range(3):
        copies.append((q_in[i], q_buf.at[i]))
    copies.append((q_in[3], q_buf.at[3, pl.ds(0, WIDTH // 2)]))
    copies.append((q_in[4], q_buf.at[3, pl.ds(WIDTH // 2, WIDTH // 2)]))
    for j in range(4):
        copies.append((k_in[j], k_buf.at[j]))
        copies.append((v_in[j], v_buf.at[j]))
    started = [pltpu.make_async_copy(a, b, sem.at[n]) for n, (a, b) in enumerate(copies)]
    for copy in started:
        copy.start()
    for copy in started:
        copy.wait()
    scale = LOG2E / math.sqrt(HEAD_DIM)

    def fold(i, j, tiles):
        live = counts[j]
        depth = tiles * 128
        tail = depth - 128
        rows = lax.broadcasted_iota(jnp.int32, (128, ROWS), 0) + tail
        for h in range(HEADS_HERE):
            cut = slice(h * HEAD_DIM, (h + 1) * HEAD_DIM)
            queries = q_buf[i, cut, :]
            parts = []
            if tail > 0:
                parts.append(
                    lax.dot_general(
                        k_buf[j, :tail, cut], queries, (((1,), (0,)), ((), ())), preferred_element_type=jnp.float32
                    )
                )
            last = lax.dot_general(
                k_buf[j, tail:depth, cut], queries, (((1,), (0,)), ((), ())), preferred_element_type=jnp.float32
            )
            parts.append(jnp.where(rows < live, last, NEG_FILL))
            before = top_ref[h]
            peak = before
            for part in parts:
                peak = jnp.maximum(peak, jnp.max(part, axis=0, keepdims=True))
            shift = peak * scale
            weights = [jnp.exp2(part * scale - shift) for part in parts]
            factor = jnp.exp2(before * scale - shift)
            total = sum_ref[h] * factor
            for weight in weights:
                total = total + jnp.sum(weight, axis=0, keepdims=True)
            narrow = [weight.astype(jnp.bfloat16) for weight in weights]
            joined = narrow[0] if len(narrow) == 1 else jnp.concatenate(narrow, axis=0)
            product = lax.dot_general(
                v_buf[j, cut, :depth], joined, (((1,), (0,)), ((), ())), preferred_element_type=jnp.float32
            )
            acc_ref[h] = acc_ref[h] * factor + product
            top_ref[h] = peak
            sum_ref[h] = total

    def query_span(i, carry):
        for h in range(HEADS_HERE):
            top_ref[h] = jnp.full((1, ROWS), NEG_FILL, jnp.float32)
            sum_ref[h] = jnp.zeros((1, ROWS), jnp.float32)
            acc_ref[h] = jnp.zeros((HEAD_DIM, ROWS), jnp.float32)

        def key_span(j, inner):
            tiles = (counts[j] + 127) // 128
            for n in range(1, 5):

                @pl.when((allowed[i * 4 + j] == 1) & (tiles == n))
                def _(n=n):
                    fold(i, j, n)

            return inner

        lax.fori_loop(0, 4, key_span, 0)
        stats = []
        for h in range(HEADS_HERE):
            total = sum_ref[h]
            some = total > 0.0
            safe = jnp.where(some, total, 1.0)
            out_buf[i, h * HEAD_DIM : (h + 1) * HEAD_DIM, :] = (acc_ref[h] / safe).astype(jnp.bfloat16)
            size = jnp.where(some, top_ref[h] * scale + jnp.log2(safe), NEG_FILL)
            high = size.astype(jnp.bfloat16).astype(jnp.float32)
            middle = (size - high).astype(jnp.bfloat16).astype(jnp.float32)
            stats += [high, middle, size - high - middle]
        stats.append(jnp.zeros((STAT_ROWS - len(stats), ROWS), jnp.float32))
        out_buf[i, WIDTH:, :] = jnp.concatenate(stats, axis=0).astype(jnp.bfloat16)
        return carry

    lax.fori_loop(0, 4, query_span, 0)
    started = [pltpu.make_async_copy(out_buf.at[i], outs[i], out_sem.at[i]) for i in range(4)]
    for copy in started:
        copy.start()
    for copy in started:
        copy.wait()


def attention(allowed, counts, queries, keys, values):
    tall = WIDTH + STAT_ROWS
    return pl.pallas_call(
        attention_kernel,
        in_specs=[pl.BlockSpec(memory_space=pltpu.SMEM)] * 2 + [pl.BlockSpec(memory_space=pl.ANY)] * 13,
        out_specs=[pl.BlockSpec(memory_space=pl.ANY)] * 4,
        out_shape=[jax.ShapeDtypeStruct((tall, ROWS), jnp.bfloat16)] * 4,
        scratch_shapes=[
            pltpu.VMEM((4, WIDTH, ROWS), jnp.bfloat16),
            pltpu.VMEM((4, ROWS, WIDTH), jnp.bfloat16),
            pltpu.VMEM((4, WIDTH, ROWS), jnp.bfloat16),
            pltpu.VMEM((HEADS_HERE, 1, ROWS), jnp.float32),
            pltpu.VMEM((HEADS_HERE, 1, ROWS), jnp.float32),
            pltpu.VMEM((HEADS_HERE, HEAD_DIM, ROWS), jnp.float32),
            pltpu.VMEM((4, tall, ROWS), jnp.bfloat16),
            pltpu.SemaphoreType.DMA((13,)),
            pltpu.SemaphoreType.DMA((4,)),
        ],
        name="attention",
    )(allowed, counts, *queries, *keys, *values)


def combine_kernel(*refs):
    parts, out_ref = refs[:4], refs[4]
    stats = [part[WIDTH:, :].astype(jnp.float32) for part in parts]
    for h in range(HEADS_HERE):
        sizes = [s[3 * h : 3 * h + 1] + s[3 * h + 1 : 3 * h + 2] + s[3 * h + 2 : 3 * h + 3] for s in stats]
        peak = functools.reduce(jnp.maximum, sizes)
        shares = [jnp.exp2(size - peak) for size in sizes]
        total = functools.reduce(jnp.add, shares)
        cut = slice(h * HEAD_DIM, (h + 1) * HEAD_DIM)
        merged = sum(part[cut, :].astype(jnp.float32) * (share / total) for part, share in zip(parts, shares))
        out_ref[:, cut] = jnp.transpose(merged).astype(jnp.bfloat16)


def combine(parts):
    vmem = pl.BlockSpec(memory_space=pltpu.VMEM)
    return pl.pallas_call(
        combine_kernel,
        in_specs=[vmem] * 4,
        out_specs=vmem,
        out_shape=pltpu.VMEM((ROWS, WIDTH), jnp.bfloat16),
        compiler_params=pltpu.CompilerParams(vmem_limit_bytes=16 * 2**20),
        name="combine",
    )(*[in_vmem(part) for part in parts])


def output_kernel(*refs):
    attended, weights = refs[:8], refs[8:12]
    latents_ref, gate_ref, out_ref, acc_ref = refs[12:16]
    for n in range(8):
        term = jnp.dot(attended[n][...], weights[n // 2][n % 2], preferred_element_type=jnp.float32)
        term = term.astype(jnp.bfloat16).astype(jnp.float32)
        if n == 0:
            acc_ref[...] = term
        elif n < 7:
            acc_ref[...] += term
        else:
            projected = acc_ref[...] + term
            updated = latents_ref[...].astype(jnp.float32) + gate_ref[...] * projected
            out_ref[...] = updated.astype(jnp.bfloat16)


def output(attended, weights, latents, gate):
    vmem = pl.BlockSpec(memory_space=pltpu.VMEM)
    wide = latents.shape[1]
    operands = [in_vmem(v) for v in (*attended, *weights, latents, gate)]
    return pl.pallas_call(
        output_kernel,
        in_specs=[vmem] * 14,
        out_specs=vmem,
        out_shape=jax.ShapeDtypeStruct(latents.shape, jnp.bfloat16),
        scratch_shapes=[pltpu.VMEM((ROWS, wide), jnp.float32)],
        compiler_params=pltpu.CompilerParams(vmem_limit_bytes=16 * 2**20),
        name="output",
    )(*operands)


def on_device(
    latents,
    w_query,
    w_key,
    w_value,
    w_out,
    query_gain,
    key_gain,
    mod_table,
    levels,
    span_counts,
    block_mask,
    span_order,
):
    shard_width = latents.shape[1]
    y, x, z, c = (lax.axis_index(name) for name in AXES)

    mask_low = permute(block_mask, along_queries(1))
    mask_high = permute(block_mask, along_queries(-1))
    mask_far = permute(block_mask, along_queries(2))
    mask_rows = jnp.concatenate([block_mask, mask_low, mask_high, mask_far])
    own = (latents[:HALF], latents[HALF:])
    below, above = [None, None], [None, None]
    below[0] = permute(own[0], along_z(1))
    above[1] = permute(own[1], along_z(-1))
    below[1] = permute(own[1], along_z(1))
    above[0] = permute(own[0], along_z(-1))

    places = [(z + step + SIDE) % SIDE * 2 + core for step in STEPS for core in (c, 1 - c)]
    columns = jnp.stack([(z + step + SIDE) % SIDE for step in STEPS] + [c]).astype(jnp.int32)
    modulation = lax.dynamic_index_in_dim(mod_table, levels[0], 0, keepdims=False)
    gate = lax.dynamic_slice(modulation, (2, places[0] * shard_width), (1, shard_width))

    def spans(along_x):
        return jnp.stack(
            [
                jnp.where(along_x, y * SIDE + (x + s + SIDE) % SIDE, (y + s + SIDE) % SIDE * SIDE + x)
                for s in STEPS
            ]
        )

    query_spans = spans(c == 1)
    key_spans = spans(c == 0)
    ids = jnp.arange(SIDE * SIDE, dtype=jnp.int32)
    pick_query = query_spans[:, None] == ids[None, :]
    pick_key = key_spans[:, None] == ids[None, :]
    query_rank = jnp.sum(jnp.where(pick_query, span_order[None, :], 0), axis=1)
    key_rank = jnp.sum(jnp.where(pick_key, span_order[None, :], 0), axis=1)
    counts = jnp.sum(jnp.where(pick_key, span_counts[None, :], 0), axis=1)
    linked = jnp.sum(jnp.where(pick_key[None, :, :], mask_rows[:, None, :], 0), axis=2) == 1
    same = query_spans[:, None] == key_spans[None, :]
    allowed = ((key_rank[None, :] <= query_rank[:, None]) & (linked | same)).astype(jnp.int32).reshape(-1)

    w_parts = [
        lax.dynamic_slice(w_out, (0, place * shard_width), (WIDTH, shard_width)) for place in places
    ]
    w_other = permute(jnp.stack(w_parts[1::2]), other_core)
    w_pairs = [jnp.stack((w_parts[2 * n], w_other[n])) for n in range(SIDE)]
    below[0], allowed, counts, columns, modulation, gate, w_pairs = lax.optimization_barrier(
        (below[0], allowed, counts, columns, modulation, gate, w_pairs)
    )

    far = (permute(below[0], along_z(1)), permute(above[1], along_z(-1)))
    pieces = []
    for half in range(2):
        for value in (own[half], below[half], above[half], far[half]):
            pieces += [value, permute(value, other_core)]
    query_own, key_own, value_own = project(
        pieces, columns, modulation, (query_gain, key_gain), (w_query, w_key, w_value)
    )

    w_pairs, key_own, value_own, query_own = lax.optimization_barrier((w_pairs, key_own, value_own, query_own))
    key_low, key_high = permute(key_own, along_keys(1)), permute(key_own, along_keys(-1))
    value_low, value_high = permute(value_own, along_keys(1)), permute(value_own, along_keys(-1))
    query_low, query_high = permute(query_own, along_queries(1)), permute(query_own, along_queries(-1))
    w_below = permute(w_pairs[2], along_z(1))
    w_above = permute(w_pairs[1], along_z(-1))
    w_far = permute(w_pairs[3], along_z(2))
    w_blocks = (w_pairs[0], w_below, w_above, w_far)
    key_far = permute(key_low, along_keys(1))
    value_far = permute(value_high, along_keys(-1))
    query_far = (
        permute(query_low[: WIDTH // 2], along_queries(1)),
        permute(query_high[WIDTH // 2 :], along_queries(-1)),
    )

    partial = attention(
        allowed,
        counts,
        (query_own, query_low, query_high, *query_far),
        (key_own, key_low, key_high, key_far),
        (value_own, value_low, value_high, value_far),
    )
    attended = combine(
        (
            partial[0],
            permute(partial[1], along_queries(-1)),
            permute(partial[2], along_queries(1)),
            permute(partial[3], along_queries(2)),
        )
    )
    shared = [attended, permute(attended, along_z(1)), permute(attended, along_z(-1)), permute(attended, along_z(2))]
    everyone = []
    for value in shared:
        everyone += [value, permute(value, other_core)]
    return output(everyone, w_blocks, latents, gate)


def solution(mesh):
    fine = Mesh(mesh.devices.reshape(SIDE, SIDE, SIDE, 2), AXES)
    frame, tensor = ("y", "x"), ("z", "core")

    return jax.shard_map(
        on_device,
        mesh=fine,
        in_specs=(
            P(frame, tensor),
            P(None, tensor),
            P(None, tensor),
            P(None, tensor),
            P(tensor, None),
            P(tensor, None),
            P(tensor, None),
            P(),
            P(frame),
            P(),
            P(frame, None),
            P(),
        ),
        out_specs=P(frame, tensor),
        check_vma=False,
    )
```

profile of v0, /device:TPU:0, one launch (start us, length us, event | category | flops | bytes accessed | tf_op | source)
XLA Modules:
  0.0 177.6 jit_solution(7121451687532132585)
XLA Ops:
  0.0 3.5 %dynamic-slice_bitcast_fusion = (bf16[1,384,640]{2,1,0:T(8,128)(2,1)S(1)}, bf16[1,384,640]{2,1,0:T(8,128)(2,1)}, bf16[1,384,640]{2,1,0:T(8,128)(2,1)S(1)}, bf16[...) fusion(bf16[384,5120]{1,0:T(8,128)(2,1)} %param.16, ...), kind=kLoop, calls=%fused_computation.5 | loop fusion | bytes 7864352 | tf_op jit(solution)/shard_map/stack | solution.py:387
  3.5 1.6 pad_maximum_fusion
  5.1 3.1 %collective-permute-start.2 = (s32[1,16]{1,0:T(1,128)S(1)}, s32[1,16]{1,0:T(1,128)S(1)}, u32[]{:S(2)}, u32[]{:S(2)}) collective-permute-start(s32[1,16]{1,0:T(1,128)S(1)} %copy-done.22), channel_id=1, source_target_pairs={{0,96},{1,25},{2,98},{3,27},{4,100},{5,29},{6,102},{7,31},{8,104},... | collective-permute-start | bytes 200 | tf_op jit(solution)/shard_map/ppermute | solution.py:37
  8.3 2.2 %collective-permute-start.3 = (s32[1,16]{1,0:T(1,128)S(1)}, s32[1,16]{1,0:T(1,128)S(1)}, u32[]{:S(2)}, u32[]{:S(2)}) collective-permute-start(s32[1,16]{1,0:T(1,128)S(1)} %copy-done.22), channel_id=1, source_target_pairs={{0,64},{1,17},{2,66},{3,19},{4,68},{5,21},{6,70},{7,23},{8,72},{9,... | collective-permute-start | bytes 200 | tf_op jit(solution)/shard_map/ppermute | solution.py:37
  10.5 4.1 %collective-permute-start.14 = (bf16[256,640]{1,0:T(8,128)(2,1)S(1)}, bf16[256,640]{1,0:T(8,128)(2,1)}, u32[]{:S(2)}, u32[]{:S(2)}) collective-permute-start(bf16[256,640]{1,0:T(8,128)(2,1)S(1)} %get-tuple-element.68.refs_8_), channel_id=1, source_target_pairs={{0,6},{1,7},{2,0},{3,1},{4,2},{5,3},{6,4},{7,5},{8,14},{9,15},{10,... | collective-permute-start | bytes 983048 | tf_op jit(solution)/shard_map/ppermute | solution.py:37
  16.6 3.2 %collective-permute-start.7 = (bf16[256,640]{1,0:T(8,128)(2,1)S(1)}, bf16[256,640]{1,0:T(8,128)(2,1)}, u32[]{:S(2)}, u32[]{:S(2)}) collective-permute-start(bf16[256,640]{1,0:T(8,128)(2,1)S(1)} %get-tuple-element.69.refs_0_), channel_id=1, source_target_pairs={{0,6},{1,7},{2,0},{3,1},{4,2},{5,3},{6,4},{7,5},{8,14},{9,15},{10,... | collective-permute-start | bytes 983048 | tf_op jit(solution)/shard_map/ppermute | solution.py:37
  20.7 1.8 %fusion = (bf16[1,384,640]{2,1,0:T(8,128)(2,1)S(1)}, bf16[1,384,640]{2,1,0:T(8,128)(2,1)S(1)}, bf16[1,384,640]{2,1,0:T(8,128)(2,1)S(1)}, bf16[1,384,640]{2,1,0:T(8,128)(2,1)S(1)}) fusion(bf16[4,384,640]{2,1,0:T(8,128)(2,1)} %collective-permute-done.4), kind=kLoop, calls=%fused_computation.26 | loop fusion | bytes 3932160 | tf_op jit(solution)/shard_map/slice | solution.py:387
  24.0 2.6 %pad_maximum_fusion.1 = (bf16[2,384,640]{2,1,0:T(8,128)(2,1)S(1)}, bf16[2,384,640]{2,1,0:T(8,128)(2,1)}) fusion(bf16[1,384,640]{2,1,0:T(8,128)(2,1)S(1)} %get-tuple-element.67, bf16[1,384,640]{2,1,0:T(8,128)(2,1)} %get-tuple-element.62, bf16[1,384,640]{2,1,0:T(8,128)(2,1)S(1)} %get-tuple-element.66, bf16[1,384,640]{2,1,0:T(8,128)(2,1)} %get-tuple-element.57), kind=kLoop, calls=%fused_computation.1 | loop fusion | flops 983040 | bytes 3932160 | tf_op jit(solution)/shard_map/stack | solution.py:387
  26.8 6.7 %collective-permute-done.refs_2_ = bf16[256,640]{1,0:T(8,128)(2,1)S(1)} collective-permute-done((bf16[256,640]{1,0:T(8,128)(2,1)S(1)}, bf16[256,640]{1,0:T(8,128)(2,1)S(1)}, u32[]{:S(2)}, u32[]{:S(2)}) %collective-permute-start) | collective-permute-done | bytes 327712 | tf_op jit(solution)/shard_map/ppermute | solution.py:37
  33.5 2.1 %collective-permute-start.9 = (bf16[256,640]{1,0:T(8,128)(2,1)S(1)}, bf16[256,640]{1,0:T(8,128)(2,1)S(1)}, u32[]{:S(2)}, u32[]{:S(2)}) collective-permute-start(bf16[256,640]{1,0:T(8,128)(2,1)S(1)} %collective-permute-done.refs_2_), channel_id=1, source_target_pairs={{0,2},{1,3},{2,4},{3,5},{4,6},{5,7},{6,0},{7,1},{8,10},{9,11},{10,... | collective-permute-start | bytes 983048 | tf_op jit(solution)/shard_map/ppermute | solution.py:37
  36.1 5.6 %collective-permute-done.16.refs_14_ = bf16[256,640]{1,0:T(8,128)(2,1)S(1)} collective-permute-done((bf16[256,640]{1,0:T(8,128)(2,1)}, bf16[256,640]{1,0:T(8,128)(2,1)S(1)}, u32[]{:S(2)}, u32[]{:S(2)}) %collective-permute-start.16) | collective-permute-done | bytes 327712 | tf_op jit(solution)/shard_map/ppermute | solution.py:37
  42.2 2.6 %collective-permute-done.9.refs_6_ = bf16[256,640]{1,0:T(8,128)(2,1)S(1)} collective-permute-done((bf16[256,640]{1,0:T(8,128)(2,1)S(1)}, bf16[256,640]{1,0:T(8,128)(2,1)S(1)}, u32[]{:S(2)}, u32[]{:S(2)}) %collective-permute-start.9) | collective-permute-done | bytes 327712 | tf_op jit(solution)/shard_map/ppermute | solution.py:37
  44.9 1.6 collective-permute-done.10.refs_7_
  46.5 13.0 %project.1 = (bf16[384,512]{1,0:T(8,128)(2,1)S(1)}, bf16[512,384]{1,0:T(8,128)(2,1)S(1)}, bf16[384,512]{1,0:T(8,128)(2,1)S(1)}) custom-call(s32[5]{0:T(128)S(1)} %stack.102.places, bf16[256,640]{1,0:T(8,128)(2,1)S(1)} %get-tuple-element.69.refs_0_, bf16[256,640]{1,0:T(8,128)(2,1)S(1)} %collective-permute-done.5.refs_1_, ...), custom_call_target="tpu_custom_call" | custom-call | tf_op jit(solution)/shard_map/project/pallas_call | solution.py:133
  59.5 2.7 %collective-permute-start.19 = (bf16[384,512]{1,0:T(8,128)(2,1)S(1)}, bf16[384,512]{1,0:T(8,128)(2,1)S(1)}, u32[]{:S(2)}, u32[]{:S(2)}) collective-permute-start(bf16[384,512]{1,0:T(8,128)(2,1)S(1)} %get-tuple-element.41.refs_0_), channel_id=1, source_target_pairs={{0,96},{1,25},{2,98},{3,27},{4,100},{5,29},{6,102},{7,31},{8,104},... | collective-permute-start | bytes 1179656 | tf_op jit(solution)/shard_map/ppermute | solution.py:37
  63.4 2.1 %collective-permute-start.26 = (bf16[384,512]{1,0:T(8,128)(2,1)S(1)}, bf16[384,512]{1,0:T(8,128)(2,1)S(1)}, u32[]{:S(2)}, u32[]{:S(2)}) collective-permute-start(bf16[384,512]{1,0:T(8,128)(2,1)S(1)} %get-tuple-element.43.refs_9_), channel_id=1, source_target_pairs={{0,24},{1,97},{2,26},{3,99},{4,28},{5,101},{6,30},{7,103},{8,0},{9... | collective-permute-start | bytes 1179656 | tf_op jit(solution)/shard_map/ppermute | solution.py:37
  65.9 5.3 %collective-permute-done.19.refs_2_ = bf16[384,512]{1,0:T(8,128)(2,1)S(1)} collective-permute-done((bf16[384,512]{1,0:T(8,128)(2,1)S(1)}, bf16[384,512]{1,0:T(8,128)(2,1)S(1)}, u32[]{:S(2)}, u32[]{:S(2)}) %collective-permute-start.19) | collective-permute-done | bytes 393248 | tf_op jit(solution)/shard_map/ppermute | solution.py:37
  71.2 1.7 collective-permute-start.25
  72.8 2.3 %collective-permute-done.22.refs_6_ = bf16[512,384]{1,0:T(8,128)(2,1)S(1)} collective-permute-done((bf16[512,384]{1,0:T(8,128)(2,1)S(1)}, bf16[512,384]{1,0:T(8,128)(2,1)S(1)}, u32[]{:S(2)}, u32[]{:S(2)}) %collective-permute-start.22) | collective-permute-done | bytes 393248 | tf_op jit(solution)/shard_map/ppermute | solution.py:37
  75.3 3.0 %collective-permute-start.27 = (bf16[384,512]{1,0:T(8,128)(2,1)S(1)}, bf16[384,512]{1,0:T(8,128)(2,1)}, u32[]{:S(2)}, u32[]{:S(2)}) collective-permute-start(bf16[384,512]{1,0:T(8,128)(2,1)S(1)} %collective-permute-done.26.refs_11_), channel_id=1, source_target_pairs={{0,24},{1,97},{2,26},{3,99},{4,28},{5,101},{6,30},{7,103},{8,0},{9... | collective-permute-start | bytes 1179656 | tf_op jit(solution)/shard_map/ppermute | solution.py:37
  81.7 3.6 %collective-permute-done.21.refs_4_ = bf16[192,512]{1,0:T(8,128)(2,1)S(1)} collective-permute-done((bf16[192,512]{1,0:T(8,128)(2,1)S(1)}, bf16[192,512]{1,0:T(8,128)(2,1)S(1)}, u32[]{:S(2)}, u32[]{:S(2)}) %collective-permute-start.21) | collective-permute-done | bytes 196640 | tf_op jit(solution)/shard_map/ppermute | solution.py:37
  85.3 2.5 %collective-permute-done.20.refs_3_ = bf16[192,512]{1,0:T(8,128)(2,1)S(1)} collective-permute-done((bf16[192,512]{1,0:T(8,128)(2,1)S(1)}, bf16[192,512]{1,0:T(8,128)(2,1)S(1)}, u32[]{:S(2)}, u32[]{:S(2)}) %collective-permute-start.20) | collective-permute-done | bytes 196640 | tf_op jit(solution)/shard_map/ppermute | solution.py:37
  88.7 10.9 %attention.1 = (bf16[400,512]{1,0:T(8,128)(2,1)}, bf16[400,512]{1,0:T(8,128)(2,1)}, bf16[400,512]{1,0:T(8,128)(2,1)}, bf16[400,512]{1,0:T(8,128)(2,1)}) custom-call(s32[16]{0:T(128)} %reshape.39.allowed, s32[4]{0:T(128)} %get-tuple-element.30.counts, bf16[384,512]{1,0:T(8,128)(2,1)} %copy-done.6, bf16[384,512]{1,0:T(8,128)(2,1)} %copy-done.12, ...), custom_call_target="tpu_custom_call" | custom-call | tf_op jit(solution)/shard_map/attention/pallas_call | solution.py:254
  99.5 8.3 %collective-permute-start.28 = (bf16[400,512]{1,0:T(8,128)(2,1)}, bf16[400,512]{1,0:T(8,128)(2,1)S(1)}, u32[]{:S(2)}, u32[]{:S(2)}) collective-permute-start(bf16[400,512]{1,0:T(8,128)(2,1)} %get-tuple-element.45), channel_id=1, source_target_pairs={{0,96},{1,25},{2,98},{3,27},{4,100},{5,29},{6,102},{7,31},{8,104},... | collective-permute-start | bytes 1228808 | tf_op jit(solution)/shard_map/ppermute | solution.py:37
  107.9 2.0 %collective-permute-start.39 = (bf16[2,384,640]{2,1,0:T(8,128)(2,1)}, bf16[2,384,640]{2,1,0:T(8,128)(2,1)S(1)}, u32[]{:S(2)}, u32[]{:S(2)}) collective-permute-start(bf16[2,384,640]{2,1,0:T(8,128)(2,1)} %get-tuple-element.50), channel_id=1, source_target_pairs={{0,6},{1,7},{2,0},{3,1},{4,2},{5,3},{6,4},{7,5},{8,14},{9,15},{10,... | collective-permute-start | bytes 2949128 | tf_op jit(solution)/shard_map/ppermute | solution.py:37
  109.9 1.6 collective-permute-start.30
  111.4 2.2 %collective-permute-done.28.refs_1_ = bf16[400,512]{1,0:T(8,128)(2,1)S(1)} collective-permute-done((bf16[400,512]{1,0:T(8,128)(2,1)}, bf16[400,512]{1,0:T(8,128)(2,1)S(1)}, u32[]{:S(2)}, u32[]{:S(2)}) %collective-permute-start.28) | collective-permute-done | bytes 409632 | tf_op jit(solution)/shard_map/ppermute | solution.py:37
  114.8 8.8 %collective-permute-done.29.refs_2_ = bf16[400,512]{1,0:T(8,128)(2,1)S(1)} collective-permute-done((bf16[400,512]{1,0:T(8,128)(2,1)}, bf16[400,512]{1,0:T(8,128)(2,1)S(1)}, u32[]{:S(2)}, u32[]{:S(2)}) %collective-permute-start.29) | collective-permute-done | bytes 409632 | tf_op jit(solution)/shard_map/ppermute | solution.py:37
  126.1 1.8 %collective-permute-start.34 = (bf16[512,384]{1,0:T(8,128)(2,1)S(1)}, bf16[512,384]{1,0:T(8,128)(2,1)S(1)}, u32[]{:S(2)}, u32[]{:S(2)}) collective-permute-start(bf16[512,384]{1,0:T(8,128)(2,1)S(1)} %combine.1.refs_0_), channel_id=1, source_target_pairs={{0,6},{1,7},{2,0},{3,1},{4,2},{5,3},{6,4},{7,5},{8,14},{9,15},{10,... | collective-permute-start | bytes 1179656 | tf_op jit(solution)/shard_map/ppermute | solution.py:37
  128.1 33.3 %collective-permute-done.39.refs_10_ = bf16[2,384,640]{2,1,0:T(8,128)(2,1)S(1)} collective-permute-done((bf16[2,384,640]{2,1,0:T(8,128)(2,1)}, bf16[2,384,640]{2,1,0:T(8,128)(2,1)S(1)}, u32[]{:S(2)}, u32[]{:S(2)}) %collective-permute-start.39) | collective-permute-done | bytes 983072 | tf_op jit(solution)/shard_map/ppermute | solution.py:37
  161.9 8.3 %collective-permute-done.34.refs_4_ = bf16[512,384]{1,0:T(8,128)(2,1)S(1)} collective-permute-done((bf16[512,384]{1,0:T(8,128)(2,1)S(1)}, bf16[512,384]{1,0:T(8,128)(2,1)S(1)}, u32[]{:S(2)}, u32[]{:S(2)}) %collective-permute-start.34) | collective-permute-done | bytes 393248 | tf_op jit(solution)/shard_map/ppermute | solution.py:37
  172.4 5.2 %output.1 = bf16[512,640]{1,0:T(8,128)(2,1)} custom-call(bf16[512,384]{1,0:T(8,128)(2,1)S(1)} %combine.1.refs_0_, bf16[512,384]{1,0:T(8,128)(2,1)S(1)} %collective-permute-done.31.refs_1_, bf16[512,384]{1,0:T(8,128)(2,1)S(1)} %collective-permute-done.32.refs_2_, bf16[512,384]{1,0:T(8,128)(2,1)S(1)} %collective-permute-done.33.refs_3_, ...), custom_call_target="tpu_custom_call" | custom-call | tf_op jit(solution)/shard_map/output/pallas_call | solution.py:319
  (119 shorter events, 17.5 us)
Async XLA Ops:
  5.1 15.6 %collective-permute-start.4 = (bf16[4,384,640]{2,1,0:T(8,128)(2,1)}, bf16[4,384,640]{2,1,0:T(8,128)(2,1)}, u32[]{:S(2)}, u32[]{:S(2)}) collective-permute-start(bf16[4,384,640]{2,1,0:T(8,128)(2,1)} %pad_maximum_fusion), channel_id=1, source_target_pairs={{0,1},{1,0},{2,3},{3,2},{4,5},{5,4},{6,7},{7,6},{8,9},{9,8},{10,11... | collective-permute-start | bytes 5898248 | tf_op jit(solution)/shard_map/ppermute | solution.py:37
  5.1 11.3 %collective-permute-start.2 = (s32[1,16]{1,0:T(1,128)S(1)}, s32[1,16]{1,0:T(1,128)S(1)}, u32[]{:S(2)}, u32[]{:S(2)}) collective-permute-start(s32[1,16]{1,0:T(1,128)S(1)} %copy-done.22), channel_id=1, source_target_pairs={{0,96},{1,25},{2,98},{3,27},{4,100},{5,29},{6,102},{7,31},{8,104},... | collective-permute-start | bytes 200 | tf_op jit(solution)/shard_map/ppermute | solution.py:37
  8.2 8.2 %collective-permute-start.1 = (s32[1,16]{1,0:T(1,128)S(1)}, s32[1,16]{1,0:T(1,128)S(1)}, u32[]{:S(2)}, u32[]{:S(2)}) collective-permute-start(s32[1,16]{1,0:T(1,128)S(1)} %copy-done.22), channel_id=1, source_target_pairs={{0,32},{1,9},{2,34},{3,11},{4,36},{5,13},{6,38},{7,15},{8,40},{9,1... | collective-permute-start | bytes 200 | tf_op jit(solution)/shard_map/ppermute | solution.py:37
  8.3 8.3 %collective-permute-start.3 = (s32[1,16]{1,0:T(1,128)S(1)}, s32[1,16]{1,0:T(1,128)S(1)}, u32[]{:S(2)}, u32[]{:S(2)}) collective-permute-start(s32[1,16]{1,0:T(1,128)S(1)} %copy-done.22), channel_id=1, source_target_pairs={{0,64},{1,17},{2,66},{3,19},{4,68},{5,21},{6,70},{7,23},{8,72},{9,... | collective-permute-start | bytes 200 | tf_op jit(solution)/shard_map/ppermute | solution.py:37
  10.5 16.1 %collective-permute-start.14 = (bf16[256,640]{1,0:T(8,128)(2,1)S(1)}, bf16[256,640]{1,0:T(8,128)(2,1)}, u32[]{:S(2)}, u32[]{:S(2)}) collective-permute-start(bf16[256,640]{1,0:T(8,128)(2,1)S(1)} %get-tuple-element.68.refs_8_), channel_id=1, source_target_pairs={{0,6},{1,7},{2,0},{3,1},{4,2},{5,3},{6,4},{7,5},{8,14},{9,15},{10,... | collective-permute-start | bytes 983048 | tf_op jit(solution)/shard_map/ppermute | solution.py:37
  16.4 17.1 %collective-permute-start.12 = (bf16[256,640]{1,0:T(8,128)(2,1)S(1)}, bf16[256,640]{1,0:T(8,128)(2,1)}, u32[]{:S(2)}, u32[]{:S(2)}) collective-permute-start(bf16[256,640]{1,0:T(8,128)(2,1)S(1)} %get-tuple-element.68.refs_8_), channel_id=1, source_target_pairs={{0,2},{1,3},{2,4},{3,5},{4,6},{5,7},{6,0},{7,1},{8,10},{9,11},{10,... | collective-permute-start | bytes 983048 | tf_op jit(solution)/shard_map/ppermute | solution.py:37
  16.5 17.1 %collective-permute-start.11 = (bf16[256,640]{1,0:T(8,128)(2,1)S(1)}, bf16[256,640]{1,0:T(8,128)(2,1)}, u32[]{:S(2)}, u32[]{:S(2)}) collective-permute-start(bf16[256,640]{1,0:T(8,128)(2,1)S(1)} %get-tuple-element.68.refs_8_), channel_id=1, source_target_pairs={{0,1},{1,0},{2,3},{3,2},{4,5},{5,4},{6,7},{7,6},{8,9},{9,8},{10,11... | collective-permute-start | bytes 983048 | tf_op jit(solution)/shard_map/ppermute | solution.py:37
  16.6 19.0 %collective-permute-start.7 = (bf16[256,640]{1,0:T(8,128)(2,1)S(1)}, bf16[256,640]{1,0:T(8,128)(2,1)}, u32[]{:S(2)}, u32[]{:S(2)}) collective-permute-start(bf16[256,640]{1,0:T(8,128)(2,1)S(1)} %get-tuple-element.69.refs_0_), channel_id=1, source_target_pairs={{0,6},{1,7},{2,0},{3,1},{4,2},{5,3},{6,4},{7,5},{8,14},{9,15},{10,... | collective-permute-start | bytes 983048 | tf_op jit(solution)/shard_map/ppermute | solution.py:37
  20.7 12.8 %collective-permute-start = (bf16[256,640]{1,0:T(8,128)(2,1)S(1)}, bf16[256,640]{1,0:T(8,128)(2,1)S(1)}, u32[]{:S(2)}, u32[]{:S(2)}) collective-permute-start(bf16[256,640]{1,0:T(8,128)(2,1)S(1)} %get-tuple-element.69.refs_0_), channel_id=1, source_target_pairs={{0,2},{1,3},{2,4},{3,5},{4,6},{5,7},{6,0},{7,1},{8,10},{9,11},{10,... | collective-permute-start | bytes 983048 | tf_op jit(solution)/shard_map/ppermute | solution.py:37
  26.7 9.1 %collective-permute-start.5 = (bf16[256,640]{1,0:T(8,128)(2,1)S(1)}, bf16[256,640]{1,0:T(8,128)(2,1)S(1)}, u32[]{:S(2)}, u32[]{:S(2)}) collective-permute-start(bf16[256,640]{1,0:T(8,128)(2,1)S(1)} %get-tuple-element.69.refs_0_), channel_id=1, source_target_pairs={{0,1},{1,0},{2,3},{3,2},{4,5},{5,4},{6,7},{7,6},{8,9},{9,8},{10,11... | collective-permute-start | bytes 983048 | tf_op jit(solution)/shard_map/ppermute | solution.py:37
  33.5 11.3 %collective-permute-start.9 = (bf16[256,640]{1,0:T(8,128)(2,1)S(1)}, bf16[256,640]{1,0:T(8,128)(2,1)S(1)}, u32[]{:S(2)}, u32[]{:S(2)}) collective-permute-start(bf16[256,640]{1,0:T(8,128)(2,1)S(1)} %collective-permute-done.refs_2_), channel_id=1, source_target_pairs={{0,2},{1,3},{2,4},{3,5},{4,6},{5,7},{6,0},{7,1},{8,10},{9,11},{10,... | collective-permute-start | bytes 983048 | tf_op jit(solution)/shard_map/ppermute | solution.py:37
  35.6 9.2 %collective-permute-start.13 = (bf16[256,640]{1,0:T(8,128)(2,1)}, bf16[256,640]{1,0:T(8,128)(2,1)S(1)}, u32[]{:S(2)}, u32[]{:S(2)}) collective-permute-start(bf16[256,640]{1,0:T(8,128)(2,1)} %collective-permute-done.12.refs_10_), channel_id=1, source_target_pairs={{0,1},{1,0},{2,3},{3,2},{4,5},{5,4},{6,7},{7,6},{8,9},{9,8},{10,11... | collective-permute-start | bytes 983048 | tf_op jit(solution)/shard_map/ppermute | solution.py:37
  35.8 9.1 %collective-permute-start.8 = (bf16[256,640]{1,0:T(8,128)(2,1)}, bf16[256,640]{1,0:T(8,128)(2,1)S(1)}, u32[]{:S(2)}, u32[]{:S(2)}) collective-permute-start(bf16[256,640]{1,0:T(8,128)(2,1)} %collective-permute-done.7.refs_4_), channel_id=1, source_target_pairs={{0,1},{1,0},{2,3},{3,2},{4,5},{5,4},{6,7},{7,6},{8,9},{9,8},{10,11... | collective-permute-start | bytes 983048 | tf_op jit(solution)/shard_map/ppermute | solution.py:37
  59.5 11.6 %collective-permute-start.19 = (bf16[384,512]{1,0:T(8,128)(2,1)S(1)}, bf16[384,512]{1,0:T(8,128)(2,1)S(1)}, u32[]{:S(2)}, u32[]{:S(2)}) collective-permute-start(bf16[384,512]{1,0:T(8,128)(2,1)S(1)} %get-tuple-element.41.refs_0_), channel_id=1, source_target_pairs={{0,96},{1,25},{2,98},{3,27},{4,100},{5,29},{6,102},{7,31},{8,104},... | collective-permute-start | bytes 1179656 | tf_op jit(solution)/shard_map/ppermute | solution.py:37
  62.2 12.9 %collective-permute-start.22 = (bf16[512,384]{1,0:T(8,128)(2,1)S(1)}, bf16[512,384]{1,0:T(8,128)(2,1)S(1)}, u32[]{:S(2)}, u32[]{:S(2)}) collective-permute-start(bf16[512,384]{1,0:T(8,128)(2,1)S(1)} %get-tuple-element.42.refs_5_), channel_id=1, source_target_pairs={{0,8},{1,33},{2,10},{3,35},{4,12},{5,37},{6,14},{7,39},{8,16},{9,4... | collective-permute-start | bytes 1179656 | tf_op jit(solution)/shard_map/ppermute | solution.py:37
  63.4 12.0 %collective-permute-start.26 = (bf16[384,512]{1,0:T(8,128)(2,1)S(1)}, bf16[384,512]{1,0:T(8,128)(2,1)S(1)}, u32[]{:S(2)}, u32[]{:S(2)}) collective-permute-start(bf16[384,512]{1,0:T(8,128)(2,1)S(1)} %get-tuple-element.43.refs_9_), channel_id=1, source_target_pairs={{0,24},{1,97},{2,26},{3,99},{4,28},{5,101},{6,30},{7,103},{8,0},{9... | collective-permute-start | bytes 1179656 | tf_op jit(solution)/shard_map/ppermute | solution.py:37
  65.4 13.0 %collective-permute-start.18 = (bf16[384,512]{1,0:T(8,128)(2,1)S(1)}, bf16[384,512]{1,0:T(8,128)(2,1)S(1)}, u32[]{:S(2)}, u32[]{:S(2)}) collective-permute-start(bf16[384,512]{1,0:T(8,128)(2,1)S(1)} %get-tuple-element.41.refs_0_), channel_id=1, source_target_pairs={{0,32},{1,9},{2,34},{3,11},{4,36},{5,13},{6,38},{7,15},{8,40},{9,1... | collective-permute-start | bytes 1179656 | tf_op jit(solution)/shard_map/ppermute | solution.py:37
  65.4 14.1 %collective-permute-start.23 = (bf16[512,384]{1,0:T(8,128)(2,1)S(1)}, bf16[512,384]{1,0:T(8,128)(2,1)S(1)}, u32[]{:S(2)}, u32[]{:S(2)}) collective-permute-start(bf16[512,384]{1,0:T(8,128)(2,1)S(1)} %get-tuple-element.42.refs_5_), channel_id=1, source_target_pairs={{0,24},{1,97},{2,26},{3,99},{4,28},{5,101},{6,30},{7,103},{8,0},{9... | collective-permute-start | bytes 1179656 | tf_op jit(solution)/shard_map/ppermute | solution.py:37
  71.2 9.7 %collective-permute-start.25 = (bf16[384,512]{1,0:T(8,128)(2,1)S(1)}, bf16[384,512]{1,0:T(8,128)(2,1)S(1)}, u32[]{:S(2)}, u32[]{:S(2)}) collective-permute-start(bf16[384,512]{1,0:T(8,128)(2,1)S(1)} %get-tuple-element.43.refs_9_), channel_id=1, source_target_pairs={{0,8},{1,33},{2,10},{3,35},{4,12},{5,37},{6,14},{7,39},{8,16},{9,4... | collective-permute-start | bytes 1179656 | tf_op jit(solution)/shard_map/ppermute | solution.py:37
  75.1 12.7 %collective-permute-start.24 = (bf16[512,384]{1,0:T(8,128)(2,1)S(1)}, bf16[512,384]{1,0:T(8,128)(2,1)S(1)}, u32[]{:S(2)}, u32[]{:S(2)}) collective-permute-start(bf16[512,384]{1,0:T(8,128)(2,1)S(1)} %collective-permute-done.22.refs_6_), channel_id=1, source_target_pairs={{0,8},{1,33},{2,10},{3,35},{4,12},{5,37},{6,14},{7,39},{8,16},{9,4... | collective-permute-start | bytes 1179656 | tf_op jit(solution)/shard_map/ppermute | solution.py:37
  75.3 13.3 %collective-permute-start.27 = (bf16[384,512]{1,0:T(8,128)(2,1)S(1)}, bf16[384,512]{1,0:T(8,128)(2,1)}, u32[]{:S(2)}, u32[]{:S(2)}) collective-permute-start(bf16[384,512]{1,0:T(8,128)(2,1)S(1)} %collective-permute-done.26.refs_11_), channel_id=1, source_target_pairs={{0,24},{1,97},{2,26},{3,99},{4,28},{5,101},{6,30},{7,103},{8,0},{9... | collective-permute-start | bytes 1179656 | tf_op jit(solution)/shard_map/ppermute | solution.py:37
  78.4 49.5 %collective-permute-start.38 = (bf16[2,384,640]{2,1,0:T(8,128)(2,1)}, bf16[2,384,640]{2,1,0:T(8,128)(2,1)}, u32[]{:S(2)}, u32[]{:S(2)}) collective-permute-start(bf16[2,384,640]{2,1,0:T(8,128)(2,1)} %get-tuple-element.49), channel_id=1, source_target_pairs={{0,2},{1,3},{2,4},{3,5},{4,6},{5,7},{6,0},{7,1},{8,10},{9,11},{10,... | collective-permute-start | bytes 2949128 | tf_op jit(solution)/shard_map/ppermute | solution.py:37
  99.5 14.1 %collective-permute-start.28 = (bf16[400,512]{1,0:T(8,128)(2,1)}, bf16[400,512]{1,0:T(8,128)(2,1)S(1)}, u32[]{:S(2)}, u32[]{:S(2)}) collective-permute-start(bf16[400,512]{1,0:T(8,128)(2,1)} %get-tuple-element.45), channel_id=1, source_target_pairs={{0,96},{1,25},{2,98},{3,27},{4,100},{5,29},{6,102},{7,31},{8,104},... | collective-permute-start | bytes 1228808 | tf_op jit(solution)/shard_map/ppermute | solution.py:37
  107.9 53.5 %collective-permute-start.39 = (bf16[2,384,640]{2,1,0:T(8,128)(2,1)}, bf16[2,384,640]{2,1,0:T(8,128)(2,1)S(1)}, u32[]{:S(2)}, u32[]{:S(2)}) collective-permute-start(bf16[2,384,640]{2,1,0:T(8,128)(2,1)} %get-tuple-element.50), channel_id=1, source_target_pairs={{0,6},{1,7},{2,0},{3,1},{4,2},{5,3},{6,4},{7,5},{8,14},{9,15},{10,... | collective-permute-start | bytes 2949128 | tf_op jit(solution)/shard_map/ppermute | solution.py:37
  109.9 13.8 %collective-permute-start.29 = (bf16[400,512]{1,0:T(8,128)(2,1)}, bf16[400,512]{1,0:T(8,128)(2,1)S(1)}, u32[]{:S(2)}, u32[]{:S(2)}) collective-permute-start(bf16[400,512]{1,0:T(8,128)(2,1)} %get-tuple-element.46), channel_id=1, source_target_pairs={{0,32},{1,9},{2,34},{3,11},{4,36},{5,13},{6,38},{7,15},{8,40},{9,1... | collective-permute-start | bytes 1228808 | tf_op jit(solution)/shard_map/ppermute | solution.py:37
  109.9 13.8 %collective-permute-start.30 = (bf16[400,512]{1,0:T(8,128)(2,1)}, bf16[400,512]{1,0:T(8,128)(2,1)S(1)}, u32[]{:S(2)}, u32[]{:S(2)}) collective-permute-start(bf16[400,512]{1,0:T(8,128)(2,1)} %get-tuple-element.47), channel_id=1, source_target_pairs={{0,64},{1,17},{2,66},{3,19},{4,68},{5,21},{6,70},{7,23},{8,72},{9,... | collective-permute-start | bytes 1228808 | tf_op jit(solution)/shard_map/ppermute | solution.py:37
  113.6 57.0 %collective-permute-start.40 = (bf16[2,384,640]{2,1,0:T(8,128)(2,1)}, bf16[2,384,640]{2,1,0:T(8,128)(2,1)S(1)}, u32[]{:S(2)}, u32[]{:S(2)}) collective-permute-start(bf16[2,384,640]{2,1,0:T(8,128)(2,1)} %get-tuple-element.51), channel_id=1, source_target_pairs={{0,4},{1,5},{2,6},{3,7},{4,0},{5,1},{6,2},{7,3},{8,12},{9,13},{10,... | collective-permute-start | bytes 2949128 | tf_op jit(solution)/shard_map/ppermute | solution.py:37
  125.1 36.3 %collective-permute-start.36 = (bf16[512,384]{1,0:T(8,128)(2,1)S(1)}, bf16[512,384]{1,0:T(8,128)(2,1)S(1)}, u32[]{:S(2)}, u32[]{:S(2)}) collective-permute-start(bf16[512,384]{1,0:T(8,128)(2,1)S(1)} %combine.1.refs_0_), channel_id=1, source_target_pairs={{0,4},{1,5},{2,6},{3,7},{4,0},{5,1},{6,2},{7,3},{8,12},{9,13},{10,... | collective-permute-start | bytes 1179656 | tf_op jit(solution)/shard_map/ppermute | solution.py:37
  126.1 44.1 %collective-permute-start.34 = (bf16[512,384]{1,0:T(8,128)(2,1)S(1)}, bf16[512,384]{1,0:T(8,128)(2,1)S(1)}, u32[]{:S(2)}, u32[]{:S(2)}) collective-permute-start(bf16[512,384]{1,0:T(8,128)(2,1)S(1)} %combine.1.refs_0_), channel_id=1, source_target_pairs={{0,6},{1,7},{2,0},{3,1},{4,2},{5,3},{6,4},{7,5},{8,14},{9,15},{10,... | collective-permute-start | bytes 1179656 | tf_op jit(solution)/shard_map/ppermute | solution.py:37
  127.9 42.6 %collective-permute-start.32 = (bf16[512,384]{1,0:T(8,128)(2,1)S(1)}, bf16[512,384]{1,0:T(8,128)(2,1)S(1)}, u32[]{:S(2)}, u32[]{:S(2)}) collective-permute-start(bf16[512,384]{1,0:T(8,128)(2,1)S(1)} %combine.1.refs_0_), channel_id=1, source_target_pairs={{0,2},{1,3},{2,4},{3,5},{4,6},{5,7},{6,0},{7,1},{8,10},{9,11},{10,... | collective-permute-start | bytes 1179656 | tf_op jit(solution)/shard_map/ppermute | solution.py:37
  161.4 9.3 %collective-permute-start.31 = (bf16[512,384]{1,0:T(8,128)(2,1)S(1)}, bf16[512,384]{1,0:T(8,128)(2,1)S(1)}, u32[]{:S(2)}, u32[]{:S(2)}) collective-permute-start(bf16[512,384]{1,0:T(8,128)(2,1)S(1)} %combine.1.refs_0_), channel_id=1, source_target_pairs={{0,1},{1,0},{2,3},{3,2},{4,5},{5,4},{6,7},{7,6},{8,9},{9,8},{10,11... | collective-permute-start | bytes 1179656 | tf_op jit(solution)/shard_map/ppermute | solution.py:37
  161.4 9.3 %collective-permute-start.37 = (bf16[512,384]{1,0:T(8,128)(2,1)S(1)}, bf16[512,384]{1,0:T(8,128)(2,1)S(1)}, u32[]{:S(2)}, u32[]{:S(2)}) collective-permute-start(bf16[512,384]{1,0:T(8,128)(2,1)S(1)} %collective-permute-done.36.refs_6_), channel_id=1, source_target_pairs={{0,1},{1,0},{2,3},{3,2},{4,5},{5,4},{6,7},{7,6},{8,9},{9,8},{10,11... | collective-permute-start | bytes 1179656 | tf_op jit(solution)/shard_map/ppermute | solution.py:37
  (32 other events, 311.0 us)
where the time goes:
time: 179 us; the launch traced here: 178 us
  waiting for transfers between devices  84.5 us (47%)
  starting transfers between devices  47.6 us (27%)
  Pallas kernels  29.5 us (16%)
  local copies, waits for them, and re-layouts  8.17 us (5%)
  other arithmetic  6.85 us (4%)
    ppermute x41, waiting for transfers between devices, permute(): return lax.ppermute(value, AXES, pairs)  84.5 us
    ppermute x41, starting transfers between devices, permute(): return lax.ppermute(value, AXES, pairs)  47.6 us
    pallas_call x1, Pallas kernels, project(): pl.pallas_call(project_kernel, in_specs=[pl.BlockSpec(memory_space=pltpu....  13 us
    pallas_call x1, Pallas kernels, attention(): pl.pallas_call(attention_kernel, in_specs=[pl.BlockSpec(memory_space=pltp...  10.9 us
    pallas_call x1, Pallas kernels, output(): pl.pallas_call(output_kernel, in_specs=[vmem] * 14, out_specs=vmem, out_s...  5.22 us
    another operation x2, other arithmetic, on_device(): w_pairs = [jnp.stack((w_parts[2 * n], w_other[n])) for n in range(SIDE)]  4.15 us
  transfers between devices with their start and end apart: 41, of which 14 were waited for; matrix products, arithmetic and copies ran while one was open for 5% of the time, Pallas kernels for 6%

commit v1 on v0

v1 whole, which is shorter than its diff:
```python
import functools
import math

import jax
import jax.numpy as jnp
from jax import lax
from jax.experimental import pallas as pl
from jax.experimental.pallas import tpu as pltpu
from jax.sharding import Mesh
from jax.sharding import PartitionSpec as P


HEAD_DIM = 128
HEADS_HERE = 3
WIDTH = HEADS_HERE * HEAD_DIM
SIDE = 4
ROWS = 512
HALF = ROWS // 2
EPSILON = 1e-06
NEG_FILL = -1e30
LOG2E = math.log2(math.e)
STEPS = (0, -1, 1, 2)
AXES = ("y", "x", "z", "core")
STAT_ROWS = 16


def permute(value, move):
    pairs = []
    for y in range(SIDE):
        for x in range(SIDE):
            for z in range(SIDE):
                for c in range(2):
                    source = ((y * SIDE + x) * SIDE + z) * 2 + c
                    ty, tx, tz, tc = move(y, x, z, c)
                    target = (((ty % SIDE) * SIDE + tx % SIDE) * SIDE + tz % SIDE) * 2 + tc
                    pairs.append((source, target))
    return lax.ppermute(value, AXES, pairs)


def along_z(step):
    return lambda y, x, z, c: (y, x, z + step, c)


def other_core(y, x, z, c):
    return (y, x, z, 1 - c)


def along_keys(step):
    return lambda y, x, z, c: (y, x + step, z, c) if c == 0 else (y + step, x, z, c)


def along_queries(step):
    return lambda y, x, z, c: (y + step, x, z, c) if c == 0 else (y, x + step, z, c)


def in_vmem(value):
    return pltpu.with_memory_space_constraint(value, pltpu.VMEM)


def project_kernel(places, *refs):
    pieces = refs[:16]
    mod_ref, gain_q, gain_k, *w_refs = refs[16:22]
    q_ref, k_ref, v_ref = refs[22:25]
    mean_ref, factor_ref, n_even, n_odd, acc_q, acc_k, acc_v, w_buf, sem = refs[25:]
    wide = pieces[0].shape[1]
    w_copies = []
    for n in range(SIDE):
        at = pl.ds(pl.multiple_of(places[n] * (2 * wide), 128), 2 * wide)
        for m in range(3):
            copy = pltpu.make_async_copy(w_refs[m].at[at], w_buf.at[n, m], sem.at[3 * n + m])
            copy.start()
            w_copies.append(copy)
    groups = wide // 128
    block = 64
    for half in range(2):
        here = pieces[half * 8 : half * 8 + 8]

        def chunk(n, carry, here=here, half=half):
            at = pl.ds(pl.multiple_of(n * block, block), block)
            total = jnp.zeros((block, 128), jnp.float32)
            square = jnp.zeros((block, 128), jnp.float32)
            for piece in here:
                for g in range(groups):
                    part = piece[at, g * 128 : (g + 1) * 128].astype(jnp.float32)
                    total = total + part
                    square = square + part * part
            mean = jnp.sum(total, axis=1, keepdims=True) * (1.0 / (8 * wide))
            mean_square = jnp.sum(square, axis=1, keepdims=True) * (1.0 / (8 * wide))
            factor = lax.rsqrt(mean_square - mean * mean + EPSILON)
            to = pl.ds(pl.multiple_of(half * HALF + n * block, block), block)
            mean_ref[to, :] = jnp.broadcast_to(mean, (block, 128))
            factor_ref[to, :] = jnp.broadcast_to(factor, (block, 128))
            return carry

        lax.fori_loop(0, HALF // block, chunk, 0)
    core = places[4]
    for n in range(SIDE):
        n_buf = n_odd if n % 2 else n_even
        start = places[n] * (2 * wide)
        for e in range(2):
            inside = (core if e == 0 else 1 - core) * wide
            at = pl.ds(pl.multiple_of(start + inside, 128), wide)
            shift = mod_ref[0:1, at]
            scale = 1.0 + mod_ref[1:2, at]
            for half in range(2):
                rows = slice(half * HALF, (half + 1) * HALF)
                mean = jnp.concatenate([mean_ref[rows, :]] * groups, axis=1)
                factor = jnp.concatenate([factor_ref[rows, :]] * groups, axis=1)
                value = pieces[half * 8 + 2 * n + e][...].astype(jnp.float32)
                normed = (value - mean) * factor * scale + shift
                n_buf[rows, pl.ds(pl.multiple_of(inside, 128), wide)] = normed.astype(jnp.bfloat16)
        for m, acc in ((0, acc_q), (1, acc_k), (2, acc_v)):
            w_copies[3 * n + m].wait()
            product = lax.dot_general(
                w_buf[n, m], n_buf[...], (((0,), (1,)), ((), ())), preferred_element_type=jnp.float32
            )
            if n == 0:
                acc[...] = product
            else:
                acc[...] += product
    for acc, gain, out, turn in ((acc_q, gain_q, q_ref, False), (acc_k, gain_k, k_ref, True)):
        for h in range(HEADS_HERE):
            cut = slice(h * HEAD_DIM, (h + 1) * HEAD_DIM)
            part = acc[cut, :]
            square = jnp.mean(part * part, axis=0, keepdims=True)
            gains = jnp.transpose(jnp.broadcast_to(gain[h : h + 1, :], (HEAD_DIM, HEAD_DIM)))
            gains = jnp.concatenate([gains] * (ROWS // HEAD_DIM), axis=1)
            scaled = part * lax.rsqrt(square + EPSILON) * gains
            if turn:
                out[:, cut] = jnp.transpose(scaled).astype(jnp.bfloat16)
            else:
                out[cut, :] = scaled.astype(jnp.bfloat16)
    v_ref[...] = acc_v[...].astype(jnp.bfloat16)


def project(pieces, places, modulation, gains, weights):
    wide = pieces[0].shape[1]
    vmem = pl.BlockSpec(memory_space=pltpu.VMEM)
    operands = [in_vmem(v) for v in (*pieces, modulation, *gains)]
    operands += [pltpu.with_memory_space_constraint(v, pltpu.HBM) for v in weights]
    return pl.pallas_call(
        project_kernel,
        in_specs=[pl.BlockSpec(memory_space=pltpu.SMEM)]
        + [vmem] * 19
        + [pl.BlockSpec(memory_space=pltpu.HBM)] * 3,
        out_specs=[vmem] * 3,
        out_shape=[
            pltpu.VMEM((WIDTH, ROWS), jnp.bfloat16),
            pltpu.VMEM((ROWS, WIDTH), jnp.bfloat16),
            pltpu.VMEM((WIDTH, ROWS), jnp.bfloat16),
        ],
        scratch_shapes=[
            pltpu.VMEM((ROWS, 128), jnp.float32),
            pltpu.VMEM((ROWS, 128), jnp.float32),
            pltpu.VMEM((ROWS, 2 * wide), jnp.bfloat16),
            pltpu.VMEM((ROWS, 2 * wide), jnp.bfloat16),
            pltpu.VMEM((WIDTH, ROWS), jnp.float32),
            pltpu.VMEM((WIDTH, ROWS), jnp.float32),
            pltpu.VMEM((WIDTH, ROWS), jnp.float32),
            pltpu.VMEM((SIDE, 3, 2 * wide, WIDTH), jnp.bfloat16),
            pltpu.SemaphoreType.DMA((3 * SIDE,)),
        ],
        compiler_params=pltpu.CompilerParams(vmem_limit_bytes=26 * 2**20),
        name="project",
    )(places, *operands)


GRAIN = 128
FAR_GRAIN = 256
SCALE = LOG2E / math.sqrt(HEAD_DIM)


def fold(queries, keys, values, live, depth, grain, acc_ref, stat_ref, i):
    tail = depth - grain
    rows = lax.broadcasted_iota(jnp.int32, (grain, ROWS), 0) + tail
    for h in range(HEADS_HERE):
        cut = slice(h * HEAD_DIM, (h + 1) * HEAD_DIM)
        query = queries(h)
        parts = []
        if tail > 0:
            parts.append(jnp.dot(keys(slice(0, tail), cut), query, preferred_element_type=jnp.float32))
        last = jnp.dot(keys(slice(tail, depth), cut), query, preferred_element_type=jnp.float32)
        parts.append(jnp.where(rows < live, last, NEG_FILL))
        before = stat_ref[i, h : h + 1, :]
        peak = before
        for part in parts:
            peak = jnp.maximum(peak, jnp.max(part, axis=0, keepdims=True))
        shift = peak * SCALE
        weights = [jnp.exp2(part * SCALE - shift) for part in parts]
        factor = jnp.exp2(before * SCALE - shift)
        total = stat_ref[i, 3 + h : 4 + h, :] * factor
        for weight in weights:
            total = total + jnp.sum(weight, axis=0, keepdims=True)
        narrow = [weight.astype(jnp.bfloat16) for weight in weights]
        joined = narrow[0] if len(narrow) == 1 else jnp.concatenate(narrow, axis=0)
        product = jnp.dot(values(cut, slice(0, depth)), joined, preferred_element_type=jnp.float32)
        acc_ref[i, cut, :] = acc_ref[i, cut, :] * factor + product
        stat_ref[i, h : h + 1, :] = peak
        stat_ref[i, 3 + h : 4 + h, :] = total


def each_size(wanted, live, grain, run):
    for depth in range(grain, ROWS + 1, grain):

        @pl.when((wanted == 1) & (live <= depth) & (live > depth - grain))
        def _(depth=depth):
            run(depth)


def clear(acc_ref, stat_ref, i):
    acc_ref[i] = jnp.zeros((WIDTH, ROWS), jnp.float32)
    stat_ref[i, 0:3, :] = jnp.full((3, ROWS), NEG_FILL, jnp.float32)
    stat_ref[i, 3:8, :] = jnp.zeros((5, ROWS), jnp.float32)


def finish(acc_ref, stat_ref, i, out_ref):
    stats = []
    for h in range(HEADS_HERE):
        cut = slice(h * HEAD_DIM, (h + 1) * HEAD_DIM)
        total = stat_ref[i, 3 + h : 4 + h, :]
        some = total > 0.0
        safe = jnp.where(some, total, 1.0)
        out_ref[cut, :] = (acc_ref[i, cut, :] / safe).astype(jnp.bfloat16)
        size = jnp.where(some, stat_ref[i, h : h + 1, :] * SCALE + jnp.log2(safe), NEG_FILL)
        high = size.astype(jnp.bfloat16).astype(jnp.float32)
        middle = (size - high).astype(jnp.bfloat16).astype(jnp.float32)
        stats += [high, middle, size - high - middle]
    stats.append(jnp.zeros((STAT_ROWS - len(stats), ROWS), jnp.float32))
    out_ref[WIDTH:, :] = jnp.concatenate(stats, axis=0).astype(jnp.bfloat16)


def near_kernel(allowed, counts, *refs):
    q_in, k_in, v_in = refs[0:3], refs[3:6], refs[6:9]
    acc_ref, stat_ref, q_buf, k_buf, v_buf, sem = refs[9:]
    copies = []
    for source, target in ((q_in, q_buf), (k_in, k_buf), (v_in, v_buf)):
        for n in range(3):
            copies.append(pltpu.make_async_copy(source[n], target.at[n], sem.at[len(copies)]))
    for copy in copies:
        copy.start()
    for i in range(3):
        clear(acc_ref, stat_ref, i)

    def pair(n, carry):
        i, j = n // 3, n % 3

        @pl.when(j == 0)
        def _():
            pltpu.make_async_copy(q_in[0], q_buf.at[i], sem.at[i]).wait()

        @pl.when(i == 0)
        def _():
            pltpu.make_async_copy(k_in[0], k_buf.at[j], sem.at[3 + j]).wait()
            pltpu.make_async_copy(v_in[0], v_buf.at[j], sem.at[6 + j]).wait()

        each_size(
            allowed[i * 4 + j],
            counts[j],
            GRAIN,
            lambda depth: fold(
                lambda h: q_buf[i, h * HEAD_DIM : (h + 1) * HEAD_DIM, :],
                lambda rows, cut: k_buf[j, rows, cut],
                lambda cut, rows: v_buf[j, cut, rows],
                counts[j],
                depth,
                GRAIN,
                acc_ref,
                stat_ref,
                i,
            ),
        )
        return carry

    lax.fori_loop(0, 9, pair, 0)


def attend_near(allowed, counts, queries, keys, values):
    vmem = pl.BlockSpec(memory_space=pltpu.VMEM)
    return pl.pallas_call(
        near_kernel,
        in_specs=[pl.BlockSpec(memory_space=pltpu.SMEM)] * 2 + [vmem] * 9,
        out_specs=[vmem] * 2,
        out_shape=[pltpu.VMEM((3, WIDTH, ROWS), jnp.float32), pltpu.VMEM((3, 8, ROWS), jnp.float32)],
        scratch_shapes=[
            pltpu.VMEM((3, WIDTH, ROWS), jnp.bfloat16),
            pltpu.VMEM((3, ROWS, WIDTH), jnp.bfloat16),
            pltpu.VMEM((3, WIDTH, ROWS), jnp.bfloat16),
            pltpu.SemaphoreType.DMA((9,)),
        ],
        compiler_params=pltpu.CompilerParams(vmem_limit_bytes=18 * 2**20),
        name="attend_near",
    )(allowed, counts, *[in_vmem(v) for v in (*queries, *keys, *values)])


def far_kernel(allowed, counts, *refs):
    q_in, k_in, v_in, acc_in, stat_in = refs[0:4], refs[4:8], refs[8:12], refs[12], refs[13]
    outs = refs[14:18]
    q_buf, k_buf, v_buf, acc_ref, stat_ref, sem = refs[18:]
    for n in range(4):
        pltpu.make_async_copy(k_in[n], k_buf.at[n], sem.at[n]).start()
        pltpu.make_async_copy(v_in[n], v_buf.at[n], sem.at[4 + n]).start()
    for n in range(3):
        pltpu.make_async_copy(q_in[n], q_buf.at[n], sem.at[8 + n]).start()
    q_buf[3] = q_in[3][...]
    stat_ref[:3] = stat_in[...]
    clear(acc_ref, stat_ref, 3)

    def block(n, carry):
        i = jnp.where(n < 4, 3, n - 4)
        j = jnp.minimum(n, 3)

        @pl.when(n < 4)
        def _():
            pltpu.make_async_copy(k_in[0], k_buf.at[j], sem.at[j]).wait()
            pltpu.make_async_copy(v_in[0], v_buf.at[j], sem.at[4 + j]).wait()

        @pl.when(n >= 4)
        def _():
            acc_ref[i] = acc_in[i]
            pltpu.make_async_copy(q_in[0], q_buf.at[i], sem.at[8 + i]).wait()

        each_size(
            allowed[i * 4 + j],
            counts[j],
            FAR_GRAIN,
            lambda depth: fold(
                lambda h: q_buf[i, h * HEAD_DIM : (h + 1) * HEAD_DIM, :],
                lambda rows, cut: k_buf[j, rows, cut],
                lambda cut, rows: v_buf[j, cut, rows],
                counts[j],
                depth,
                FAR_GRAIN,
                acc_ref,
                stat_ref,
                i,
            ),
        )
        return carry

    lax.fori_loop(0, 7, block, 0)
    for i in range(4):
        finish(acc_ref, stat_ref, i, outs[i])


def attend_far(allowed, counts, queries, keys, values, state):
    vmem = pl.BlockSpec(memory_space=pltpu.VMEM)
    return pl.pallas_call(
        far_kernel,
        in_specs=[pl.BlockSpec(memory_space=pltpu.SMEM)] * 2 + [vmem] * 14,
        out_specs=[vmem] * 4,
        out_shape=[pltpu.VMEM((WIDTH + STAT_ROWS, ROWS), jnp.bfloat16)] * 4,
        scratch_shapes=[
            pltpu.VMEM((4, WIDTH, ROWS), jnp.bfloat16),
            pltpu.VMEM((4, ROWS, WIDTH), jnp.bfloat16),
            pltpu.VMEM((4, WIDTH, ROWS), jnp.bfloat16),
            pltpu.VMEM((4, WIDTH, ROWS), jnp.float32),
            pltpu.VMEM((4, 8, ROWS), jnp.float32),
            pltpu.SemaphoreType.DMA((11,)),
        ],
        compiler_params=pltpu.CompilerParams(vmem_limit_bytes=22 * 2**20),
        name="attend_far",
    )(allowed, counts, *[in_vmem(v) for v in (*queries, *keys, *values, *state)])


def combine_kernel(*refs):
    parts, out_ref = refs[:4], refs[4]
    stats = [part[WIDTH:, :].astype(jnp.float32) for part in parts]
    for h in range(HEADS_HERE):
        sizes = [s[3 * h : 3 * h + 1] + s[3 * h + 1 : 3 * h + 2] + s[3 * h + 2 : 3 * h + 3] for s in stats]
        peak = functools.reduce(jnp.maximum, sizes)
        shares = [jnp.exp2(size - peak) for size in sizes]
        total = functools.reduce(jnp.add, shares)
        cut = slice(h * HEAD_DIM, (h + 1) * HEAD_DIM)
        merged = sum(part[cut, :].astype(jnp.float32) * (share / total) for part, share in zip(parts, shares))
        out_ref[:, cut] = jnp.transpose(merged).astype(jnp.bfloat16)


def combine(parts):
    vmem = pl.BlockSpec(memory_space=pltpu.VMEM)
    return pl.pallas_call(
        combine_kernel,
        in_specs=[vmem] * 4,
        out_specs=vmem,
        out_shape=pltpu.VMEM((ROWS, WIDTH), jnp.bfloat16),
        compiler_params=pltpu.CompilerParams(vmem_limit_bytes=8 * 2**20),
        name="combine",
    )(*[in_vmem(part) for part in parts])


def head_terms(attended, weights):
    for n, value in enumerate(attended):
        term = jnp.dot(value[...], weights[n // 2][n % 2], preferred_element_type=jnp.float32)
        yield term.astype(jnp.bfloat16).astype(jnp.float32)


def output_own_kernel(first_ref, second_ref, weight_ref, acc_ref):
    first, second = head_terms((first_ref, second_ref), (weight_ref,))
    acc_ref[...] = first + second


def output_rest_kernel(acc_in, *refs):
    attended, weights, latents_ref, gate_ref, out_ref, acc_ref = refs[:6], refs[6:9], *refs[9:]
    acc_ref[...] = acc_in[...]
    for n, term in enumerate(head_terms(attended, weights)):
        if n < 5:
            acc_ref[...] += term
        else:
            projected = acc_ref[...] + term
            updated = latents_ref[...].astype(jnp.float32) + gate_ref[...] * projected
            out_ref[...] = updated.astype(jnp.bfloat16)


def output_own(attended, weight):
    vmem = pl.BlockSpec(memory_space=pltpu.VMEM)
    return pl.pallas_call(
        output_own_kernel,
        in_specs=[vmem] * 3,
        out_specs=vmem,
        out_shape=pltpu.VMEM((ROWS, weight.shape[2]), jnp.float32),
        compiler_params=pltpu.CompilerParams(vmem_limit_bytes=10 * 2**20),
        name="output_own",
    )(*[in_vmem(v) for v in (*attended, weight)])


def output_rest(acc, attended, weights, latents, gate):
    vmem = pl.BlockSpec(memory_space=pltpu.VMEM)
    return pl.pallas_call(
        output_rest_kernel,
        in_specs=[vmem] * 12,
        out_specs=vmem,
        out_shape=jax.ShapeDtypeStruct(latents.shape, jnp.bfloat16),
        scratch_shapes=[pltpu.VMEM(latents.shape, jnp.float32)],
        compiler_params=pltpu.CompilerParams(vmem_limit_bytes=12 * 2**20),
        name="output_rest",
    )(*[in_vmem(v) for v in (acc, *attended, *weights, latents, gate)])


def take_kernel(places, w_ref, out_ref, sem):
    wide = out_ref.shape[2]
    copies = []
    for n in range(SIDE):
        columns = pl.ds(pl.multiple_of(places[2 * n + 1] * wide, 128), wide)
        copies.append(pltpu.make_async_copy(w_ref.at[:, columns], out_ref.at[n], sem.at[n]))
    for copy in copies:
        copy.start()
    for copy in copies:
        copy.wait()


def take_other(places, w_out, wide):
    return pl.pallas_call(
        take_kernel,
        in_specs=[pl.BlockSpec(memory_space=pltpu.SMEM), pl.BlockSpec(memory_space=pltpu.HBM)],
        out_specs=pl.BlockSpec(memory_space=pltpu.VMEM),
        out_shape=pltpu.VMEM((SIDE, WIDTH, wide), jnp.bfloat16),
        scratch_shapes=[pltpu.SemaphoreType.DMA((SIDE,))],
        compiler_params=pltpu.CompilerParams(vmem_limit_bytes=8 * 2**20),
        name="take_other",
    )(places, pltpu.with_memory_space_constraint(w_out, pltpu.HBM))


def pair_kernel(places, w_ref, other_ref, *refs):
    outs, (held, in_sem, own_sem, other_sem) = refs[:SIDE], refs[SIDE:]
    wide = other_ref.shape[2]
    arriving, leaving = [], []
    for n in range(SIDE):
        columns = pl.ds(pl.multiple_of(places[2 * n] * wide, 128), wide)
        arriving.append(pltpu.make_async_copy(w_ref.at[:, columns], held.at[n], in_sem.at[n]))
        arriving[n].start()
    for n in range(SIDE):
        leaving.append(pltpu.make_async_copy(other_ref.at[n], outs[n].at[1], other_sem.at[n]))
        leaving[n].start()
    for n in range(SIDE):
        arriving[n].wait()
        leaving.append(pltpu.make_async_copy(held.at[n], outs[n].at[0], own_sem.at[n]))
        leaving[SIDE + n].start()
    for copy in leaving:
        copy.wait()


def pair_up(places, w_out, w_other):
    hbm = pl.BlockSpec(memory_space=pltpu.HBM)
    return pl.pallas_call(
        pair_kernel,
        in_specs=[pl.BlockSpec(memory_space=pltpu.SMEM), hbm, pl.BlockSpec(memory_space=pltpu.VMEM)],
        out_specs=[hbm] * SIDE,
        out_shape=[pltpu.HBM((2, *w_other.shape[1:]), jnp.bfloat16)] * SIDE,
        scratch_shapes=[
            pltpu.VMEM(w_other.shape, jnp.bfloat16),
            pltpu.SemaphoreType.DMA((SIDE,)),
            pltpu.SemaphoreType.DMA((SIDE,)),
            pltpu.SemaphoreType.DMA((SIDE,)),
        ],
        compiler_params=pltpu.CompilerParams(vmem_limit_bytes=8 * 2**20),
        name="pair_up",
    )(places, pltpu.with_memory_space_constraint(w_out, pltpu.HBM), in_vmem(w_other))


def on_device(
    latents,
    w_query,
    w_key,
    w_value,
    w_out,
    query_gain,
    key_gain,
    mod_table,
    levels,
    span_counts,
    block_mask,
    span_order,
):
    shard_width = latents.shape[1]
    y, x, z, c = (lax.axis_index(name) for name in AXES)

    mask_low = permute(block_mask, along_queries(1))
    mask_high = permute(block_mask, along_queries(-1))
    mask_far = permute(block_mask, along_queries(2))
    mask_rows = jnp.concatenate([block_mask, mask_low, mask_high, mask_far])
    own = (latents[:HALF], latents[HALF:])
    below, above = [None, None], [None, None]
    below[0] = permute(own[0], along_z(1))
    above[1] = permute(own[1], along_z(-1))
    below[1] = permute(own[1], along_z(1))
    above[0] = permute(own[0], along_z(-1))

    places = [(z + step + SIDE) % SIDE * 2 + core for step in STEPS for core in (c, 1 - c)]
    columns = jnp.stack([(z + step + SIDE) % SIDE for step in STEPS] + [c]).astype(jnp.int32)
    modulation = lax.dynamic_index_in_dim(mod_table, levels[0], 0, keepdims=False)
    gate = lax.dynamic_slice(modulation, (2, places[0] * shard_width), (1, shard_width))

    def spans(along_x):
        return jnp.stack(
            [
                jnp.where(along_x, y * SIDE + (x + s + SIDE) % SIDE, (y + s + SIDE) % SIDE * SIDE + x)
                for s in STEPS
            ]
        )

    query_spans = spans(c == 1)
    key_spans = spans(c == 0)
    ids = jnp.arange(SIDE * SIDE, dtype=jnp.int32)
    pick_query = query_spans[:, None] == ids[None, :]
    pick_key = key_spans[:, None] == ids[None, :]
    query_rank = jnp.sum(jnp.where(pick_query, span_order[None, :], 0), axis=1)
    key_rank = jnp.sum(jnp.where(pick_key, span_order[None, :], 0), axis=1)
    counts = jnp.sum(jnp.where(pick_key, span_counts[None, :], 0), axis=1)
    w_places = jnp.stack(places).astype(jnp.int32)
    w_other = permute(take_other(w_places, w_out, shard_width), other_core)
    w_pairs = pair_up(w_places, w_out, w_other)

    far_low = permute(below[0], along_z(1))
    far_high = permute(above[1], along_z(-1))
    far_low, far_high, columns, modulation, w_pairs, mask_rows = lax.optimization_barrier(
        (far_low, far_high, columns, modulation, w_pairs, mask_rows)
    )
    far = (far_low, far_high)
    linked = jnp.sum(jnp.where(pick_key[None, :, :], mask_rows[:, None, :], 0), axis=2) == 1
    same = query_spans[:, None] == key_spans[None, :]
    allowed = ((key_rank[None, :] <= query_rank[:, None]) & (linked | same)).astype(jnp.int32).reshape(-1)
    pieces = []
    for half in range(2):
        for value in (own[half], below[half], above[half], far[half]):
            pieces += [value, permute(value, other_core)]
    w_below = permute(w_pairs[2], along_z(1))
    w_above = permute(w_pairs[1], along_z(-1))
    w_far = permute(w_pairs[3], along_z(2))
    query_own, key_own, value_own = project(
        pieces, columns, modulation, (query_gain, key_gain), (w_query, w_key, w_value)
    )

    key_low, key_high = permute(key_own, along_keys(1)), permute(key_own, along_keys(-1))
    value_low, value_high = permute(value_own, along_keys(1)), permute(value_own, along_keys(-1))
    query_low, query_high = permute(query_own, along_queries(1)), permute(query_own, along_queries(-1))
    w_blocks = (w_pairs[0], w_below, w_above, w_far)
    key_far = permute(key_low, along_keys(1))
    value_far = permute(value_high, along_keys(-1))
    query_far = permute(query_own, along_queries(2))

    near_queries = (query_own, query_low, query_high)
    near_keys = (key_own, key_low, key_high)
    near_values = (value_own, value_low, value_high)
    state = attend_near(allowed, counts, near_queries, near_keys, near_values)
    partial = attend_far(
        allowed,
        counts,
        (*near_queries, query_far),
        (*near_keys, key_far),
        (*near_values, value_far),
        state,
    )
    sent_far = permute(partial[3], along_queries(2))
    sent_low = permute(partial[1], along_queries(-1))
    sent_high = permute(partial[2], along_queries(1))
    attended = combine((partial[0], sent_low, sent_high, sent_far))

    shared_low = permute(attended, along_z(1))
    shared_high = permute(attended, along_z(-1))
    shared_far = permute(attended, along_z(2))
    own_other = permute(attended, other_core)
    low_other = permute(shared_low, other_core)
    high_other = permute(shared_high, other_core)
    acc = output_own((attended, own_other), w_blocks[0])
    rest = (shared_low, low_other, shared_high, high_other, shared_far, permute(shared_far, other_core))
    return output_rest(acc, rest, w_blocks[1:], latents, gate)


def solution(mesh):
    fine = Mesh(mesh.devices.reshape(SIDE, SIDE, SIDE, 2), AXES)
    frame, tensor = ("y", "x"), ("z", "core")

    return jax.shard_map(
        on_device,
        mesh=fine,
        in_specs=(
            P(frame, tensor),
            P(None, tensor),
            P(None, tensor),
            P(None, tensor),
            P(tensor, None),
            P(tensor, None),
            P(tensor, None),
            P(),
            P(frame),
            P(),
            P(frame, None),
            P(),
        ),
        out_specs=P(frame, tensor),
        check_vma=False,
    )
```

time: 179 us -> 195 us (1.089)
  the two profiles are of different devices: /device:TPU:0 before, /device:TPU:7 now
where the time goes in v1:
time: 195 us; the launch traced here: 194 us
  waiting for transfers between devices  81.6 us (42%)
  Pallas kernels  52.7 us (27%)
  starting transfers between devices  47.5 us (24%)
  local copies, waits for them, and re-layouts  8.94 us (5%)
  other arithmetic  2.61 us (1%)
    ppermute x40, waiting for transfers between devices, permute(): return lax.ppermute(value, AXES, pairs)  81.6 us
    ppermute x40, starting transfers between devices, permute(): return lax.ppermute(value, AXES, pairs)  47.5 us
    pallas_call x1, Pallas kernels, project(): pl.pallas_call(project_kernel, in_specs=[pl.BlockSpec(memory_space=pltpu....  13.9 us
    pallas_call x1, Pallas kernels, attend_near(): pl.pallas_call(near_kernel, in_specs=[pl.BlockSpec(memory_space=pltpu.SME...  12.1 us
    pallas_call x1, Pallas kernels, attend_far(): pl.pallas_call(far_kernel, in_specs=[pl.BlockSpec(memory_space=pltpu.SMEM...  11.9 us
    unnamed x31, local copies, waits for them, and re-layouts  7.93 us
    pallas_call x1, Pallas kernels, output_rest(): pl.pallas_call(output_rest_kernel, in_specs=[vmem] * 12, out_specs=vmem,...  5.38 us
    pallas_call x1, Pallas kernels, pair_up(): pl.pallas_call(pair_kernel, in_specs=[pl.BlockSpec(memory_space=pltpu.SME...  4.7 us
  transfers between devices with their start and end apart: 40, of which 14 were waited for; matrix products, arithmetic and copies ran while one was open for 2% of the time, Pallas kernels for 15%

profile of v1, /device:TPU:7, one launch (start us, length us, event | category | flops | bytes accessed | tf_op | source)
XLA Modules:
  0.0 194.3 jit_solution(3398417033178730221)
XLA Ops:
  0.2 3.3 %take_other.1 = bf16[4,384,640]{2,1,0:T(8,128)(2,1)} custom-call(s32[8]{0:T(128)S(1)} %stack.99.places, bf16[384,5120]{1,0:T(8,128)(2,1)} %w_ref.3), custom_call_target="tpu_custom_call" | custom-call | tf_op jit(solution)/shard_map/take_other/pallas_call | solution.py:451
  4.3 1.7 collective-permute-start
  6.0 2.2 %collective-permute-start.2 = (bf16[256,640]{1,0:T(8,128)(2,1)S(1)}, bf16[256,640]{1,0:T(8,128)(2,1)S(1)}, u32[]{:S(2)}, u32[]{:S(2)}) collective-permute-start(bf16[256,640]{1,0:T(8,128)(2,1)S(1)} %get-tuple-element.52.refs_8_), channel_id=1, source_target_pairs={{0,6},{1,7},{2,0},{3,1},{4,2},{5,3},{6,4},{7,5},{8,14},{9,15},{10,... | collective-permute-start | bytes 983048 | tf_op jit(solution)/shard_map/ppermute | solution.py:37
  8.2 8.0 %collective-permute-done.refs_2_ = bf16[256,640]{1,0:T(8,128)(2,1)S(1)} collective-permute-done((bf16[256,640]{1,0:T(8,128)(2,1)S(1)}, bf16[256,640]{1,0:T(8,128)(2,1)S(1)}, u32[]{:S(2)}, u32[]{:S(2)}) %collective-permute-start) | collective-permute-done | bytes 327712 | tf_op jit(solution)/shard_map/ppermute | solution.py:37
  16.2 2.7 %collective-permute-start.3 = (bf16[256,640]{1,0:T(8,128)(2,1)S(1)}, bf16[256,640]{1,0:T(8,128)(2,1)}, u32[]{:S(2)}, u32[]{:S(2)}) collective-permute-start(bf16[256,640]{1,0:T(8,128)(2,1)S(1)} %collective-permute-done.2.refs_12_), channel_id=1, source_target_pairs={{0,6},{1,7},{2,0},{3,1},{4,2},{5,3},{6,4},{7,5},{8,14},{9,15},{10,... | collective-permute-start | bytes 983048 | tf_op jit(solution)/shard_map/ppermute | solution.py:37
  19.1 1.3 collective-permute-start.6
  21.7 1.1 collective-permute-start.7
  23.0 2.6 %collective-permute-done.7 = s32[1,16]{1,0:T(1,128)S(1)} collective-permute-done((s32[1,16]{1,0:T(1,128)S(1)}, s32[1,16]{1,0:T(1,128)S(1)}, u32[]{:S(2)}, u32[]{:S(2)}) %collective-permute-start.7) | collective-permute-done | bytes 96 | tf_op jit(solution)/shard_map/ppermute | solution.py:37
  26.1 3.9 %collective-permute-start.13 = (bf16[256,640]{1,0:T(8,128)(2,1)S(1)}, bf16[256,640]{1,0:T(8,128)(2,1)}, u32[]{:S(2)}, u32[]{:S(2)}) collective-permute-start(bf16[256,640]{1,0:T(8,128)(2,1)S(1)} %get-tuple-element.52.refs_8_), channel_id=1, source_target_pairs={{0,1},{1,0},{2,3},{3,2},{4,5},{5,4},{6,7},{7,6},{8,9},{9,8},{10,11... | collective-permute-start | bytes 983048 | tf_op jit(solution)/shard_map/ppermute | solution.py:37
  31.9 4.7 %pair_up.1 = (bf16[2,384,640]{2,1,0:T(8,128)(2,1)}, bf16[2,384,640]{2,1,0:T(8,128)(2,1)}, bf16[2,384,640]{2,1,0:T(8,128)(2,1)}, bf16[2,384,640]{2,1,0:T(8,128)(2,1)}) custom-call(s32[8]{0:T(128)S(1)} %stack.99.places, bf16[384,5120]{1,0:T(8,128)(2,1)} %w_ref.3, bf16[4,384,640]{2,1,0:T(8,128)(2,1)} %collective-permute-done.4.other_ref), custom_call_target="tpu_custom_call" | custom-call | tf_op jit(solution)/shard_map/pair_up/pallas_call | solution.py:483
  36.8 1.5 collective-permute-start.11
  46.3 13.9 %project.1 = (bf16[384,512]{1,0:T(8,128)(2,1)S(1)}, bf16[512,384]{1,0:T(8,128)(2,1)S(1)}, bf16[384,512]{1,0:T(8,128)(2,1)S(1)}) custom-call(s32[5]{0:T(128)S(1)} %copy-done.11, bf16[256,640]{1,0:T(8,128)(2,1)S(1)} %get-tuple-element.53.refs_0_, bf16[256,640]{1,0:T(8,128)(2,1)} %collective-permute-done.8.refs_1_, bf16[256,640]{1,0:T(8,128)(2,1)S(1)} %copy-done.6, ...), custom_call_target="tpu_custom_call" | custom-call | tf_op jit(solution)/shard_map/project/pallas_call | solution.py:141
  60.5 1.2 collective-permute-start.19
  61.9 2.6 %collective-permute-start.25 = (bf16[384,512]{1,0:T(8,128)(2,1)S(1)}, bf16[384,512]{1,0:T(8,128)(2,1)}, u32[]{:S(2)}, u32[]{:S(2)}) collective-permute-start(bf16[384,512]{1,0:T(8,128)(2,1)S(1)} %get-tuple-element.38.refs_6_.refs_8_), channel_id=1, source_target_pairs={{0,24},{1,97},{2,26},{3,99},{4,28},{5,101},{6,30},{7,103},{8,0},{9... | collective-permute-start | bytes 1179656 | tf_op jit(solution)/shard_map/ppermute | solution.py:37
  65.0 2.4 %collective-permute-done.18.refs_1_ = bf16[384,512]{1,0:T(8,128)(2,1)S(1)} collective-permute-done((bf16[384,512]{1,0:T(8,128)(2,1)S(1)}, bf16[384,512]{1,0:T(8,128)(2,1)S(1)}, u32[]{:S(2)}, u32[]{:S(2)}) %collective-permute-start.18) | collective-permute-done | bytes 393248 | tf_op jit(solution)/shard_map/ppermute | solution.py:37
  67.4 1.3 collective-permute-start.24
  68.7 1.4 collective-permute-start.20
  70.2 3.5 %collective-permute-done.21.refs_4_.refs_5_ = bf16[512,384]{1,0:T(8,128)(2,1)} collective-permute-done((bf16[512,384]{1,0:T(8,128)(2,1)S(1)}, bf16[512,384]{1,0:T(8,128)(2,1)}, u32[]{:S(2)}, u32[]{:S(2)}) %collective-permute-start.21) | collective-permute-done | bytes 393248 | tf_op jit(solution)/shard_map/ppermute | solution.py:37
  73.6 3.0 %collective-permute-start.26 = (bf16[384,512]{1,0:T(8,128)(2,1)}, bf16[384,512]{1,0:T(8,128)(2,1)}, u32[]{:S(2)}, u32[]{:S(2)}) collective-permute-start(bf16[384,512]{1,0:T(8,128)(2,1)} %collective-permute-done.25.refs_8_.refs_10_), channel_id=1, source_target_pairs={{0,24},{1,97},{2,26},{3,99},{4,28},{5,101},{6,30},{7,103},{8,0},{9... | collective-permute-start | bytes 1179656 | tf_op jit(solution)/shard_map/ppermute | solution.py:37
  78.8 12.1 %attend_near.1 = (f32[3,384,512]{2,1,0:T(8,128)S(1)}, f32[3,8,512]{2,1,0:T(8,128)S(1)}) custom-call(s32[16]{0:T(128)S(1)} %reshape.39.allowed, s32[4]{0:T(128)S(1)} %get-tuple-element.49.counts, bf16[384,512]{1,0:T(8,128)(2,1)S(1)} %get-tuple-element.36.refs_0_, bf16[384,512]{1,0:T(8,128)(2,1)S(1)} %collective-permute-done.18.refs_1_, ...), custom_call_target="tpu_custom_call" | custom-call | tf_op jit(solution)/shard_map/attend_near/pallas_call | solution.py:279
  90.9 11.9 %attend_far.1 = (bf16[400,512]{1,0:T(8,128)(2,1)S(1)}, bf16[400,512]{1,0:T(8,128)(2,1)S(1)}, bf16[400,512]{1,0:T(8,128)(2,1)S(1)}, bf16[400,512]{1,0:T(8,128)(2,1)S(1)}) custom-call(s32[16]{0:T(128)S(1)} %reshape.39.allowed, s32[4]{0:T(128)S(1)} %get-tuple-element.49.counts, bf16[384,512]{1,0:T(8,128)(2,1)S(1)} %get-tuple-element.36.refs_0_, ...), custom_call_target="tpu_custom_call" | custom-call | tf_op jit(solution)/shard_map/attend_far/pallas_call | solution.py:347
  102.9 2.7 %collective-permute-start.28 = (bf16[400,512]{1,0:T(8,128)(2,1)S(1)}, bf16[400,512]{1,0:T(8,128)(2,1)S(1)}, u32[]{:S(2)}, u32[]{:S(2)}) collective-permute-start(bf16[400,512]{1,0:T(8,128)(2,1)S(1)} %get-tuple-element.43), channel_id=1, source_target_pairs={{0,32},{1,9},{2,34},{3,11},{4,36},{5,13},{6,38},{7,15},{8,40},{9,1... | collective-permute-start | bytes 1228808 | tf_op jit(solution)/shard_map/ppermute | solution.py:37
  106.7 8.9 %collective-permute-done.27.refs_1_ = bf16[400,512]{1,0:T(8,128)(2,1)S(1)} collective-permute-done((bf16[400,512]{1,0:T(8,128)(2,1)S(1)}, bf16[400,512]{1,0:T(8,128)(2,1)S(1)}, u32[]{:S(2)}, u32[]{:S(2)}) %collective-permute-start.27) | collective-permute-done | bytes 409632 | tf_op jit(solution)/shard_map/ppermute | solution.py:37
  116.0 6.5 %collective-permute-start.30 = (bf16[512,384]{1,0:T(8,128)(2,1)S(1)}, bf16[512,384]{1,0:T(8,128)(2,1)S(1)}, u32[]{:S(2)}, u32[]{:S(2)}) collective-permute-start(bf16[512,384]{1,0:T(8,128)(2,1)S(1)} %combine.1.first_ref), channel_id=1, source_target_pairs={{0,1},{1,0},{2,3},{3,2},{4,5},{5,4},{6,7},{7,6},{8,9},{9,8},{10,11... | collective-permute-start | bytes 1179656 | tf_op jit(solution)/shard_map/ppermute | solution.py:37
  122.6 2.9 %collective-permute-start.38 = (bf16[2,384,640]{2,1,0:T(8,128)(2,1)}, bf16[2,384,640]{2,1,0:T(8,128)(2,1)S(1)}, u32[]{:S(2)}, u32[]{:S(2)}) collective-permute-start(bf16[2,384,640]{2,1,0:T(8,128)(2,1)} %get-tuple-element.47), channel_id=1, source_target_pairs={{0,6},{1,7},{2,0},{3,1},{4,2},{5,3},{6,4},{7,5},{8,14},{9,15},{10,... | collective-permute-start | bytes 2949128 | tf_op jit(solution)/shard_map/ppermute | solution.py:37
  126.1 2.1 %collective-permute-start.33 = (bf16[512,384]{1,0:T(8,128)(2,1)S(1)}, bf16[512,384]{1,0:T(8,128)(2,1)}, u32[]{:S(2)}, u32[]{:S(2)}) collective-permute-start(bf16[512,384]{1,0:T(8,128)(2,1)S(1)} %combine.1.first_ref), channel_id=1, source_target_pairs={{0,6},{1,7},{2,0},{3,1},{4,2},{5,3},{6,4},{7,5},{8,14},{9,15},{10,... | collective-permute-start | bytes 1179656 | tf_op jit(solution)/shard_map/ppermute | solution.py:37
  129.0 1.8 collective-permute-start.35
  130.7 27.6 %collective-permute-done.31.refs_0_ = bf16[512,384]{1,0:T(8,128)(2,1)S(1)} collective-permute-done((bf16[512,384]{1,0:T(8,128)(2,1)S(1)}, bf16[512,384]{1,0:T(8,128)(2,1)S(1)}, u32[]{:S(2)}, u32[]{:S(2)}) %collective-permute-start.31) | collective-permute-done | bytes 393248 | tf_op jit(solution)/shard_map/ppermute | solution.py:37
  158.3 1.3 collective-permute-start.32
  159.6 24.9 %collective-permute-done.33.refs_2_ = bf16[512,384]{1,0:T(8,128)(2,1)} collective-permute-done((bf16[512,384]{1,0:T(8,128)(2,1)S(1)}, bf16[512,384]{1,0:T(8,128)(2,1)}, u32[]{:S(2)}, u32[]{:S(2)}) %collective-permute-start.33) | collective-permute-done | bytes 393248 | tf_op jit(solution)/shard_map/ppermute | solution.py:37
  185.7 1.2 copy-done.2
  188.9 5.4 %output_rest.1 = bf16[512,640]{1,0:T(8,128)(2,1)} custom-call(f32[512,640]{1,0:T(8,128)S(1)} %output_own.1.acc_in, bf16[512,384]{1,0:T(8,128)(2,1)S(1)} %collective-permute-done.31.refs_0_, bf16[512,384]{1,0:T(8,128)(2,1)} %collective-permute-done.32.refs_1_, bf16[512,384]{1,0:T(8,128)(2,1)} %collective-permute-done.33.refs_2_, ...), custom_call_target="tpu_custom_call" | custom-call | tf_op jit(solution)/shard_map/output_rest/pallas_call | solution.py:427
  (100 shorter events, 21.6 us)
Async XLA Ops:
  3.5 26.6 %collective-permute-start.4 = (bf16[4,384,640]{2,1,0:T(8,128)(2,1)}, bf16[4,384,640]{2,1,0:T(8,128)(2,1)}, u32[]{:S(2)}, u32[]{:S(2)}) collective-permute-start(bf16[4,384,640]{2,1,0:T(8,128)(2,1)} %take_other.1), channel_id=1, source_target_pairs={{0,1},{1,0},{2,3},{3,2},{4,5},{5,4},{6,7},{7,6},{8,9},{9,8},{10,11... | collective-permute-start | bytes 5898248 | tf_op jit(solution)/shard_map/ppermute | solution.py:37
  4.3 11.9 %collective-permute-start = (bf16[256,640]{1,0:T(8,128)(2,1)S(1)}, bf16[256,640]{1,0:T(8,128)(2,1)S(1)}, u32[]{:S(2)}, u32[]{:S(2)}) collective-permute-start(bf16[256,640]{1,0:T(8,128)(2,1)S(1)} %get-tuple-element.53.refs_0_), channel_id=1, source_target_pairs={{0,2},{1,3},{2,4},{3,5},{4,6},{5,7},{6,0},{7,1},{8,10},{9,11},{10,... | collective-permute-start | bytes 983048 | tf_op jit(solution)/shard_map/ppermute | solution.py:37
  6.0 10.2 %collective-permute-start.2 = (bf16[256,640]{1,0:T(8,128)(2,1)S(1)}, bf16[256,640]{1,0:T(8,128)(2,1)S(1)}, u32[]{:S(2)}, u32[]{:S(2)}) collective-permute-start(bf16[256,640]{1,0:T(8,128)(2,1)S(1)} %get-tuple-element.52.refs_8_), channel_id=1, source_target_pairs={{0,6},{1,7},{2,0},{3,1},{4,2},{5,3},{6,4},{7,5},{8,14},{9,15},{10,... | collective-permute-start | bytes 983048 | tf_op jit(solution)/shard_map/ppermute | solution.py:37
  16.2 9.9 %collective-permute-start.1 = (bf16[256,640]{1,0:T(8,128)(2,1)S(1)}, bf16[256,640]{1,0:T(8,128)(2,1)S(1)}, u32[]{:S(2)}, u32[]{:S(2)}) collective-permute-start(bf16[256,640]{1,0:T(8,128)(2,1)S(1)} %collective-permute-done.refs_2_), channel_id=1, source_target_pairs={{0,2},{1,3},{2,4},{3,5},{4,6},{5,7},{6,0},{7,1},{8,10},{9,11},{10,... | collective-permute-start | bytes 983048 | tf_op jit(solution)/shard_map/ppermute | solution.py:37
  16.2 13.8 %collective-permute-start.3 = (bf16[256,640]{1,0:T(8,128)(2,1)S(1)}, bf16[256,640]{1,0:T(8,128)(2,1)}, u32[]{:S(2)}, u32[]{:S(2)}) collective-permute-start(bf16[256,640]{1,0:T(8,128)(2,1)S(1)} %collective-permute-done.2.refs_12_), channel_id=1, source_target_pairs={{0,6},{1,7},{2,0},{3,1},{4,2},{5,3},{6,4},{7,5},{8,14},{9,15},{10,... | collective-permute-start | bytes 983048 | tf_op jit(solution)/shard_map/ppermute | solution.py:37
  19.1 3.9 %collective-permute-start.6 = (s32[1,16]{1,0:T(1,128)S(1)}, s32[1,16]{1,0:T(1,128)S(1)}, u32[]{:S(2)}, u32[]{:S(2)}) collective-permute-start(s32[1,16]{1,0:T(1,128)S(1)} %copy-done.14), channel_id=1, source_target_pairs={{0,96},{1,25},{2,98},{3,27},{4,100},{5,29},{6,102},{7,31},{8,104},... | collective-permute-start | bytes 200 | tf_op jit(solution)/shard_map/ppermute | solution.py:37
  23.0 13.6 %collective-permute-start.10 = (bf16[256,640]{1,0:T(8,128)(2,1)S(1)}, bf16[256,640]{1,0:T(8,128)(2,1)}, u32[]{:S(2)}, u32[]{:S(2)}) collective-permute-start(bf16[256,640]{1,0:T(8,128)(2,1)S(1)} %get-tuple-element.53.refs_0_), channel_id=1, source_target_pairs={{0,6},{1,7},{2,0},{3,1},{4,2},{5,3},{6,4},{7,5},{8,14},{9,15},{10,... | collective-permute-start | bytes 983048 | tf_op jit(solution)/shard_map/ppermute | solution.py:37
  25.6 11.1 %collective-permute-start.14 = (bf16[256,640]{1,0:T(8,128)(2,1)S(1)}, bf16[256,640]{1,0:T(8,128)(2,1)}, u32[]{:S(2)}, u32[]{:S(2)}) collective-permute-start(bf16[256,640]{1,0:T(8,128)(2,1)S(1)} %get-tuple-element.52.refs_8_), channel_id=1, source_target_pairs={{0,2},{1,3},{2,4},{3,5},{4,6},{5,7},{6,0},{7,1},{8,10},{9,11},{10,... | collective-permute-start | bytes 983048 | tf_op jit(solution)/shard_map/ppermute | solution.py:37
  26.1 12.2 %collective-permute-start.13 = (bf16[256,640]{1,0:T(8,128)(2,1)S(1)}, bf16[256,640]{1,0:T(8,128)(2,1)}, u32[]{:S(2)}, u32[]{:S(2)}) collective-permute-start(bf16[256,640]{1,0:T(8,128)(2,1)S(1)} %get-tuple-element.52.refs_8_), channel_id=1, source_target_pairs={{0,1},{1,0},{2,3},{3,2},{4,5},{5,4},{6,7},{7,6},{8,9},{9,8},{10,11... | collective-permute-start | bytes 983048 | tf_op jit(solution)/shard_map/ppermute | solution.py:37
  30.0 8.3 %collective-permute-start.8 = (bf16[256,640]{1,0:T(8,128)(2,1)S(1)}, bf16[256,640]{1,0:T(8,128)(2,1)}, u32[]{:S(2)}, u32[]{:S(2)}) collective-permute-start(bf16[256,640]{1,0:T(8,128)(2,1)S(1)} %get-tuple-element.53.refs_0_), channel_id=1, source_target_pairs={{0,1},{1,0},{2,3},{3,2},{4,5},{5,4},{6,7},{7,6},{8,9},{9,8},{10,11... | collective-permute-start | bytes 983048 | tf_op jit(solution)/shard_map/ppermute | solution.py:37
  30.1 8.7 %collective-permute-start.16 = (bf16[256,640]{1,0:T(8,128)(2,1)S(1)}, bf16[256,640]{1,0:T(8,128)(2,1)}, u32[]{:S(2)}, u32[]{:S(2)}) collective-permute-start(bf16[256,640]{1,0:T(8,128)(2,1)S(1)} %collective-permute-done.2.refs_12_), channel_id=1, source_target_pairs={{0,1},{1,0},{2,3},{3,2},{4,5},{5,4},{6,7},{7,6},{8,9},{9,8},{10,11... | collective-permute-start | bytes 983048 | tf_op jit(solution)/shard_map/ppermute | solution.py:37
  60.2 7.2 %collective-permute-start.18 = (bf16[384,512]{1,0:T(8,128)(2,1)S(1)}, bf16[384,512]{1,0:T(8,128)(2,1)S(1)}, u32[]{:S(2)}, u32[]{:S(2)}) collective-permute-start(bf16[384,512]{1,0:T(8,128)(2,1)S(1)} %get-tuple-element.36.refs_0_), channel_id=1, source_target_pairs={{0,32},{1,9},{2,34},{3,11},{4,36},{5,13},{6,38},{7,15},{8,40},{9,1... | collective-permute-start | bytes 1179656 | tf_op jit(solution)/shard_map/ppermute | solution.py:37
  60.5 8.2 %collective-permute-start.19 = (bf16[384,512]{1,0:T(8,128)(2,1)S(1)}, bf16[384,512]{1,0:T(8,128)(2,1)}, u32[]{:S(2)}, u32[]{:S(2)}) collective-permute-start(bf16[384,512]{1,0:T(8,128)(2,1)S(1)} %get-tuple-element.36.refs_0_), channel_id=1, source_target_pairs={{0,96},{1,25},{2,98},{3,27},{4,100},{5,29},{6,102},{7,31},{8,104},... | collective-permute-start | bytes 1179656 | tf_op jit(solution)/shard_map/ppermute | solution.py:37
  61.7 11.9 %collective-permute-start.21 = (bf16[512,384]{1,0:T(8,128)(2,1)S(1)}, bf16[512,384]{1,0:T(8,128)(2,1)}, u32[]{:S(2)}, u32[]{:S(2)}) collective-permute-start(bf16[512,384]{1,0:T(8,128)(2,1)S(1)} %get-tuple-element.37.refs_3_.refs_4_), channel_id=1, source_target_pairs={{0,8},{1,33},{2,10},{3,35},{4,12},{5,37},{6,14},{7,39},{8,16},{9,4... | collective-permute-start | bytes 1179656 | tf_op jit(solution)/shard_map/ppermute | solution.py:37
  61.9 11.8 %collective-permute-start.25 = (bf16[384,512]{1,0:T(8,128)(2,1)S(1)}, bf16[384,512]{1,0:T(8,128)(2,1)}, u32[]{:S(2)}, u32[]{:S(2)}) collective-permute-start(bf16[384,512]{1,0:T(8,128)(2,1)S(1)} %get-tuple-element.38.refs_6_.refs_8_), channel_id=1, source_target_pairs={{0,24},{1,97},{2,26},{3,99},{4,28},{5,101},{6,30},{7,103},{8,0},{9... | collective-permute-start | bytes 1179656 | tf_op jit(solution)/shard_map/ppermute | solution.py:37
  64.5 13.8 %collective-permute-start.22 = (bf16[512,384]{1,0:T(8,128)(2,1)S(1)}, bf16[512,384]{1,0:T(8,128)(2,1)}, u32[]{:S(2)}, u32[]{:S(2)}) collective-permute-start(bf16[512,384]{1,0:T(8,128)(2,1)S(1)} %get-tuple-element.37.refs_3_.refs_4_), channel_id=1, source_target_pairs={{0,24},{1,97},{2,26},{3,99},{4,28},{5,101},{6,30},{7,103},{8,0},{9... | collective-permute-start | bytes 1179656 | tf_op jit(solution)/shard_map/ppermute | solution.py:37
  67.4 11.3 %collective-permute-start.24 = (bf16[384,512]{1,0:T(8,128)(2,1)S(1)}, bf16[384,512]{1,0:T(8,128)(2,1)}, u32[]{:S(2)}, u32[]{:S(2)}) collective-permute-start(bf16[384,512]{1,0:T(8,128)(2,1)S(1)} %get-tuple-element.38.refs_6_.refs_8_), channel_id=1, source_target_pairs={{0,8},{1,33},{2,10},{3,35},{4,12},{5,37},{6,14},{7,39},{8,16},{9,4... | collective-permute-start | bytes 1179656 | tf_op jit(solution)/shard_map/ppermute | solution.py:37
  68.7 22.2 %collective-permute-start.20 = (bf16[384,512]{1,0:T(8,128)(2,1)S(1)}, bf16[384,512]{1,0:T(8,128)(2,1)}, u32[]{:S(2)}, u32[]{:S(2)}) collective-permute-start(bf16[384,512]{1,0:T(8,128)(2,1)S(1)} %get-tuple-element.36.refs_0_), channel_id=1, source_target_pairs={{0,64},{1,17},{2,66},{3,19},{4,68},{5,21},{6,70},{7,23},{8,72},{9,... | collective-permute-start | bytes 1179656 | tf_op jit(solution)/shard_map/ppermute | solution.py:37
  73.6 17.3 %collective-permute-start.23 = (bf16[512,384]{1,0:T(8,128)(2,1)}, bf16[512,384]{1,0:T(8,128)(2,1)}, u32[]{:S(2)}, u32[]{:S(2)}) collective-permute-start(bf16[512,384]{1,0:T(8,128)(2,1)} %collective-permute-done.21.refs_4_.refs_5_), channel_id=1, source_target_pairs={{0,8},{1,33},{2,10},{3,35},{4,12},{5,37},{6,14},{7,39},{8,16},{9,4... | collective-permute-start | bytes 1179656 | tf_op jit(solution)/shard_map/ppermute | solution.py:37
  73.6 17.3 %collective-permute-start.26 = (bf16[384,512]{1,0:T(8,128)(2,1)}, bf16[384,512]{1,0:T(8,128)(2,1)}, u32[]{:S(2)}, u32[]{:S(2)}) collective-permute-start(bf16[384,512]{1,0:T(8,128)(2,1)} %collective-permute-done.25.refs_8_.refs_10_), channel_id=1, source_target_pairs={{0,24},{1,97},{2,26},{3,99},{4,28},{5,101},{6,30},{7,103},{8,0},{9... | collective-permute-start | bytes 1179656 | tf_op jit(solution)/shard_map/ppermute | solution.py:37
  78.3 47.8 %collective-permute-start.37 = (bf16[2,384,640]{2,1,0:T(8,128)(2,1)}, bf16[2,384,640]{2,1,0:T(8,128)(2,1)}, u32[]{:S(2)}, u32[]{:S(2)}) collective-permute-start(bf16[2,384,640]{2,1,0:T(8,128)(2,1)} %get-tuple-element.46), channel_id=1, source_target_pairs={{0,2},{1,3},{2,4},{3,5},{4,6},{5,7},{6,0},{7,1},{8,10},{9,11},{10,... | collective-permute-start | bytes 2949128 | tf_op jit(solution)/shard_map/ppermute | solution.py:37
  102.8 12.8 %collective-permute-start.27 = (bf16[400,512]{1,0:T(8,128)(2,1)S(1)}, bf16[400,512]{1,0:T(8,128)(2,1)S(1)}, u32[]{:S(2)}, u32[]{:S(2)}) collective-permute-start(bf16[400,512]{1,0:T(8,128)(2,1)S(1)} %get-tuple-element.42), channel_id=1, source_target_pairs={{0,96},{1,25},{2,98},{3,27},{4,100},{5,29},{6,102},{7,31},{8,104},... | collective-permute-start | bytes 1228808 | tf_op jit(solution)/shard_map/ppermute | solution.py:37
  102.9 12.7 %collective-permute-start.28 = (bf16[400,512]{1,0:T(8,128)(2,1)S(1)}, bf16[400,512]{1,0:T(8,128)(2,1)S(1)}, u32[]{:S(2)}, u32[]{:S(2)}) collective-permute-start(bf16[400,512]{1,0:T(8,128)(2,1)S(1)} %get-tuple-element.43), channel_id=1, source_target_pairs={{0,32},{1,9},{2,34},{3,11},{4,36},{5,13},{6,38},{7,15},{8,40},{9,1... | collective-permute-start | bytes 1228808 | tf_op jit(solution)/shard_map/ppermute | solution.py:37
  105.6 10.0 %collective-permute-start.29 = (bf16[400,512]{1,0:T(8,128)(2,1)S(1)}, bf16[400,512]{1,0:T(8,128)(2,1)S(1)}, u32[]{:S(2)}, u32[]{:S(2)}) collective-permute-start(bf16[400,512]{1,0:T(8,128)(2,1)S(1)} %get-tuple-element.44), channel_id=1, source_target_pairs={{0,64},{1,17},{2,66},{3,19},{4,68},{5,21},{6,70},{7,23},{8,72},{9,... | collective-permute-start | bytes 1228808 | tf_op jit(solution)/shard_map/ppermute | solution.py:37
  116.0 12.2 %collective-permute-start.30 = (bf16[512,384]{1,0:T(8,128)(2,1)S(1)}, bf16[512,384]{1,0:T(8,128)(2,1)S(1)}, u32[]{:S(2)}, u32[]{:S(2)}) collective-permute-start(bf16[512,384]{1,0:T(8,128)(2,1)S(1)} %combine.1.first_ref), channel_id=1, source_target_pairs={{0,1},{1,0},{2,3},{3,2},{4,5},{5,4},{6,7},{7,6},{8,9},{9,8},{10,11... | collective-permute-start | bytes 1179656 | tf_op jit(solution)/shard_map/ppermute | solution.py:37
  122.6 66.3 %collective-permute-start.38 = (bf16[2,384,640]{2,1,0:T(8,128)(2,1)}, bf16[2,384,640]{2,1,0:T(8,128)(2,1)S(1)}, u32[]{:S(2)}, u32[]{:S(2)}) collective-permute-start(bf16[2,384,640]{2,1,0:T(8,128)(2,1)} %get-tuple-element.47), channel_id=1, source_target_pairs={{0,6},{1,7},{2,0},{3,1},{4,2},{5,3},{6,4},{7,5},{8,14},{9,15},{10,... | collective-permute-start | bytes 2949128 | tf_op jit(solution)/shard_map/ppermute | solution.py:37
  125.5 63.3 %collective-permute-start.39 = (bf16[2,384,640]{2,1,0:T(8,128)(2,1)}, bf16[2,384,640]{2,1,0:T(8,128)(2,1)}, u32[]{:S(2)}, u32[]{:S(2)}) collective-permute-start(bf16[2,384,640]{2,1,0:T(8,128)(2,1)} %get-tuple-element.48), channel_id=1, source_target_pairs={{0,4},{1,5},{2,6},{3,7},{4,0},{5,1},{6,2},{7,3},{8,12},{9,13},{10,... | collective-permute-start | bytes 2949128 | tf_op jit(solution)/shard_map/ppermute | solution.py:37
  125.5 32.8 %collective-permute-start.31 = (bf16[512,384]{1,0:T(8,128)(2,1)S(1)}, bf16[512,384]{1,0:T(8,128)(2,1)S(1)}, u32[]{:S(2)}, u32[]{:S(2)}) collective-permute-start(bf16[512,384]{1,0:T(8,128)(2,1)S(1)} %combine.1.first_ref), channel_id=1, source_target_pairs={{0,2},{1,3},{2,4},{3,5},{4,6},{5,7},{6,0},{7,1},{8,10},{9,11},{10,... | collective-permute-start | bytes 1179656 | tf_op jit(solution)/shard_map/ppermute | solution.py:37
  126.1 58.4 %collective-permute-start.33 = (bf16[512,384]{1,0:T(8,128)(2,1)S(1)}, bf16[512,384]{1,0:T(8,128)(2,1)}, u32[]{:S(2)}, u32[]{:S(2)}) collective-permute-start(bf16[512,384]{1,0:T(8,128)(2,1)S(1)} %combine.1.first_ref), channel_id=1, source_target_pairs={{0,6},{1,7},{2,0},{3,1},{4,2},{5,3},{6,4},{7,5},{8,14},{9,15},{10,... | collective-permute-start | bytes 1179656 | tf_op jit(solution)/shard_map/ppermute | solution.py:37
  129.0 56.7 %collective-permute-start.35 = (bf16[512,384]{1,0:T(8,128)(2,1)S(1)}, bf16[512,384]{1,0:T(8,128)(2,1)}, u32[]{:S(2)}, u32[]{:S(2)}) collective-permute-start(bf16[512,384]{1,0:T(8,128)(2,1)S(1)} %combine.1.first_ref), channel_id=1, source_target_pairs={{0,4},{1,5},{2,6},{3,7},{4,0},{5,1},{6,2},{7,3},{8,12},{9,13},{10,... | collective-permute-start | bytes 1179656 | tf_op jit(solution)/shard_map/ppermute | solution.py:37
  158.3 30.5 %collective-permute-start.32 = (bf16[512,384]{1,0:T(8,128)(2,1)S(1)}, bf16[512,384]{1,0:T(8,128)(2,1)}, u32[]{:S(2)}, u32[]{:S(2)}) collective-permute-start(bf16[512,384]{1,0:T(8,128)(2,1)S(1)} %collective-permute-done.31.refs_0_), channel_id=1, source_target_pairs={{0,1},{1,0},{2,3},{3,2},{4,5},{5,4},{6,7},{7,6},{8,9},{9,8},{10,11... | collective-permute-start | bytes 1179656 | tf_op jit(solution)/shard_map/ppermute | solution.py:37
  184.5 4.3 %collective-permute-start.34 = (bf16[512,384]{1,0:T(8,128)(2,1)}, bf16[512,384]{1,0:T(8,128)(2,1)}, u32[]{:S(2)}, u32[]{:S(2)}) collective-permute-start(bf16[512,384]{1,0:T(8,128)(2,1)} %collective-permute-done.33.refs_2_), channel_id=1, source_target_pairs={{0,1},{1,0},{2,3},{3,2},{4,5},{5,4},{6,7},{7,6},{8,9},{9,8},{10,11... | collective-permute-start | bytes 1179656 | tf_op jit(solution)/shard_map/ppermute | solution.py:37
  (23 other events, 148.3 us)

commit v2 on v1

--- a/solution.py
+++ b/solution.py
@@ -166,21 +166,25 @@
 
 
 GRAIN = 128
-FAR_GRAIN = 256
+FAR_GRAIN = 128
 SCALE = LOG2E / math.sqrt(HEAD_DIM)
 
 
 def fold(queries, keys, values, live, depth, grain, acc_ref, stat_ref, i):
     tail = depth - grain
     rows = lax.broadcasted_iota(jnp.int32, (grain, ROWS), 0) + tail
-    for h in range(HEADS_HERE):
-        cut = slice(h * HEAD_DIM, (h + 1) * HEAD_DIM)
+    cuts = [slice(h * HEAD_DIM, (h + 1) * HEAD_DIM) for h in range(HEADS_HERE)]
+    scores = []
+    for h, cut in enumerate(cuts):
         query = queries(h)
         parts = []
         if tail > 0:
             parts.append(jnp.dot(keys(slice(0, tail), cut), query, preferred_element_type=jnp.float32))
         last = jnp.dot(keys(slice(tail, depth), cut), query, preferred_element_type=jnp.float32)
         parts.append(jnp.where(rows < live, last, NEG_FILL))
+        scores.append(parts)
+    joined, factors = [], []
+    for h, parts in enumerate(scores):
         before = stat_ref[i, h : h + 1, :]
         peak = before
         for part in parts:
@@ -192,11 +196,13 @@
         for weight in weights:
             total = total + jnp.sum(weight, axis=0, keepdims=True)
         narrow = [weight.astype(jnp.bfloat16) for weight in weights]
-        joined = narrow[0] if len(narrow) == 1 else jnp.concatenate(narrow, axis=0)
-        product = jnp.dot(values(cut, slice(0, depth)), joined, preferred_element_type=jnp.float32)
-        acc_ref[i, cut, :] = acc_ref[i, cut, :] * factor + product
+        joined.append(narrow[0] if len(narrow) == 1 else jnp.concatenate(narrow, axis=0))
+        factors.append(factor)
         stat_ref[i, h : h + 1, :] = peak
         stat_ref[i, 3 + h : 4 + h, :] = total
+    for h, cut in enumerate(cuts):
+        product = jnp.dot(values(cut, slice(0, depth)), joined[h], preferred_element_type=jnp.float32)
+        acc_ref[i, cut, :] = acc_ref[i, cut, :] * factors[h] + product
 
 
 def each_size(wanted, live, grain, run):

time: 195 us -> 191 us (0.979)
  Pallas kernels: 52.7 us -> 49.3 us
  transfers between devices with their start and end apart: 40 -> 40, of which waited for: 14 -> 14; matrix products, arithmetic and copies ran while one was open for 2% -> 2% of each run, Pallas kernels for 15% -> 14%
where the time goes in v2:
time: 191 us
  waiting for transfers between devices  82.3 us (43%)
  Pallas kernels  49.3 us (26%)
  starting transfers between devices  46.7 us (24%)
  local copies, waits for them, and re-layouts  8.94 us (5%)
  other arithmetic  2.61 us (1%)
    ppermute x40, waiting for transfers between devices, permute(): return lax.ppermute(value, AXES, pairs)  82.3 us
    ppermute x40, starting transfers between devices, permute(): return lax.ppermute(value, AXES, pairs)  46.7 us
    pallas_call x1, Pallas kernels, project(): pl.pallas_call(project_kernel, in_specs=[pl.BlockSpec(memory_space=pltpu....  13.9 us
    pallas_call x1, Pallas kernels, attend_far(): pl.pallas_call(far_kernel, in_specs=[pl.BlockSpec(memory_space=pltpu.SMEM...  10.3 us
    pallas_call x1, Pallas kernels, attend_near(): pl.pallas_call(near_kernel, in_specs=[pl.BlockSpec(memory_space=pltpu.SME...  10.2 us
    unnamed x31, local copies, waits for them, and re-layouts  7.93 us
    pallas_call x1, Pallas kernels, output_rest(): pl.pallas_call(output_rest_kernel, in_specs=[vmem] * 12, out_specs=vmem,...  5.38 us
    pallas_call x1, Pallas kernels, pair_up(): pl.pallas_call(pair_kernel, in_specs=[pl.BlockSpec(memory_space=pltpu.SME...  4.7 us
  transfers between devices with their start and end apart: 40, of which 14 were waited for; matrix products, arithmetic and copies ran while one was open for 2% of the time, Pallas kernels for 14%

profile of v2, /device:TPU:7, one launch (start us, length us, event | category | flops | bytes accessed | tf_op | source)
XLA Modules:
  0.0 190.8 jit_solution(10834944642381409206)
XLA Ops:
  0.2 3.3 %take_other.1 = bf16[4,384,640]{2,1,0:T(8,128)(2,1)} custom-call(s32[8]{0:T(128)S(1)} %stack.99.places, bf16[384,5120]{1,0:T(8,128)(2,1)} %w_ref.3), custom_call_target="tpu_custom_call" | custom-call | tf_op jit(solution)/shard_map/take_other/pallas_call | solution.py:457
  4.3 1.7 collective-permute-start
  6.0 2.2 %collective-permute-start.2 = (bf16[256,640]{1,0:T(8,128)(2,1)S(1)}, bf16[256,640]{1,0:T(8,128)(2,1)S(1)}, u32[]{:S(2)}, u32[]{:S(2)}) collective-permute-start(bf16[256,640]{1,0:T(8,128)(2,1)S(1)} %get-tuple-element.52.refs_8_), channel_id=1, source_target_pairs={{0,6},{1,7},{2,0},{3,1},{4,2},{5,3},{6,4},{7,5},{8,14},{9,15},{10,... | collective-permute-start | bytes 983048 | tf_op jit(solution)/shard_map/ppermute | solution.py:37
  8.2 8.0 %collective-permute-done.refs_2_ = bf16[256,640]{1,0:T(8,128)(2,1)S(1)} collective-permute-done((bf16[256,640]{1,0:T(8,128)(2,1)S(1)}, bf16[256,640]{1,0:T(8,128)(2,1)S(1)}, u32[]{:S(2)}, u32[]{:S(2)}) %collective-permute-start) | collective-permute-done | bytes 327712 | tf_op jit(solution)/shard_map/ppermute | solution.py:37
  16.2 2.7 %collective-permute-start.3 = (bf16[256,640]{1,0:T(8,128)(2,1)S(1)}, bf16[256,640]{1,0:T(8,128)(2,1)}, u32[]{:S(2)}, u32[]{:S(2)}) collective-permute-start(bf16[256,640]{1,0:T(8,128)(2,1)S(1)} %collective-permute-done.2.refs_12_), channel_id=1, source_target_pairs={{0,6},{1,7},{2,0},{3,1},{4,2},{5,3},{6,4},{7,5},{8,14},{9,15},{10,... | collective-permute-start | bytes 983048 | tf_op jit(solution)/shard_map/ppermute | solution.py:37
  19.1 1.3 collective-permute-start.6
  21.7 1.1 collective-permute-start.7
  23.0 2.6 %collective-permute-done.7 = s32[1,16]{1,0:T(1,128)S(1)} collective-permute-done((s32[1,16]{1,0:T(1,128)S(1)}, s32[1,16]{1,0:T(1,128)S(1)}, u32[]{:S(2)}, u32[]{:S(2)}) %collective-permute-start.7) | collective-permute-done | bytes 96 | tf_op jit(solution)/shard_map/ppermute | solution.py:37
  26.1 3.9 %collective-permute-start.13 = (bf16[256,640]{1,0:T(8,128)(2,1)S(1)}, bf16[256,640]{1,0:T(8,128)(2,1)}, u32[]{:S(2)}, u32[]{:S(2)}) collective-permute-start(bf16[256,640]{1,0:T(8,128)(2,1)S(1)} %get-tuple-element.52.refs_8_), channel_id=1, source_target_pairs={{0,1},{1,0},{2,3},{3,2},{4,5},{5,4},{6,7},{7,6},{8,9},{9,8},{10,11... | collective-permute-start | bytes 983048 | tf_op jit(solution)/shard_map/ppermute | solution.py:37
  31.9 4.7 %pair_up.1 = (bf16[2,384,640]{2,1,0:T(8,128)(2,1)}, bf16[2,384,640]{2,1,0:T(8,128)(2,1)}, bf16[2,384,640]{2,1,0:T(8,128)(2,1)}, bf16[2,384,640]{2,1,0:T(8,128)(2,1)}) custom-call(s32[8]{0:T(128)S(1)} %stack.99.places, bf16[384,5120]{1,0:T(8,128)(2,1)} %w_ref.3, bf16[4,384,640]{2,1,0:T(8,128)(2,1)} %collective-permute-done.4.other_ref), custom_call_target="tpu_custom_call" | custom-call | tf_op jit(solution)/shard_map/pair_up/pallas_call | solution.py:489
  36.8 1.5 collective-permute-start.11
  46.3 13.9 %project.1 = (bf16[384,512]{1,0:T(8,128)(2,1)S(1)}, bf16[512,384]{1,0:T(8,128)(2,1)S(1)}, bf16[384,512]{1,0:T(8,128)(2,1)S(1)}) custom-call(s32[5]{0:T(128)S(1)} %copy-done.11, bf16[256,640]{1,0:T(8,128)(2,1)S(1)} %get-tuple-element.53.refs_0_, bf16[256,640]{1,0:T(8,128)(2,1)} %collective-permute-done.8.refs_1_, bf16[256,640]{1,0:T(8,128)(2,1)S(1)} %copy-done.6, ...), custom_call_target="tpu_custom_call" | custom-call | tf_op jit(solution)/shard_map/project/pallas_call | solution.py:141
  60.5 1.2 collective-permute-start.19
  61.9 2.6 %collective-permute-start.25 = (bf16[384,512]{1,0:T(8,128)(2,1)S(1)}, bf16[384,512]{1,0:T(8,128)(2,1)}, u32[]{:S(2)}, u32[]{:S(2)}) collective-permute-start(bf16[384,512]{1,0:T(8,128)(2,1)S(1)} %get-tuple-element.38.refs_6_.refs_8_), channel_id=1, source_target_pairs={{0,24},{1,97},{2,26},{3,99},{4,28},{5,101},{6,30},{7,103},{8,0},{9... | collective-permute-start | bytes 1179656 | tf_op jit(solution)/shard_map/ppermute | solution.py:37
  65.0 2.4 %collective-permute-done.18.refs_1_ = bf16[384,512]{1,0:T(8,128)(2,1)S(1)} collective-permute-done((bf16[384,512]{1,0:T(8,128)(2,1)S(1)}, bf16[384,512]{1,0:T(8,128)(2,1)S(1)}, u32[]{:S(2)}, u32[]{:S(2)}) %collective-permute-start.18) | collective-permute-done | bytes 393248 | tf_op jit(solution)/shard_map/ppermute | solution.py:37
  67.4 1.3 collective-permute-start.24
  68.7 1.4 collective-permute-start.20
  70.2 3.5 %collective-permute-done.21.refs_4_.refs_5_ = bf16[512,384]{1,0:T(8,128)(2,1)} collective-permute-done((bf16[512,384]{1,0:T(8,128)(2,1)S(1)}, bf16[512,384]{1,0:T(8,128)(2,1)}, u32[]{:S(2)}, u32[]{:S(2)}) %collective-permute-start.21) | collective-permute-done | bytes 393248 | tf_op jit(solution)/shard_map/ppermute | solution.py:37
  73.6 3.0 %collective-permute-start.26 = (bf16[384,512]{1,0:T(8,128)(2,1)}, bf16[384,512]{1,0:T(8,128)(2,1)}, u32[]{:S(2)}, u32[]{:S(2)}) collective-permute-start(bf16[384,512]{1,0:T(8,128)(2,1)} %collective-permute-done.25.refs_8_.refs_10_), channel_id=1, source_target_pairs={{0,24},{1,97},{2,26},{3,99},{4,28},{5,101},{6,30},{7,103},{8,0},{9... | collective-permute-start | bytes 1179656 | tf_op jit(solution)/shard_map/ppermute | solution.py:37
  78.8 10.2 %attend_near.1 = (f32[3,384,512]{2,1,0:T(8,128)S(1)}, f32[3,8,512]{2,1,0:T(8,128)S(1)}) custom-call(s32[16]{0:T(128)S(1)} %reshape.39.allowed, s32[4]{0:T(128)S(1)} %get-tuple-element.49.counts, bf16[384,512]{1,0:T(8,128)(2,1)S(1)} %get-tuple-element.36.refs_0_, bf16[384,512]{1,0:T(8,128)(2,1)S(1)} %collective-permute-done.18.refs_1_, ...), custom_call_target="tpu_custom_call" | custom-call | tf_op jit(solution)/shard_map/attend_near/pallas_call | solution.py:285
  89.0 10.3 %attend_far.1 = (bf16[400,512]{1,0:T(8,128)(2,1)S(1)}, bf16[400,512]{1,0:T(8,128)(2,1)S(1)}, bf16[400,512]{1,0:T(8,128)(2,1)S(1)}, bf16[400,512]{1,0:T(8,128)(2,1)S(1)}) custom-call(s32[16]{0:T(128)S(1)} %reshape.39.allowed, s32[4]{0:T(128)S(1)} %get-tuple-element.49.counts, bf16[384,512]{1,0:T(8,128)(2,1)S(1)} %get-tuple-element.36.refs_0_, ...), custom_call_target="tpu_custom_call" | custom-call | tf_op jit(solution)/shard_map/attend_far/pallas_call | solution.py:353
  99.5 2.7 %collective-permute-start.28 = (bf16[400,512]{1,0:T(8,128)(2,1)S(1)}, bf16[400,512]{1,0:T(8,128)(2,1)S(1)}, u32[]{:S(2)}, u32[]{:S(2)}) collective-permute-start(bf16[400,512]{1,0:T(8,128)(2,1)S(1)} %get-tuple-element.43), channel_id=1, source_target_pairs={{0,32},{1,9},{2,34},{3,11},{4,36},{5,13},{6,38},{7,15},{8,40},{9,1... | collective-permute-start | bytes 1228808 | tf_op jit(solution)/shard_map/ppermute | solution.py:37
  102.5 9.7 %collective-permute-done.27.refs_1_ = bf16[400,512]{1,0:T(8,128)(2,1)S(1)} collective-permute-done((bf16[400,512]{1,0:T(8,128)(2,1)S(1)}, bf16[400,512]{1,0:T(8,128)(2,1)S(1)}, u32[]{:S(2)}, u32[]{:S(2)}) %collective-permute-start.27) | collective-permute-done | bytes 409632 | tf_op jit(solution)/shard_map/ppermute | solution.py:37
  112.6 6.5 %collective-permute-start.30 = (bf16[512,384]{1,0:T(8,128)(2,1)S(1)}, bf16[512,384]{1,0:T(8,128)(2,1)S(1)}, u32[]{:S(2)}, u32[]{:S(2)}) collective-permute-start(bf16[512,384]{1,0:T(8,128)(2,1)S(1)} %combine.1.first_ref), channel_id=1, source_target_pairs={{0,1},{1,0},{2,3},{3,2},{4,5},{5,4},{6,7},{7,6},{8,9},{9,8},{10,11... | collective-permute-start | bytes 1179656 | tf_op jit(solution)/shard_map/ppermute | solution.py:37
  119.1 3.0 %collective-permute-start.38 = (bf16[2,384,640]{2,1,0:T(8,128)(2,1)}, bf16[2,384,640]{2,1,0:T(8,128)(2,1)S(1)}, u32[]{:S(2)}, u32[]{:S(2)}) collective-permute-start(bf16[2,384,640]{2,1,0:T(8,128)(2,1)} %get-tuple-element.47), channel_id=1, source_target_pairs={{0,6},{1,7},{2,0},{3,1},{4,2},{5,3},{6,4},{7,5},{8,14},{9,15},{10,... | collective-permute-start | bytes 2949128 | tf_op jit(solution)/shard_map/ppermute | solution.py:37
  122.6 2.1 %collective-permute-start.33 = (bf16[512,384]{1,0:T(8,128)(2,1)S(1)}, bf16[512,384]{1,0:T(8,128)(2,1)}, u32[]{:S(2)}, u32[]{:S(2)}) collective-permute-start(bf16[512,384]{1,0:T(8,128)(2,1)S(1)} %combine.1.first_ref), channel_id=1, source_target_pairs={{0,6},{1,7},{2,0},{3,1},{4,2},{5,3},{6,4},{7,5},{8,14},{9,15},{10,... | collective-permute-start | bytes 1179656 | tf_op jit(solution)/shard_map/ppermute | solution.py:37
  125.5 1.8 collective-permute-start.35
  127.2 27.6 %collective-permute-done.31.refs_0_ = bf16[512,384]{1,0:T(8,128)(2,1)S(1)} collective-permute-done((bf16[512,384]{1,0:T(8,128)(2,1)S(1)}, bf16[512,384]{1,0:T(8,128)(2,1)S(1)}, u32[]{:S(2)}, u32[]{:S(2)}) %collective-permute-start.31) | collective-permute-done | bytes 393248 | tf_op jit(solution)/shard_map/ppermute | solution.py:37
  154.8 1.3 collective-permute-start.32
  156.1 24.9 %collective-permute-done.33.refs_2_ = bf16[512,384]{1,0:T(8,128)(2,1)} collective-permute-done((bf16[512,384]{1,0:T(8,128)(2,1)S(1)}, bf16[512,384]{1,0:T(8,128)(2,1)}, u32[]{:S(2)}, u32[]{:S(2)}) %collective-permute-start.33) | collective-permute-done | bytes 393248 | tf_op jit(solution)/shard_map/ppermute | solution.py:37
  182.2 1.2 copy-done.2
  185.4 5.4 %output_rest.1 = bf16[512,640]{1,0:T(8,128)(2,1)} custom-call(f32[512,640]{1,0:T(8,128)S(1)} %output_own.1.acc_in, bf16[512,384]{1,0:T(8,128)(2,1)S(1)} %collective-permute-done.31.refs_0_, bf16[512,384]{1,0:T(8,128)(2,1)} %collective-permute-done.32.refs_1_, bf16[512,384]{1,0:T(8,128)(2,1)} %collective-permute-done.33.refs_2_, ...), custom_call_target="tpu_custom_call" | custom-call | tf_op jit(solution)/shard_map/output_rest/pallas_call | solution.py:433
  (100 shorter events, 20.8 us)
Async XLA Ops:
  3.5 26.6 %collective-permute-start.4 = (bf16[4,384,640]{2,1,0:T(8,128)(2,1)}, bf16[4,384,640]{2,1,0:T(8,128)(2,1)}, u32[]{:S(2)}, u32[]{:S(2)}) collective-permute-start(bf16[4,384,640]{2,1,0:T(8,128)(2,1)} %take_other.1), channel_id=1, source_target_pairs={{0,1},{1,0},{2,3},{3,2},{4,5},{5,4},{6,7},{7,6},{8,9},{9,8},{10,11... | collective-permute-start | bytes 5898248 | tf_op jit(solution)/shard_map/ppermute | solution.py:37
  4.3 11.9 %collective-permute-start = (bf16[256,640]{1,0:T(8,128)(2,1)S(1)}, bf16[256,640]{1,0:T(8,128)(2,1)S(1)}, u32[]{:S(2)}, u32[]{:S(2)}) collective-permute-start(bf16[256,640]{1,0:T(8,128)(2,1)S(1)} %get-tuple-element.53.refs_0_), channel_id=1, source_target_pairs={{0,2},{1,3},{2,4},{3,5},{4,6},{5,7},{6,0},{7,1},{8,10},{9,11},{10,... | collective-permute-start | bytes 983048 | tf_op jit(solution)/shard_map/ppermute | solution.py:37
  6.0 10.2 %collective-permute-start.2 = (bf16[256,640]{1,0:T(8,128)(2,1)S(1)}, bf16[256,640]{1,0:T(8,128)(2,1)S(1)}, u32[]{:S(2)}, u32[]{:S(2)}) collective-permute-start(bf16[256,640]{1,0:T(8,128)(2,1)S(1)} %get-tuple-element.52.refs_8_), channel_id=1, source_target_pairs={{0,6},{1,7},{2,0},{3,1},{4,2},{5,3},{6,4},{7,5},{8,14},{9,15},{10,... | collective-permute-start | bytes 983048 | tf_op jit(solution)/shard_map/ppermute | solution.py:37
  16.2 9.9 %collective-permute-start.1 = (bf16[256,640]{1,0:T(8,128)(2,1)S(1)}, bf16[256,640]{1,0:T(8,128)(2,1)S(1)}, u32[]{:S(2)}, u32[]{:S(2)}) collective-permute-start(bf16[256,640]{1,0:T(8,128)(2,1)S(1)} %collective-permute-done.refs_2_), channel_id=1, source_target_pairs={{0,2},{1,3},{2,4},{3,5},{4,6},{5,7},{6,0},{7,1},{8,10},{9,11},{10,... | collective-permute-start | bytes 983048 | tf_op jit(solution)/shard_map/ppermute | solution.py:37
  16.2 13.8 %collective-permute-start.3 = (bf16[256,640]{1,0:T(8,128)(2,1)S(1)}, bf16[256,640]{1,0:T(8,128)(2,1)}, u32[]{:S(2)}, u32[]{:S(2)}) collective-permute-start(bf16[256,640]{1,0:T(8,128)(2,1)S(1)} %collective-permute-done.2.refs_12_), channel_id=1, source_target_pairs={{0,6},{1,7},{2,0},{3,1},{4,2},{5,3},{6,4},{7,5},{8,14},{9,15},{10,... | collective-permute-start | bytes 983048 | tf_op jit(solution)/shard_map/ppermute | solution.py:37
  19.1 3.9 %collective-permute-start.6 = (s32[1,16]{1,0:T(1,128)S(1)}, s32[1,16]{1,0:T(1,128)S(1)}, u32[]{:S(2)}, u32[]{:S(2)}) collective-permute-start(s32[1,16]{1,0:T(1,128)S(1)} %copy-done.14), channel_id=1, source_target_pairs={{0,96},{1,25},{2,98},{3,27},{4,100},{5,29},{6,102},{7,31},{8,104},... | collective-permute-start | bytes 200 | tf_op jit(solution)/shard_map/ppermute | solution.py:37
  23.0 13.6 %collective-permute-start.10 = (bf16[256,640]{1,0:T(8,128)(2,1)S(1)}, bf16[256,640]{1,0:T(8,128)(2,1)}, u32[]{:S(2)}, u32[]{:S(2)}) collective-permute-start(bf16[256,640]{1,0:T(8,128)(2,1)S(1)} %get-tuple-element.53.refs_0_), channel_id=1, source_target_pairs={{0,6},{1,7},{2,0},{3,1},{4,2},{5,3},{6,4},{7,5},{8,14},{9,15},{10,... | collective-permute-start | bytes 983048 | tf_op jit(solution)/shard_map/ppermute | solution.py:37
  25.6 11.1 %collective-permute-start.14 = (bf16[256,640]{1,0:T(8,128)(2,1)S(1)}, bf16[256,640]{1,0:T(8,128)(2,1)}, u32[]{:S(2)}, u32[]{:S(2)}) collective-permute-start(bf16[256,640]{1,0:T(8,128)(2,1)S(1)} %get-tuple-element.52.refs_8_), channel_id=1, source_target_pairs={{0,2},{1,3},{2,4},{3,5},{4,6},{5,7},{6,0},{7,1},{8,10},{9,11},{10,... | collective-permute-start | bytes 983048 | tf_op jit(solution)/shard_map/ppermute | solution.py:37
  26.1 12.2 %collective-permute-start.13 = (bf16[256,640]{1,0:T(8,128)(2,1)S(1)}, bf16[256,640]{1,0:T(8,128)(2,1)}, u32[]{:S(2)}, u32[]{:S(2)}) collective-permute-start(bf16[256,640]{1,0:T(8,128)(2,1)S(1)} %get-tuple-element.52.refs_8_), channel_id=1, source_target_pairs={{0,1},{1,0},{2,3},{3,2},{4,5},{5,4},{6,7},{7,6},{8,9},{9,8},{10,11... | collective-permute-start | bytes 983048 | tf_op jit(solution)/shard_map/ppermute | solution.py:37
  30.0 8.3 %collective-permute-start.8 = (bf16[256,640]{1,0:T(8,128)(2,1)S(1)}, bf16[256,640]{1,0:T(8,128)(2,1)}, u32[]{:S(2)}, u32[]{:S(2)}) collective-permute-start(bf16[256,640]{1,0:T(8,128)(2,1)S(1)} %get-tuple-element.53.refs_0_), channel_id=1, source_target_pairs={{0,1},{1,0},{2,3},{3,2},{4,5},{5,4},{6,7},{7,6},{8,9},{9,8},{10,11... | collective-permute-start | bytes 983048 | tf_op jit(solution)/shard_map/ppermute | solution.py:37
  30.1 8.7 %collective-permute-start.16 = (bf16[256,640]{1,0:T(8,128)(2,1)S(1)}, bf16[256,640]{1,0:T(8,128)(2,1)}, u32[]{:S(2)}, u32[]{:S(2)}) collective-permute-start(bf16[256,640]{1,0:T(8,128)(2,1)S(1)} %collective-permute-done.2.refs_12_), channel_id=1, source_target_pairs={{0,1},{1,0},{2,3},{3,2},{4,5},{5,4},{6,7},{7,6},{8,9},{9,8},{10,11... | collective-permute-start | bytes 983048 | tf_op jit(solution)/shard_map/ppermute | solution.py:37
  60.2 7.2 %collective-permute-start.18 = (bf16[384,512]{1,0:T(8,128)(2,1)S(1)}, bf16[384,512]{1,0:T(8,128)(2,1)S(1)}, u32[]{:S(2)}, u32[]{:S(2)}) collective-permute-start(bf16[384,512]{1,0:T(8,128)(2,1)S(1)} %get-tuple-element.36.refs_0_), channel_id=1, source_target_pairs={{0,32},{1,9},{2,34},{3,11},{4,36},{5,13},{6,38},{7,15},{8,40},{9,1... | collective-permute-start | bytes 1179656 | tf_op jit(solution)/shard_map/ppermute | solution.py:37
  60.5 8.2 %collective-permute-start.19 = (bf16[384,512]{1,0:T(8,128)(2,1)S(1)}, bf16[384,512]{1,0:T(8,128)(2,1)}, u32[]{:S(2)}, u32[]{:S(2)}) collective-permute-start(bf16[384,512]{1,0:T(8,128)(2,1)S(1)} %get-tuple-element.36.refs_0_), channel_id=1, source_target_pairs={{0,96},{1,25},{2,98},{3,27},{4,100},{5,29},{6,102},{7,31},{8,104},... | collective-permute-start | bytes 1179656 | tf_op jit(solution)/shard_map/ppermute | solution.py:37
  61.7 11.9 %collective-permute-start.21 = (bf16[512,384]{1,0:T(8,128)(2,1)S(1)}, bf16[512,384]{1,0:T(8,128)(2,1)}, u32[]{:S(2)}, u32[]{:S(2)}) collective-permute-start(bf16[512,384]{1,0:T(8,128)(2,1)S(1)} %get-tuple-element.37.refs_3_.refs_4_), channel_id=1, source_target_pairs={{0,8},{1,33},{2,10},{3,35},{4,12},{5,37},{6,14},{7,39},{8,16},{9,4... | collective-permute-start | bytes 1179656 | tf_op jit(solution)/shard_map/ppermute | solution.py:37
  61.9 11.8 %collective-permute-start.25 = (bf16[384,512]{1,0:T(8,128)(2,1)S(1)}, bf16[384,512]{1,0:T(8,128)(2,1)}, u32[]{:S(2)}, u32[]{:S(2)}) collective-permute-start(bf16[384,512]{1,0:T(8,128)(2,1)S(1)} %get-tuple-element.38.refs_6_.refs_8_), channel_id=1, source_target_pairs={{0,24},{1,97},{2,26},{3,99},{4,28},{5,101},{6,30},{7,103},{8,0},{9... | collective-permute-start | bytes 1179656 | tf_op jit(solution)/shard_map/ppermute | solution.py:37
  64.5 13.8 %collective-permute-start.22 = (bf16[512,384]{1,0:T(8,128)(2,1)S(1)}, bf16[512,384]{1,0:T(8,128)(2,1)}, u32[]{:S(2)}, u32[]{:S(2)}) collective-permute-start(bf16[512,384]{1,0:T(8,128)(2,1)S(1)} %get-tuple-element.37.refs_3_.refs_4_), channel_id=1, source_target_pairs={{0,24},{1,97},{2,26},{3,99},{4,28},{5,101},{6,30},{7,103},{8,0},{9... | collective-permute-start | bytes 1179656 | tf_op jit(solution)/shard_map/ppermute | solution.py:37
  67.4 11.3 %collective-permute-start.24 = (bf16[384,512]{1,0:T(8,128)(2,1)S(1)}, bf16[384,512]{1,0:T(8,128)(2,1)}, u32[]{:S(2)}, u32[]{:S(2)}) collective-permute-start(bf16[384,512]{1,0:T(8,128)(2,1)S(1)} %get-tuple-element.38.refs_6_.refs_8_), channel_id=1, source_target_pairs={{0,8},{1,33},{2,10},{3,35},{4,12},{5,37},{6,14},{7,39},{8,16},{9,4... | collective-permute-start | bytes 1179656 | tf_op jit(solution)/shard_map/ppermute | solution.py:37
  68.7 20.2 %collective-permute-start.20 = (bf16[384,512]{1,0:T(8,128)(2,1)S(1)}, bf16[384,512]{1,0:T(8,128)(2,1)}, u32[]{:S(2)}, u32[]{:S(2)}) collective-permute-start(bf16[384,512]{1,0:T(8,128)(2,1)S(1)} %get-tuple-element.36.refs_0_), channel_id=1, source_target_pairs={{0,64},{1,17},{2,66},{3,19},{4,68},{5,21},{6,70},{7,23},{8,72},{9,... | collective-permute-start | bytes 1179656 | tf_op jit(solution)/shard_map/ppermute | solution.py:37
  73.6 15.4 %collective-permute-start.23 = (bf16[512,384]{1,0:T(8,128)(2,1)}, bf16[512,384]{1,0:T(8,128)(2,1)}, u32[]{:S(2)}, u32[]{:S(2)}) collective-permute-start(bf16[512,384]{1,0:T(8,128)(2,1)} %collective-permute-done.21.refs_4_.refs_5_), channel_id=1, source_target_pairs={{0,8},{1,33},{2,10},{3,35},{4,12},{5,37},{6,14},{7,39},{8,16},{9,4... | collective-permute-start | bytes 1179656 | tf_op jit(solution)/shard_map/ppermute | solution.py:37
  73.6 15.4 %collective-permute-start.26 = (bf16[384,512]{1,0:T(8,128)(2,1)}, bf16[384,512]{1,0:T(8,128)(2,1)}, u32[]{:S(2)}, u32[]{:S(2)}) collective-permute-start(bf16[384,512]{1,0:T(8,128)(2,1)} %collective-permute-done.25.refs_8_.refs_10_), channel_id=1, source_target_pairs={{0,24},{1,97},{2,26},{3,99},{4,28},{5,101},{6,30},{7,103},{8,0},{9... | collective-permute-start | bytes 1179656 | tf_op jit(solution)/shard_map/ppermute | solution.py:37
  78.3 44.3 %collective-permute-start.37 = (bf16[2,384,640]{2,1,0:T(8,128)(2,1)}, bf16[2,384,640]{2,1,0:T(8,128)(2,1)}, u32[]{:S(2)}, u32[]{:S(2)}) collective-permute-start(bf16[2,384,640]{2,1,0:T(8,128)(2,1)} %get-tuple-element.46), channel_id=1, source_target_pairs={{0,2},{1,3},{2,4},{3,5},{4,6},{5,7},{6,0},{7,1},{8,10},{9,11},{10,... | collective-permute-start | bytes 2949128 | tf_op jit(solution)/shard_map/ppermute | solution.py:37
  99.4 12.8 %collective-permute-start.27 = (bf16[400,512]{1,0:T(8,128)(2,1)S(1)}, bf16[400,512]{1,0:T(8,128)(2,1)S(1)}, u32[]{:S(2)}, u32[]{:S(2)}) collective-permute-start(bf16[400,512]{1,0:T(8,128)(2,1)S(1)} %get-tuple-element.42), channel_id=1, source_target_pairs={{0,96},{1,25},{2,98},{3,27},{4,100},{5,29},{6,102},{7,31},{8,104},... | collective-permute-start | bytes 1228808 | tf_op jit(solution)/shard_map/ppermute | solution.py:37
  99.5 12.7 %collective-permute-start.28 = (bf16[400,512]{1,0:T(8,128)(2,1)S(1)}, bf16[400,512]{1,0:T(8,128)(2,1)S(1)}, u32[]{:S(2)}, u32[]{:S(2)}) collective-permute-start(bf16[400,512]{1,0:T(8,128)(2,1)S(1)} %get-tuple-element.43), channel_id=1, source_target_pairs={{0,32},{1,9},{2,34},{3,11},{4,36},{5,13},{6,38},{7,15},{8,40},{9,1... | collective-permute-start | bytes 1228808 | tf_op jit(solution)/shard_map/ppermute | solution.py:37
  102.1 10.0 %collective-permute-start.29 = (bf16[400,512]{1,0:T(8,128)(2,1)S(1)}, bf16[400,512]{1,0:T(8,128)(2,1)S(1)}, u32[]{:S(2)}, u32[]{:S(2)}) collective-permute-start(bf16[400,512]{1,0:T(8,128)(2,1)S(1)} %get-tuple-element.44), channel_id=1, source_target_pairs={{0,64},{1,17},{2,66},{3,19},{4,68},{5,21},{6,70},{7,23},{8,72},{9,... | collective-permute-start | bytes 1228808 | tf_op jit(solution)/shard_map/ppermute | solution.py:37
  112.6 12.1 %collective-permute-start.30 = (bf16[512,384]{1,0:T(8,128)(2,1)S(1)}, bf16[512,384]{1,0:T(8,128)(2,1)S(1)}, u32[]{:S(2)}, u32[]{:S(2)}) collective-permute-start(bf16[512,384]{1,0:T(8,128)(2,1)S(1)} %combine.1.first_ref), channel_id=1, source_target_pairs={{0,1},{1,0},{2,3},{3,2},{4,5},{5,4},{6,7},{7,6},{8,9},{9,8},{10,11... | collective-permute-start | bytes 1179656 | tf_op jit(solution)/shard_map/ppermute | solution.py:37
  119.1 66.3 %collective-permute-start.38 = (bf16[2,384,640]{2,1,0:T(8,128)(2,1)}, bf16[2,384,640]{2,1,0:T(8,128)(2,1)S(1)}, u32[]{:S(2)}, u32[]{:S(2)}) collective-permute-start(bf16[2,384,640]{2,1,0:T(8,128)(2,1)} %get-tuple-element.47), channel_id=1, source_target_pairs={{0,6},{1,7},{2,0},{3,1},{4,2},{5,3},{6,4},{7,5},{8,14},{9,15},{10,... | collective-permute-start | bytes 2949128 | tf_op jit(solution)/shard_map/ppermute | solution.py:37
  122.0 63.3 %collective-permute-start.39 = (bf16[2,384,640]{2,1,0:T(8,128)(2,1)}, bf16[2,384,640]{2,1,0:T(8,128)(2,1)}, u32[]{:S(2)}, u32[]{:S(2)}) collective-permute-start(bf16[2,384,640]{2,1,0:T(8,128)(2,1)} %get-tuple-element.48), channel_id=1, source_target_pairs={{0,4},{1,5},{2,6},{3,7},{4,0},{5,1},{6,2},{7,3},{8,12},{9,13},{10,... | collective-permute-start | bytes 2949128 | tf_op jit(solution)/shard_map/ppermute | solution.py:37
  122.0 32.8 %collective-permute-start.31 = (bf16[512,384]{1,0:T(8,128)(2,1)S(1)}, bf16[512,384]{1,0:T(8,128)(2,1)S(1)}, u32[]{:S(2)}, u32[]{:S(2)}) collective-permute-start(bf16[512,384]{1,0:T(8,128)(2,1)S(1)} %combine.1.first_ref), channel_id=1, source_target_pairs={{0,2},{1,3},{2,4},{3,5},{4,6},{5,7},{6,0},{7,1},{8,10},{9,11},{10,... | collective-permute-start | bytes 1179656 | tf_op jit(solution)/shard_map/ppermute | solution.py:37
  122.6 58.4 %collective-permute-start.33 = (bf16[512,384]{1,0:T(8,128)(2,1)S(1)}, bf16[512,384]{1,0:T(8,128)(2,1)}, u32[]{:S(2)}, u32[]{:S(2)}) collective-permute-start(bf16[512,384]{1,0:T(8,128)(2,1)S(1)} %combine.1.first_ref), channel_id=1, source_target_pairs={{0,6},{1,7},{2,0},{3,1},{4,2},{5,3},{6,4},{7,5},{8,14},{9,15},{10,... | collective-permute-start | bytes 1179656 | tf_op jit(solution)/shard_map/ppermute | solution.py:37
  125.5 56.7 %collective-permute-start.35 = (bf16[512,384]{1,0:T(8,128)(2,1)S(1)}, bf16[512,384]{1,0:T(8,128)(2,1)}, u32[]{:S(2)}, u32[]{:S(2)}) collective-permute-start(bf16[512,384]{1,0:T(8,128)(2,1)S(1)} %combine.1.first_ref), channel_id=1, source_target_pairs={{0,4},{1,5},{2,6},{3,7},{4,0},{5,1},{6,2},{7,3},{8,12},{9,13},{10,... | collective-permute-start | bytes 1179656 | tf_op jit(solution)/shard_map/ppermute | solution.py:37
  154.8 30.5 %collective-permute-start.32 = (bf16[512,384]{1,0:T(8,128)(2,1)S(1)}, bf16[512,384]{1,0:T(8,128)(2,1)}, u32[]{:S(2)}, u32[]{:S(2)}) collective-permute-start(bf16[512,384]{1,0:T(8,128)(2,1)S(1)} %collective-permute-done.31.refs_0_), channel_id=1, source_target_pairs={{0,1},{1,0},{2,3},{3,2},{4,5},{5,4},{6,7},{7,6},{8,9},{9,8},{10,11... | collective-permute-start | bytes 1179656 | tf_op jit(solution)/shard_map/ppermute | solution.py:37
  181.1 4.3 %collective-permute-start.34 = (bf16[512,384]{1,0:T(8,128)(2,1)}, bf16[512,384]{1,0:T(8,128)(2,1)}, u32[]{:S(2)}, u32[]{:S(2)}) collective-permute-start(bf16[512,384]{1,0:T(8,128)(2,1)} %collective-permute-done.33.refs_2_), channel_id=1, source_target_pairs={{0,1},{1,0},{2,3},{3,2},{4,5},{5,4},{6,7},{7,6},{8,9},{9,8},{10,11... | collective-permute-start | bytes 1179656 | tf_op jit(solution)/shard_map/ppermute | solution.py:37
  (23 other events, 148.3 us)

commit v3 on v2

--- a/solution.py
+++ b/solution.py
@@ -393,27 +393,23 @@
     )(*[in_vmem(part) for part in parts])
 
 
-def head_terms(attended, weights):
-    for n, value in enumerate(attended):
-        term = jnp.dot(value[...], weights[n // 2][n % 2], preferred_element_type=jnp.float32)
-        yield term.astype(jnp.bfloat16).astype(jnp.float32)
+def group_terms(first, second, weight):
+    both = jnp.concatenate([first[...], second[...]], axis=1)
+    depth, wide = 2 * weight.shape[1], weight.shape[2]
+    return jnp.dot(both, weight[...].reshape(depth, wide), preferred_element_type=jnp.float32)
 
 
 def output_own_kernel(first_ref, second_ref, weight_ref, acc_ref):
-    first, second = head_terms((first_ref, second_ref), (weight_ref,))
-    acc_ref[...] = first + second
+    acc_ref[...] = group_terms(first_ref, second_ref, weight_ref)
 
 
 def output_rest_kernel(acc_in, *refs):
-    attended, weights, latents_ref, gate_ref, out_ref, acc_ref = refs[:6], refs[6:9], *refs[9:]
-    acc_ref[...] = acc_in[...]
-    for n, term in enumerate(head_terms(attended, weights)):
-        if n < 5:
-            acc_ref[...] += term
-        else:
-            projected = acc_ref[...] + term
-            updated = latents_ref[...].astype(jnp.float32) + gate_ref[...] * projected
-            out_ref[...] = updated.astype(jnp.bfloat16)
+    attended, weights, latents_ref, gate_ref, out_ref = refs[:6], refs[6:9], *refs[9:]
+    projected = acc_in[...]
+    for n in range(3):
+        projected = projected + group_terms(attended[2 * n], attended[2 * n + 1], weights[n])
+    updated = latents_ref[...].astype(jnp.float32) + gate_ref[...] * projected
+    out_ref[...] = updated.astype(jnp.bfloat16)
 
 
 def output_own(attended, weight):
@@ -435,7 +431,6 @@
         in_specs=[vmem] * 12,
         out_specs=vmem,
         out_shape=jax.ShapeDtypeStruct(latents.shape, jnp.bfloat16),
-        scratch_shapes=[pltpu.VMEM(latents.shape, jnp.float32)],
         compiler_params=pltpu.CompilerParams(vmem_limit_bytes=12 * 2**20),
         name="output_rest",
     )(*[in_vmem(v) for v in (acc, *attended, *weights, latents, gate)])
@@ -575,7 +570,8 @@
         pieces, columns, modulation, (query_gain, key_gain), (w_query, w_key, w_value)
     )
 
-    key_low, key_high = permute(key_own, along_keys(1)), permute(key_own, along_keys(-1))
+    key_low = permute(key_own, along_keys(1))
+    key_high = permute(key_own, along_keys(-1))
     value_low, value_high = permute(value_own, along_keys(1)), permute(value_own, along_keys(-1))
     query_low, query_high = permute(query_own, along_queries(1)), permute(query_own, along_queries(-1))
     w_blocks = (w_pairs[0], w_below, w_above, w_far)

time: 191 us -> 191 us (level)
  no operation moved by 1% of the time
where the time goes in v3:
time: 191 us; the launch traced here: 190 us
  waiting for transfers between devices  82.3 us (43%)
  Pallas kernels  48.7 us (25%)
  starting transfers between devices  46.7 us (24%)
  local copies, waits for them, and re-layouts  8.94 us (5%)
  other arithmetic  2.61 us (1%)
    ppermute x40, waiting for transfers between devices, permute(): return lax.ppermute(value, AXES, pairs)  82.3 us
    ppermute x40, starting transfers between devices, permute(): return lax.ppermute(value, AXES, pairs)  46.7 us
    pallas_call x1, Pallas kernels, project(): pl.pallas_call(project_kernel, in_specs=[pl.BlockSpec(memory_space=pltpu....  13.9 us
    pallas_call x1, Pallas kernels, attend_far(): pl.pallas_call(far_kernel, in_specs=[pl.BlockSpec(memory_space=pltpu.SMEM...  10.3 us
    pallas_call x1, Pallas kernels, attend_near(): pl.pallas_call(near_kernel, in_specs=[pl.BlockSpec(memory_space=pltpu.SME...  10.2 us
    unnamed x31, local copies, waits for them, and re-layouts  7.93 us
    pallas_call x1, Pallas kernels, output_rest(): pl.pallas_call(output_rest_kernel, in_specs=[vmem] * 12, out_specs=vmem,...  4.94 us
    pallas_call x1, Pallas kernels, pair_up(): pl.pallas_call(pair_kernel, in_specs=[pl.BlockSpec(memory_space=pltpu.SME...  4.7 us
  transfers between devices with their start and end apart: 40, of which 14 were waited for; matrix products, arithmetic and copies ran while one was open for 2% of the time, Pallas kernels for 14%

profile of v3, /device:TPU:7, one launch (start us, length us, event | category | flops | bytes accessed | tf_op | source)
XLA Modules:
  0.0 190.2 jit_solution(638603174464067124)
XLA Ops:
  0.2 3.3 %take_other.1 = bf16[4,384,640]{2,1,0:T(8,128)(2,1)} custom-call(s32[8]{0:T(128)S(1)} %stack.99.places, bf16[384,5120]{1,0:T(8,128)(2,1)} %w_ref.3), custom_call_target="tpu_custom_call" | custom-call | tf_op jit(solution)/shard_map/take_other/pallas_call | solution.py:452
  4.3 1.7 collective-permute-start
  6.0 2.2 %collective-permute-start.2 = (bf16[256,640]{1,0:T(8,128)(2,1)S(1)}, bf16[256,640]{1,0:T(8,128)(2,1)S(1)}, u32[]{:S(2)}, u32[]{:S(2)}) collective-permute-start(bf16[256,640]{1,0:T(8,128)(2,1)S(1)} %get-tuple-element.52.refs_8_), channel_id=1, source_target_pairs={{0,6},{1,7},{2,0},{3,1},{4,2},{5,3},{6,4},{7,5},{8,14},{9,15},{10,... | collective-permute-start | bytes 983048 | tf_op jit(solution)/shard_map/ppermute | solution.py:37
  8.2 8.0 %collective-permute-done.refs_2_ = bf16[256,640]{1,0:T(8,128)(2,1)S(1)} collective-permute-done((bf16[256,640]{1,0:T(8,128)(2,1)S(1)}, bf16[256,640]{1,0:T(8,128)(2,1)S(1)}, u32[]{:S(2)}, u32[]{:S(2)}) %collective-permute-start) | collective-permute-done | bytes 327712 | tf_op jit(solution)/shard_map/ppermute | solution.py:37
  16.2 2.7 %collective-permute-start.3 = (bf16[256,640]{1,0:T(8,128)(2,1)S(1)}, bf16[256,640]{1,0:T(8,128)(2,1)}, u32[]{:S(2)}, u32[]{:S(2)}) collective-permute-start(bf16[256,640]{1,0:T(8,128)(2,1)S(1)} %collective-permute-done.2.refs_12_), channel_id=1, source_target_pairs={{0,6},{1,7},{2,0},{3,1},{4,2},{5,3},{6,4},{7,5},{8,14},{9,15},{10,... | collective-permute-start | bytes 983048 | tf_op jit(solution)/shard_map/ppermute | solution.py:37
  19.1 1.3 collective-permute-start.6
  21.7 1.1 collective-permute-start.7
  23.0 2.6 %collective-permute-done.7 = s32[1,16]{1,0:T(1,128)S(1)} collective-permute-done((s32[1,16]{1,0:T(1,128)S(1)}, s32[1,16]{1,0:T(1,128)S(1)}, u32[]{:S(2)}, u32[]{:S(2)}) %collective-permute-start.7) | collective-permute-done | bytes 96 | tf_op jit(solution)/shard_map/ppermute | solution.py:37
  26.1 3.9 %collective-permute-start.13 = (bf16[256,640]{1,0:T(8,128)(2,1)S(1)}, bf16[256,640]{1,0:T(8,128)(2,1)}, u32[]{:S(2)}, u32[]{:S(2)}) collective-permute-start(bf16[256,640]{1,0:T(8,128)(2,1)S(1)} %get-tuple-element.52.refs_8_), channel_id=1, source_target_pairs={{0,1},{1,0},{2,3},{3,2},{4,5},{5,4},{6,7},{7,6},{8,9},{9,8},{10,11... | collective-permute-start | bytes 983048 | tf_op jit(solution)/shard_map/ppermute | solution.py:37
  31.9 4.7 %pair_up.1 = (bf16[2,384,640]{2,1,0:T(8,128)(2,1)}, bf16[2,384,640]{2,1,0:T(8,128)(2,1)}, bf16[2,384,640]{2,1,0:T(8,128)(2,1)}, bf16[2,384,640]{2,1,0:T(8,128)(2,1)}) custom-call(s32[8]{0:T(128)S(1)} %stack.99.places, bf16[384,5120]{1,0:T(8,128)(2,1)} %w_ref.3, bf16[4,384,640]{2,1,0:T(8,128)(2,1)} %collective-permute-done.4.other_ref), custom_call_target="tpu_custom_call" | custom-call | tf_op jit(solution)/shard_map/pair_up/pallas_call | solution.py:484
  36.8 1.5 collective-permute-start.11
  46.3 13.9 %project.1 = (bf16[384,512]{1,0:T(8,128)(2,1)S(1)}, bf16[512,384]{1,0:T(8,128)(2,1)S(1)}, bf16[384,512]{1,0:T(8,128)(2,1)S(1)}) custom-call(s32[5]{0:T(128)S(1)} %copy-done.11, bf16[256,640]{1,0:T(8,128)(2,1)S(1)} %get-tuple-element.53.refs_0_, bf16[256,640]{1,0:T(8,128)(2,1)} %collective-permute-done.8.refs_1_, bf16[256,640]{1,0:T(8,128)(2,1)S(1)} %copy-done.6, ...), custom_call_target="tpu_custom_call" | custom-call | tf_op jit(solution)/shard_map/project/pallas_call | solution.py:141
  60.5 1.2 collective-permute-start.19
  61.9 2.6 %collective-permute-start.25 = (bf16[384,512]{1,0:T(8,128)(2,1)S(1)}, bf16[384,512]{1,0:T(8,128)(2,1)}, u32[]{:S(2)}, u32[]{:S(2)}) collective-permute-start(bf16[384,512]{1,0:T(8,128)(2,1)S(1)} %get-tuple-element.38.refs_6_.refs_8_), channel_id=1, source_target_pairs={{0,24},{1,97},{2,26},{3,99},{4,28},{5,101},{6,30},{7,103},{8,0},{9... | collective-permute-start | bytes 1179656 | tf_op jit(solution)/shard_map/ppermute | solution.py:37
  65.0 2.4 %collective-permute-done.18.refs_1_ = bf16[384,512]{1,0:T(8,128)(2,1)S(1)} collective-permute-done((bf16[384,512]{1,0:T(8,128)(2,1)S(1)}, bf16[384,512]{1,0:T(8,128)(2,1)S(1)}, u32[]{:S(2)}, u32[]{:S(2)}) %collective-permute-start.18) | collective-permute-done | bytes 393248 | tf_op jit(solution)/shard_map/ppermute | solution.py:37
  67.4 1.3 collective-permute-start.24
  68.7 1.4 collective-permute-start.20
  70.2 3.5 %collective-permute-done.21.refs_4_.refs_5_ = bf16[512,384]{1,0:T(8,128)(2,1)} collective-permute-done((bf16[512,384]{1,0:T(8,128)(2,1)S(1)}, bf16[512,384]{1,0:T(8,128)(2,1)}, u32[]{:S(2)}, u32[]{:S(2)}) %collective-permute-start.21) | collective-permute-done | bytes 393248 | tf_op jit(solution)/shard_map/ppermute | solution.py:37
  73.6 3.0 %collective-permute-start.26 = (bf16[384,512]{1,0:T(8,128)(2,1)}, bf16[384,512]{1,0:T(8,128)(2,1)}, u32[]{:S(2)}, u32[]{:S(2)}) collective-permute-start(bf16[384,512]{1,0:T(8,128)(2,1)} %collective-permute-done.25.refs_8_.refs_10_), channel_id=1, source_target_pairs={{0,24},{1,97},{2,26},{3,99},{4,28},{5,101},{6,30},{7,103},{8,0},{9... | collective-permute-start | bytes 1179656 | tf_op jit(solution)/shard_map/ppermute | solution.py:37
  78.8 10.2 %attend_near.1 = (f32[3,384,512]{2,1,0:T(8,128)S(1)}, f32[3,8,512]{2,1,0:T(8,128)S(1)}) custom-call(s32[16]{0:T(128)S(1)} %reshape.39.allowed, s32[4]{0:T(128)S(1)} %get-tuple-element.49.counts, bf16[384,512]{1,0:T(8,128)(2,1)S(1)} %get-tuple-element.36.refs_0_, bf16[384,512]{1,0:T(8,128)(2,1)S(1)} %collective-permute-done.18.refs_1_, ...), custom_call_target="tpu_custom_call" | custom-call | tf_op jit(solution)/shard_map/attend_near/pallas_call | solution.py:285
  89.0 10.3 %attend_far.1 = (bf16[400,512]{1,0:T(8,128)(2,1)S(1)}, bf16[400,512]{1,0:T(8,128)(2,1)S(1)}, bf16[400,512]{1,0:T(8,128)(2,1)S(1)}, bf16[400,512]{1,0:T(8,128)(2,1)S(1)}) custom-call(s32[16]{0:T(128)S(1)} %reshape.39.allowed, s32[4]{0:T(128)S(1)} %get-tuple-element.49.counts, bf16[384,512]{1,0:T(8,128)(2,1)S(1)} %get-tuple-element.36.refs_0_, ...), custom_call_target="tpu_custom_call" | custom-call | tf_op jit(solution)/shard_map/attend_far/pallas_call | solution.py:353
  99.5 2.7 %collective-permute-start.28 = (bf16[400,512]{1,0:T(8,128)(2,1)S(1)}, bf16[400,512]{1,0:T(8,128)(2,1)S(1)}, u32[]{:S(2)}, u32[]{:S(2)}) collective-permute-start(bf16[400,512]{1,0:T(8,128)(2,1)S(1)} %get-tuple-element.43), channel_id=1, source_target_pairs={{0,32},{1,9},{2,34},{3,11},{4,36},{5,13},{6,38},{7,15},{8,40},{9,1... | collective-permute-start | bytes 1228808 | tf_op jit(solution)/shard_map/ppermute | solution.py:37
  102.5 9.7 %collective-permute-done.27.refs_1_ = bf16[400,512]{1,0:T(8,128)(2,1)S(1)} collective-permute-done((bf16[400,512]{1,0:T(8,128)(2,1)S(1)}, bf16[400,512]{1,0:T(8,128)(2,1)S(1)}, u32[]{:S(2)}, u32[]{:S(2)}) %collective-permute-start.27) | collective-permute-done | bytes 409632 | tf_op jit(solution)/shard_map/ppermute | solution.py:37
  112.6 6.5 %collective-permute-start.30 = (bf16[512,384]{1,0:T(8,128)(2,1)S(1)}, bf16[512,384]{1,0:T(8,128)(2,1)S(1)}, u32[]{:S(2)}, u32[]{:S(2)}) collective-permute-start(bf16[512,384]{1,0:T(8,128)(2,1)S(1)} %combine.1.first_ref), channel_id=1, source_target_pairs={{0,1},{1,0},{2,3},{3,2},{4,5},{5,4},{6,7},{7,6},{8,9},{9,8},{10,11... | collective-permute-start | bytes 1179656 | tf_op jit(solution)/shard_map/ppermute | solution.py:37
  119.1 3.0 %collective-permute-start.38 = (bf16[2,384,640]{2,1,0:T(8,128)(2,1)}, bf16[2,384,640]{2,1,0:T(8,128)(2,1)S(1)}, u32[]{:S(2)}, u32[]{:S(2)}) collective-permute-start(bf16[2,384,640]{2,1,0:T(8,128)(2,1)} %get-tuple-element.47), channel_id=1, source_target_pairs={{0,6},{1,7},{2,0},{3,1},{4,2},{5,3},{6,4},{7,5},{8,14},{9,15},{10,... | collective-permute-start | bytes 2949128 | tf_op jit(solution)/shard_map/ppermute | solution.py:37
  122.6 2.1 %collective-permute-start.33 = (bf16[512,384]{1,0:T(8,128)(2,1)S(1)}, bf16[512,384]{1,0:T(8,128)(2,1)}, u32[]{:S(2)}, u32[]{:S(2)}) collective-permute-start(bf16[512,384]{1,0:T(8,128)(2,1)S(1)} %combine.1.first_ref), channel_id=1, source_target_pairs={{0,6},{1,7},{2,0},{3,1},{4,2},{5,3},{6,4},{7,5},{8,14},{9,15},{10,... | collective-permute-start | bytes 1179656 | tf_op jit(solution)/shard_map/ppermute | solution.py:37
  125.5 1.8 collective-permute-start.35
  127.2 27.6 %collective-permute-done.31.refs_0_ = bf16[512,384]{1,0:T(8,128)(2,1)S(1)} collective-permute-done((bf16[512,384]{1,0:T(8,128)(2,1)S(1)}, bf16[512,384]{1,0:T(8,128)(2,1)S(1)}, u32[]{:S(2)}, u32[]{:S(2)}) %collective-permute-start.31) | collective-permute-done | bytes 393248 | tf_op jit(solution)/shard_map/ppermute | solution.py:37
  154.8 1.3 collective-permute-start.32
  156.1 24.9 %collective-permute-done.33.refs_2_ = bf16[512,384]{1,0:T(8,128)(2,1)} collective-permute-done((bf16[512,384]{1,0:T(8,128)(2,1)S(1)}, bf16[512,384]{1,0:T(8,128)(2,1)}, u32[]{:S(2)}, u32[]{:S(2)}) %collective-permute-start.33) | collective-permute-done | bytes 393248 | tf_op jit(solution)/shard_map/ppermute | solution.py:37
  182.2 1.2 copy-done.2
  185.3 4.9 %output_rest.1 = bf16[512,640]{1,0:T(8,128)(2,1)} custom-call(f32[512,640]{1,0:T(8,128)S(1)} %output_own.1.acc_in, bf16[512,384]{1,0:T(8,128)(2,1)S(1)} %collective-permute-done.31.refs_0_, bf16[512,384]{1,0:T(8,128)(2,1)} %collective-permute-done.32.refs_1_, bf16[512,384]{1,0:T(8,128)(2,1)} %collective-permute-done.33.refs_2_, ...), custom_call_target="tpu_custom_call" | custom-call | tf_op jit(solution)/shard_map/output_rest/pallas_call | solution.py:429
  (100 shorter events, 20.7 us)
Async XLA Ops:
  3.5 26.6 %collective-permute-start.4 = (bf16[4,384,640]{2,1,0:T(8,128)(2,1)}, bf16[4,384,640]{2,1,0:T(8,128)(2,1)}, u32[]{:S(2)}, u32[]{:S(2)}) collective-permute-start(bf16[4,384,640]{2,1,0:T(8,128)(2,1)} %take_other.1), channel_id=1, source_target_pairs={{0,1},{1,0},{2,3},{3,2},{4,5},{5,4},{6,7},{7,6},{8,9},{9,8},{10,11... | collective-permute-start | bytes 5898248 | tf_op jit(solution)/shard_map/ppermute | solution.py:37
  4.3 11.9 %collective-permute-start = (bf16[256,640]{1,0:T(8,128)(2,1)S(1)}, bf16[256,640]{1,0:T(8,128)(2,1)S(1)}, u32[]{:S(2)}, u32[]{:S(2)}) collective-permute-start(bf16[256,640]{1,0:T(8,128)(2,1)S(1)} %get-tuple-element.53.refs_0_), channel_id=1, source_target_pairs={{0,2},{1,3},{2,4},{3,5},{4,6},{5,7},{6,0},{7,1},{8,10},{9,11},{10,... | collective-permute-start | bytes 983048 | tf_op jit(solution)/shard_map/ppermute | solution.py:37
  6.0 10.2 %collective-permute-start.2 = (bf16[256,640]{1,0:T(8,128)(2,1)S(1)}, bf16[256,640]{1,0:T(8,128)(2,1)S(1)}, u32[]{:S(2)}, u32[]{:S(2)}) collective-permute-start(bf16[256,640]{1,0:T(8,128)(2,1)S(1)} %get-tuple-element.52.refs_8_), channel_id=1, source_target_pairs={{0,6},{1,7},{2,0},{3,1},{4,2},{5,3},{6,4},{7,5},{8,14},{9,15},{10,... | collective-permute-start | bytes 983048 | tf_op jit(solution)/shard_map/ppermute | solution.py:37
  16.2 9.9 %collective-permute-start.1 = (bf16[256,640]{1,0:T(8,128)(2,1)S(1)}, bf16[256,640]{1,0:T(8,128)(2,1)S(1)}, u32[]{:S(2)}, u32[]{:S(2)}) collective-permute-start(bf16[256,640]{1,0:T(8,128)(2,1)S(1)} %collective-permute-done.refs_2_), channel_id=1, source_target_pairs={{0,2},{1,3},{2,4},{3,5},{4,6},{5,7},{6,0},{7,1},{8,10},{9,11},{10,... | collective-permute-start | bytes 983048 | tf_op jit(solution)/shard_map/ppermute | solution.py:37
  16.2 13.8 %collective-permute-start.3 = (bf16[256,640]{1,0:T(8,128)(2,1)S(1)}, bf16[256,640]{1,0:T(8,128)(2,1)}, u32[]{:S(2)}, u32[]{:S(2)}) collective-permute-start(bf16[256,640]{1,0:T(8,128)(2,1)S(1)} %collective-permute-done.2.refs_12_), channel_id=1, source_target_pairs={{0,6},{1,7},{2,0},{3,1},{4,2},{5,3},{6,4},{7,5},{8,14},{9,15},{10,... | collective-permute-start | bytes 983048 | tf_op jit(solution)/shard_map/ppermute | solution.py:37
  19.1 3.9 %collective-permute-start.6 = (s32[1,16]{1,0:T(1,128)S(1)}, s32[1,16]{1,0:T(1,128)S(1)}, u32[]{:S(2)}, u32[]{:S(2)}) collective-permute-start(s32[1,16]{1,0:T(1,128)S(1)} %copy-done.14), channel_id=1, source_target_pairs={{0,96},{1,25},{2,98},{3,27},{4,100},{5,29},{6,102},{7,31},{8,104},... | collective-permute-start | bytes 200 | tf_op jit(solution)/shard_map/ppermute | solution.py:37
  23.0 13.6 %collective-permute-start.10 = (bf16[256,640]{1,0:T(8,128)(2,1)S(1)}, bf16[256,640]{1,0:T(8,128)(2,1)}, u32[]{:S(2)}, u32[]{:S(2)}) collective-permute-start(bf16[256,640]{1,0:T(8,128)(2,1)S(1)} %get-tuple-element.53.refs_0_), channel_id=1, source_target_pairs={{0,6},{1,7},{2,0},{3,1},{4,2},{5,3},{6,4},{7,5},{8,14},{9,15},{10,... | collective-permute-start | bytes 983048 | tf_op jit(solution)/shard_map/ppermute | solution.py:37
  25.6 11.1 %collective-permute-start.14 = (bf16[256,640]{1,0:T(8,128)(2,1)S(1)}, bf16[256,640]{1,0:T(8,128)(2,1)}, u32[]{:S(2)}, u32[]{:S(2)}) collective-permute-start(bf16[256,640]{1,0:T(8,128)(2,1)S(1)} %get-tuple-element.52.refs_8_), channel_id=1, source_target_pairs={{0,2},{1,3},{2,4},{3,5},{4,6},{5,7},{6,0},{7,1},{8,10},{9,11},{10,... | collective-permute-start | bytes 983048 | tf_op jit(solution)/shard_map/ppermute | solution.py:37
  26.1 12.2 %collective-permute-start.13 = (bf16[256,640]{1,0:T(8,128)(2,1)S(1)}, bf16[256,640]{1,0:T(8,128)(2,1)}, u32[]{:S(2)}, u32[]{:S(2)}) collective-permute-start(bf16[256,640]{1,0:T(8,128)(2,1)S(1)} %get-tuple-element.52.refs_8_), channel_id=1, source_target_pairs={{0,1},{1,0},{2,3},{3,2},{4,5},{5,4},{6,7},{7,6},{8,9},{9,8},{10,11... | collective-permute-start | bytes 983048 | tf_op jit(solution)/shard_map/ppermute | solution.py:37
  30.0 8.3 %collective-permute-start.8 = (bf16[256,640]{1,0:T(8,128)(2,1)S(1)}, bf16[256,640]{1,0:T(8,128)(2,1)}, u32[]{:S(2)}, u32[]{:S(2)}) collective-permute-start(bf16[256,640]{1,0:T(8,128)(2,1)S(1)} %get-tuple-element.53.refs_0_), channel_id=1, source_target_pairs={{0,1},{1,0},{2,3},{3,2},{4,5},{5,4},{6,7},{7,6},{8,9},{9,8},{10,11... | collective-permute-start | bytes 983048 | tf_op jit(solution)/shard_map/ppermute | solution.py:37
  30.1 8.7 %collective-permute-start.16 = (bf16[256,640]{1,0:T(8,128)(2,1)S(1)}, bf16[256,640]{1,0:T(8,128)(2,1)}, u32[]{:S(2)}, u32[]{:S(2)}) collective-permute-start(bf16[256,640]{1,0:T(8,128)(2,1)S(1)} %collective-permute-done.2.refs_12_), channel_id=1, source_target_pairs={{0,1},{1,0},{2,3},{3,2},{4,5},{5,4},{6,7},{7,6},{8,9},{9,8},{10,11... | collective-permute-start | bytes 983048 | tf_op jit(solution)/shard_map/ppermute | solution.py:37
  60.2 7.2 %collective-permute-start.18 = (bf16[384,512]{1,0:T(8,128)(2,1)S(1)}, bf16[384,512]{1,0:T(8,128)(2,1)S(1)}, u32[]{:S(2)}, u32[]{:S(2)}) collective-permute-start(bf16[384,512]{1,0:T(8,128)(2,1)S(1)} %get-tuple-element.36.refs_0_), channel_id=1, source_target_pairs={{0,32},{1,9},{2,34},{3,11},{4,36},{5,13},{6,38},{7,15},{8,40},{9,1... | collective-permute-start | bytes 1179656 | tf_op jit(solution)/shard_map/ppermute | solution.py:37
  60.5 8.2 %collective-permute-start.19 = (bf16[384,512]{1,0:T(8,128)(2,1)S(1)}, bf16[384,512]{1,0:T(8,128)(2,1)}, u32[]{:S(2)}, u32[]{:S(2)}) collective-permute-start(bf16[384,512]{1,0:T(8,128)(2,1)S(1)} %get-tuple-element.36.refs_0_), channel_id=1, source_target_pairs={{0,96},{1,25},{2,98},{3,27},{4,100},{5,29},{6,102},{7,31},{8,104},... | collective-permute-start | bytes 1179656 | tf_op jit(solution)/shard_map/ppermute | solution.py:37
  61.7 11.9 %collective-permute-start.21 = (bf16[512,384]{1,0:T(8,128)(2,1)S(1)}, bf16[512,384]{1,0:T(8,128)(2,1)}, u32[]{:S(2)}, u32[]{:S(2)}) collective-permute-start(bf16[512,384]{1,0:T(8,128)(2,1)S(1)} %get-tuple-element.37.refs_3_.refs_4_), channel_id=1, source_target_pairs={{0,8},{1,33},{2,10},{3,35},{4,12},{5,37},{6,14},{7,39},{8,16},{9,4... | collective-permute-start | bytes 1179656 | tf_op jit(solution)/shard_map/ppermute | solution.py:37
  61.9 11.8 %collective-permute-start.25 = (bf16[384,512]{1,0:T(8,128)(2,1)S(1)}, bf16[384,512]{1,0:T(8,128)(2,1)}, u32[]{:S(2)}, u32[]{:S(2)}) collective-permute-start(bf16[384,512]{1,0:T(8,128)(2,1)S(1)} %get-tuple-element.38.refs_6_.refs_8_), channel_id=1, source_target_pairs={{0,24},{1,97},{2,26},{3,99},{4,28},{5,101},{6,30},{7,103},{8,0},{9... | collective-permute-start | bytes 1179656 | tf_op jit(solution)/shard_map/ppermute | solution.py:37
  64.5 13.8 %collective-permute-start.22 = (bf16[512,384]{1,0:T(8,128)(2,1)S(1)}, bf16[512,384]{1,0:T(8,128)(2,1)}, u32[]{:S(2)}, u32[]{:S(2)}) collective-permute-start(bf16[512,384]{1,0:T(8,128)(2,1)S(1)} %get-tuple-element.37.refs_3_.refs_4_), channel_id=1, source_target_pairs={{0,24},{1,97},{2,26},{3,99},{4,28},{5,101},{6,30},{7,103},{8,0},{9... | collective-permute-start | bytes 1179656 | tf_op jit(solution)/shard_map/ppermute | solution.py:37
  67.4 11.3 %collective-permute-start.24 = (bf16[384,512]{1,0:T(8,128)(2,1)S(1)}, bf16[384,512]{1,0:T(8,128)(2,1)}, u32[]{:S(2)}, u32[]{:S(2)}) collective-permute-start(bf16[384,512]{1,0:T(8,128)(2,1)S(1)} %get-tuple-element.38.refs_6_.refs_8_), channel_id=1, source_target_pairs={{0,8},{1,33},{2,10},{3,35},{4,12},{5,37},{6,14},{7,39},{8,16},{9,4... | collective-permute-start | bytes 1179656 | tf_op jit(solution)/shard_map/ppermute | solution.py:37
  68.7 20.2 %collective-permute-start.20 = (bf16[384,512]{1,0:T(8,128)(2,1)S(1)}, bf16[384,512]{1,0:T(8,128)(2,1)}, u32[]{:S(2)}, u32[]{:S(2)}) collective-permute-start(bf16[384,512]{1,0:T(8,128)(2,1)S(1)} %get-tuple-element.36.refs_0_), channel_id=1, source_target_pairs={{0,64},{1,17},{2,66},{3,19},{4,68},{5,21},{6,70},{7,23},{8,72},{9,... | collective-permute-start | bytes 1179656 | tf_op jit(solution)/shard_map/ppermute | solution.py:37
  73.6 15.4 %collective-permute-start.23 = (bf16[512,384]{1,0:T(8,128)(2,1)}, bf16[512,384]{1,0:T(8,128)(2,1)}, u32[]{:S(2)}, u32[]{:S(2)}) collective-permute-start(bf16[512,384]{1,0:T(8,128)(2,1)} %collective-permute-done.21.refs_4_.refs_5_), channel_id=1, source_target_pairs={{0,8},{1,33},{2,10},{3,35},{4,12},{5,37},{6,14},{7,39},{8,16},{9,4... | collective-permute-start | bytes 1179656 | tf_op jit(solution)/shard_map/ppermute | solution.py:37
  73.6 15.4 %collective-permute-start.26 = (bf16[384,512]{1,0:T(8,128)(2,1)}, bf16[384,512]{1,0:T(8,128)(2,1)}, u32[]{:S(2)}, u32[]{:S(2)}) collective-permute-start(bf16[384,512]{1,0:T(8,128)(2,1)} %collective-permute-done.25.refs_8_.refs_10_), channel_id=1, source_target_pairs={{0,24},{1,97},{2,26},{3,99},{4,28},{5,101},{6,30},{7,103},{8,0},{9... | collective-permute-start | bytes 1179656 | tf_op jit(solution)/shard_map/ppermute | solution.py:37
  78.3 44.3 %collective-permute-start.37 = (bf16[2,384,640]{2,1,0:T(8,128)(2,1)}, bf16[2,384,640]{2,1,0:T(8,128)(2,1)}, u32[]{:S(2)}, u32[]{:S(2)}) collective-permute-start(bf16[2,384,640]{2,1,0:T(8,128)(2,1)} %get-tuple-element.46), channel_id=1, source_target_pairs={{0,2},{1,3},{2,4},{3,5},{4,6},{5,7},{6,0},{7,1},{8,10},{9,11},{10,... | collective-permute-start | bytes 2949128 | tf_op jit(solution)/shard_map/ppermute | solution.py:37
  99.4 12.8 %collective-permute-start.27 = (bf16[400,512]{1,0:T(8,128)(2,1)S(1)}, bf16[400,512]{1,0:T(8,128)(2,1)S(1)}, u32[]{:S(2)}, u32[]{:S(2)}) collective-permute-start(bf16[400,512]{1,0:T(8,128)(2,1)S(1)} %get-tuple-element.42), channel_id=1, source_target_pairs={{0,96},{1,25},{2,98},{3,27},{4,100},{5,29},{6,102},{7,31},{8,104},... | collective-permute-start | bytes 1228808 | tf_op jit(solution)/shard_map/ppermute | solution.py:37
  99.5 12.7 %collective-permute-start.28 = (bf16[400,512]{1,0:T(8,128)(2,1)S(1)}, bf16[400,512]{1,0:T(8,128)(2,1)S(1)}, u32[]{:S(2)}, u32[]{:S(2)}) collective-permute-start(bf16[400,512]{1,0:T(8,128)(2,1)S(1)} %get-tuple-element.43), channel_id=1, source_target_pairs={{0,32},{1,9},{2,34},{3,11},{4,36},{5,13},{6,38},{7,15},{8,40},{9,1... | collective-permute-start | bytes 1228808 | tf_op jit(solution)/shard_map/ppermute | solution.py:37
  102.1 10.0 %collective-permute-start.29 = (bf16[400,512]{1,0:T(8,128)(2,1)S(1)}, bf16[400,512]{1,0:T(8,128)(2,1)S(1)}, u32[]{:S(2)}, u32[]{:S(2)}) collective-permute-start(bf16[400,512]{1,0:T(8,128)(2,1)S(1)} %get-tuple-element.44), channel_id=1, source_target_pairs={{0,64},{1,17},{2,66},{3,19},{4,68},{5,21},{6,70},{7,23},{8,72},{9,... | collective-permute-start | bytes 1228808 | tf_op jit(solution)/shard_map/ppermute | solution.py:37
  112.6 12.1 %collective-permute-start.30 = (bf16[512,384]{1,0:T(8,128)(2,1)S(1)}, bf16[512,384]{1,0:T(8,128)(2,1)S(1)}, u32[]{:S(2)}, u32[]{:S(2)}) collective-permute-start(bf16[512,384]{1,0:T(8,128)(2,1)S(1)} %combine.1.first_ref), channel_id=1, source_target_pairs={{0,1},{1,0},{2,3},{3,2},{4,5},{5,4},{6,7},{7,6},{8,9},{9,8},{10,11... | collective-permute-start | bytes 1179656 | tf_op jit(solution)/shard_map/ppermute | solution.py:37
  119.1 66.1 %collective-permute-start.38 = (bf16[2,384,640]{2,1,0:T(8,128)(2,1)}, bf16[2,384,640]{2,1,0:T(8,128)(2,1)S(1)}, u32[]{:S(2)}, u32[]{:S(2)}) collective-permute-start(bf16[2,384,640]{2,1,0:T(8,128)(2,1)} %get-tuple-element.47), channel_id=1, source_target_pairs={{0,6},{1,7},{2,0},{3,1},{4,2},{5,3},{6,4},{7,5},{8,14},{9,15},{10,... | collective-permute-start | bytes 2949128 | tf_op jit(solution)/shard_map/ppermute | solution.py:37
  122.0 63.2 %collective-permute-start.39 = (bf16[2,384,640]{2,1,0:T(8,128)(2,1)}, bf16[2,384,640]{2,1,0:T(8,128)(2,1)}, u32[]{:S(2)}, u32[]{:S(2)}) collective-permute-start(bf16[2,384,640]{2,1,0:T(8,128)(2,1)} %get-tuple-element.48), channel_id=1, source_target_pairs={{0,4},{1,5},{2,6},{3,7},{4,0},{5,1},{6,2},{7,3},{8,12},{9,13},{10,... | collective-permute-start | bytes 2949128 | tf_op jit(solution)/shard_map/ppermute | solution.py:37
  122.0 32.8 %collective-permute-start.31 = (bf16[512,384]{1,0:T(8,128)(2,1)S(1)}, bf16[512,384]{1,0:T(8,128)(2,1)S(1)}, u32[]{:S(2)}, u32[]{:S(2)}) collective-permute-start(bf16[512,384]{1,0:T(8,128)(2,1)S(1)} %combine.1.first_ref), channel_id=1, source_target_pairs={{0,2},{1,3},{2,4},{3,5},{4,6},{5,7},{6,0},{7,1},{8,10},{9,11},{10,... | collective-permute-start | bytes 1179656 | tf_op jit(solution)/shard_map/ppermute | solution.py:37
  122.6 58.4 %collective-permute-start.33 = (bf16[512,384]{1,0:T(8,128)(2,1)S(1)}, bf16[512,384]{1,0:T(8,128)(2,1)}, u32[]{:S(2)}, u32[]{:S(2)}) collective-permute-start(bf16[512,384]{1,0:T(8,128)(2,1)S(1)} %combine.1.first_ref), channel_id=1, source_target_pairs={{0,6},{1,7},{2,0},{3,1},{4,2},{5,3},{6,4},{7,5},{8,14},{9,15},{10,... | collective-permute-start | bytes 1179656 | tf_op jit(solution)/shard_map/ppermute | solution.py:37
  125.5 56.7 %collective-permute-start.35 = (bf16[512,384]{1,0:T(8,128)(2,1)S(1)}, bf16[512,384]{1,0:T(8,128)(2,1)}, u32[]{:S(2)}, u32[]{:S(2)}) collective-permute-start(bf16[512,384]{1,0:T(8,128)(2,1)S(1)} %combine.1.first_ref), channel_id=1, source_target_pairs={{0,4},{1,5},{2,6},{3,7},{4,0},{5,1},{6,2},{7,3},{8,12},{9,13},{10,... | collective-permute-start | bytes 1179656 | tf_op jit(solution)/shard_map/ppermute | solution.py:37
  154.8 30.4 %collective-permute-start.32 = (bf16[512,384]{1,0:T(8,128)(2,1)S(1)}, bf16[512,384]{1,0:T(8,128)(2,1)}, u32[]{:S(2)}, u32[]{:S(2)}) collective-permute-start(bf16[512,384]{1,0:T(8,128)(2,1)S(1)} %collective-permute-done.31.refs_0_), channel_id=1, source_target_pairs={{0,1},{1,0},{2,3},{3,2},{4,5},{5,4},{6,7},{7,6},{8,9},{9,8},{10,11... | collective-permute-start | bytes 1179656 | tf_op jit(solution)/shard_map/ppermute | solution.py:37
  181.1 4.2 %collective-permute-start.34 = (bf16[512,384]{1,0:T(8,128)(2,1)}, bf16[512,384]{1,0:T(8,128)(2,1)}, u32[]{:S(2)}, u32[]{:S(2)}) collective-permute-start(bf16[512,384]{1,0:T(8,128)(2,1)} %collective-permute-done.33.refs_2_), channel_id=1, source_target_pairs={{0,1},{1,0},{2,3},{3,2},{4,5},{5,4},{6,7},{7,6},{8,9},{9,8},{10,11... | collective-permute-start | bytes 1179656 | tf_op jit(solution)/shard_map/ppermute | solution.py:37
  (23 other events, 148.1 us)
